TPU v7x, 32 devices: a whole 2x2x4 slice. The times are simulated.
32 devices in a mesh: dp: 4 (over y, x), row: 2 (over core), col: 4 (over z).
Axes of the slice: x: 2, y: 2, z: 4, core: 2. Of those that a mesh axis runs over, the one named last changes fastest.
Arguments:
- inputs: bfloat16 [8192, 1536], P('dp', 'row'), may hold values from -6 to 6
- segments: int32 [4, 2048], P('dp'), may hold values from 0 to 5, never falling along the last dimension, each value on 1 to 1024 neighbouring positions
- cotangent: bfloat16 [8192, 1536], P('dp', 'row'), may hold values from -6 to 6
- norm_gain: float32 [1536], P('row'), may hold values from 0.1 to 1.9
- gate_proj: float32 [1536, 48, 64], P('dp', 'col', 'row'), may hold values from -0.15625 to 0.15625
- inner_proj: float32 [1536, 48, 64], P('dp', 'col', 'row'), may hold values from -0.15625 to 0.15625
- state_proj: float32 [1536, 256], P('dp'), may hold values from -0.15625 to 0.15625
- step_proj: float32 [1536, 48], P('dp', 'col'), may hold values from -0.15625 to 0.15625
- conv_inner: float32 [4, 48, 64], P(None, 'col', 'row'), may hold values from -0.5 to 0.5
- bias_inner: float32 [48, 64], P('col', 'row'), may hold values from -0.5 to 0.5
- conv_state: float32 [4, 256], replicated, may hold values from -0.5 to 0.5
- bias_state: float32 [256], replicated, may hold values from -0.5 to 0.5
- step_bias: float32 [48], P('col'), may hold values from -3 to -1
- decay_log: float32 [48], P('col'), may hold values from -2.3 to 1.4
- skip_gain: float32 [48], P('col'), may hold values from 0.25 to 1
- gate_norm: float32 [48, 64], P('col', 'row'), may hold values from 0.1 to 1.9
- out_proj: float32 [1536, 48, 64], P('dp', 'col', 'row'), may hold values from -0.109375 to 0.109375
Outputs:
- output: bfloat16 [8192, 1536], P('dp', 'row')
- grad_inputs: float32 [8192, 1536], P('dp', 'row')
- grad_norm_gain: float32 [1536], P('row')
- grad_gate_proj: float32 [1536, 48, 64], P('dp', 'col', 'row')
- grad_inner_proj: float32 [1536, 48, 64], P('dp', 'col', 'row')
- grad_state_proj: float32 [1536, 256], P('dp')
- grad_step_proj: float32 [1536, 48], P('dp', 'col')
- grad_conv_inner: float32 [4, 48, 64], P(None, 'col', 'row')
- grad_bias_inner: float32 [48, 64], P('col', 'row')
- grad_conv_state: float32 [4, 256], replicated
- grad_bias_state: float32 [256], replicated
- grad_step_bias: float32 [48], P('col')
- grad_decay_log: float32 [48], P('col')
- grad_skip_gain: float32 [48], P('col')
- grad_gate_norm: float32 [48, 64], P('col', 'row')
- grad_out_proj: float32 [1536, 48, 64], P('dp', 'col', 'row')
Inputs may be any that keep to these rules, and one draw needn't show every extreme that they name: `segments`: in each sequence the numbers never fall; a document is a run of equal numbers of at most 1024 tokens, and one document has exactly 1024.
All inputs are finite; a program needn't handle non-finite values.
Results may differ from a plain program's by a relative error of at most 0.012.
The roundings to bfloat16 on the way count: a program that leaves them out, or rounds other values in their place, can miss the bound.
Values may be sent and summed in bfloat16 or wider, within the bound.
A program may use at most 192 MiB of HBM per device.

v0:
```python
import jax
import jax.numpy as jnp
from jax import lax
from jax.sharding import PartitionSpec as P

H = 48
P_SIZE = 64
BLOCK_LEN = 256


EPSILON = 1e-05
HIGHEST = lax.Precision.HIGHEST


def conv_act(values, kernel, offset_bias, seg_ids):
    length = values.shape[0]
    width_k = kernel.shape[0]
    summed = offset_bias[None, :] + kernel[width_k - 1][None, :] * values
    for offset in range(1, width_k):
        shifted = jnp.pad(values, ((offset, 0), (0, 0)))[:length]
        earlier = jnp.pad(seg_ids, (offset, 0), constant_values=-1)[:length]
        within = (earlier == seg_ids).astype(jnp.float32)
        summed = summed + kernel[width_k - 1 - offset][None, :] * shifted * within[:, None]
    return jax.nn.silu(summed)


def ssm_gate(
    gate_pre, inner_act, state_act, step_size, decay_rate, skip_vals, seg_ids, head_count, block_len
):
    length = gate_pre.shape[0]
    channels = inner_act.shape[1] // head_count
    state_dim = state_act.shape[1] // 2
    block_count = length // block_len
    inner_heads = inner_act.reshape(length, head_count, channels)
    log_decay = step_size * decay_rate[None, :]
    cumul = jnp.cumsum(log_decay.reshape(block_count, block_len, head_count), axis=1)
    seg_blocks = seg_ids.reshape(block_count, block_len)
    driven = (inner_heads * step_size[:, :, None]).reshape(
        block_count, block_len, head_count, channels
    )
    in_blocks = state_act[:, :state_dim].reshape(block_count, block_len, state_dim)
    out_blocks = state_act[:, state_dim:].reshape(block_count, block_len, state_dim)
    positions = jnp.arange(block_len)
    causal = positions[:, None] >= positions[None, :]

    def intra_block(item):
        cum_block, seg_block, in_block, out_block, driven_block = item
        inner_prod = jnp.dot(out_block, in_block.T, precision=HIGHEST)
        gaps = cum_block.T[:, :, None] - cum_block.T[:, None, :]
        allowed = (causal & (seg_block[:, None] == seg_block[None, :]))[None]
        decays = jnp.where(allowed, jnp.exp(jnp.where(allowed, gaps, 0.0)), 0.0)
        mixing = decays * inner_prod[None]
        return jnp.einsum("hts,shp->thp", mixing, driven_block, precision=HIGHEST)

    local_out = lax.map(
        jax.checkpoint(intra_block), (cumul, seg_blocks, in_blocks, out_blocks, driven)
    )
    last_cum = cumul[:, -1, :]
    last_seg = seg_blocks[:, -1]
    tails = jnp.where(
        seg_blocks[:, :, None] == last_seg[:, None, None],
        jnp.exp(last_cum[:, None, :] - cumul),
        0.0,
    )
    contrib = jnp.einsum("kqhp,kqn->khpn", driven * tails[..., None], in_blocks, precision=HIGHEST)
    before_seg = jnp.concatenate([jnp.full((1,), -1, seg_ids.dtype), last_seg[:-1]])
    carried = (last_seg == before_seg).astype(jnp.float32)

    def advance(state, item):
        keep_flag, last_block, contrib_block = item
        renewed = keep_flag * jnp.exp(last_block)[:, None, None] * state + contrib_block
        return (renewed, state)

    initial = jnp.zeros((head_count, channels, state_dim), jnp.float32)
    final_state, entering = lax.scan(advance, initial, (carried, last_cum, contrib))
    reach = jnp.where(seg_blocks[:, :, None] == before_seg[:, None, None], jnp.exp(cumul), 0.0)
    from_state = (
        jnp.einsum("kqn,khpn->kqhp", out_blocks, entering, precision=HIGHEST) * reach[..., None]
    )
    mixed = (local_out + from_state).reshape(length, head_count, channels) + skip_vals[
        None, :, None
    ] * inner_heads
    gated = mixed * jax.nn.silu(gate_pre.reshape(length, head_count, channels))
    return gated.reshape(length, head_count * channels)


def contract_last(left, right):
    return lax.dot_general(
        left, right, (((1,), (1,)), ((), ())), preferred_element_type=jnp.float32
    )


def contract_first(left, right):
    return lax.dot_general(
        left, right, (((0,), (0,)), ((), ())), preferred_element_type=jnp.float32
    )


def per_device(
    inputs,
    segments,
    cotangent,
    norm_gain,
    gate_proj,
    inner_proj,
    state_proj,
    step_proj,
    conv_inner,
    bias_inner,
    conv_state,
    bias_state,
    step_bias,
    decay_log,
    skip_gain,
    gate_norm,
    out_proj,
):
    seg_ids = segments[0]
    length = inputs.shape[0]
    row_count = lax.axis_size("row")
    col_count = lax.axis_size("col")
    row_at = lax.axis_index("row")
    col_at = lax.axis_index("col")
    group_size = row_count * col_count
    model_width = inputs.shape[1] * row_count
    head_count = gate_proj.shape[1]
    channels = gate_proj.shape[2]
    local_width = head_count * channels
    state_width = state_proj.shape[1]
    pieces = model_width // group_size
    member = row_at * col_count + col_at
    state_share = state_width // group_size
    half_heads = head_count // row_count
    inner_width = H * P_SIZE
    plain = inputs.astype(jnp.float32)
    sq_total = lax.psum(jnp.sum(plain * plain, axis=1), "row")
    scaling = lax.rsqrt(sq_total / model_width + EPSILON)
    normed_half = (plain * scaling[:, None] * norm_gain[None, :]).astype(jnp.bfloat16)
    normed = lax.all_gather(normed_half, "row", axis=1, tiled=True)
    gathered = (
        lax.all_gather(gate_proj.astype(jnp.bfloat16), "dp", axis=0, tiled=True),
        lax.all_gather(inner_proj.astype(jnp.bfloat16), "dp", axis=0, tiled=True),
        lax.all_gather(state_proj.astype(jnp.bfloat16), "dp", axis=0, tiled=True),
        lax.all_gather(step_proj.astype(jnp.bfloat16), "dp", axis=0, tiled=True),
        lax.all_gather(out_proj.astype(jnp.bfloat16), "dp", axis=0, tiled=True),
    )
    gate_w = gathered[0].reshape(model_width, local_width)
    inner_w = gathered[1].reshape(model_width, local_width)
    state_w = gathered[2]
    step_w = gathered[3]
    out_w = gathered[4].reshape(model_width, local_width)
    gate_pre = jnp.dot(normed, gate_w, preferred_element_type=jnp.float32)
    inner_pre = jnp.dot(normed, inner_w, preferred_element_type=jnp.float32)
    state_pre = jnp.dot(normed, state_w, preferred_element_type=jnp.float32)
    step_pre = jnp.dot(normed, step_w, preferred_element_type=jnp.float32)
    step_arg = step_pre + step_bias[None, :]
    step_size = jax.nn.softplus(step_arg)
    decay_rate = -jnp.exp(decay_log)

    def state_conv(pre_vals, kernel, offset_bias):
        return conv_act(pre_vals, kernel, offset_bias, seg_ids)

    state_act, state_back = jax.vjp(state_conv, state_pre, conv_state, bias_state)

    def mixer(
        gate_vals, inner_vals, state_vals, step_vals, decay_vals, skip_vals, kernel, offset_bias
    ):
        inner_act = conv_act(inner_vals, kernel, offset_bias, seg_ids)
        return ssm_gate(
            gate_vals,
            inner_act,
            state_vals,
            step_vals,
            decay_vals,
            skip_vals,
            seg_ids,
            head_count,
            BLOCK_LEN,
        )

    gated, mixer_back = jax.vjp(
        mixer,
        gate_pre,
        inner_pre,
        state_act,
        step_size,
        decay_rate,
        skip_gain,
        conv_inner.reshape(conv_inner.shape[0], local_width),
        bias_inner.reshape(local_width),
    )
    gsum = lax.psum(jnp.sum(gated * gated, axis=1), ("row", "col"))
    gate_scale = lax.rsqrt(gsum / inner_width + EPSILON)
    gain_flat = gate_norm.reshape(local_width)
    normed_gate = (gated * gate_scale[:, None] * gain_flat[None, :]).astype(jnp.bfloat16)
    partial_out = contract_last(normed_gate, out_w)
    out_slice = lax.psum_scatter(partial_out, ("row", "col"), scatter_dimension=1, tiled=True)
    plain_slice = lax.dynamic_slice_in_dim(plain, col_at * pieces, pieces, 1)
    out_rows = (plain_slice + out_slice).astype(jnp.bfloat16)
    output = lax.all_gather(out_rows, "col", axis=1, tiled=True)
    cot_full = lax.all_gather(cotangent, "row", axis=1, tiled=True)
    d_normed_gate = jnp.dot(cot_full, out_w, preferred_element_type=jnp.float32)
    grad_out = contract_first(cot_full, normed_gate)
    grad_gate_gain = jnp.sum(d_normed_gate * gated * gate_scale[:, None], axis=0)
    weighted = d_normed_gate * gain_flat[None, :]
    gate_dot = lax.psum(jnp.sum(weighted * gated, axis=1), ("row", "col"))
    d_gated = (
        gate_scale[:, None] * weighted - gated * (gate_scale**3 * gate_dot / inner_width)[:, None]
    )
    d_gate_pre, d_inner_pre, d_state_act, d_step, d_decay, d_skip, d_conv_in, d_bias_in = (
        mixer_back(d_gated)
    )
    wide_heads = head_count * col_count
    wide_step = lax.dynamic_update_slice_in_dim(
        jnp.zeros((length, wide_heads), jnp.float32), d_step, col_at * head_count, 1
    )
    wide_decay = lax.dynamic_update_slice_in_dim(
        jnp.zeros((wide_heads,), jnp.float32), d_decay, col_at * head_count, 0
    )
    wide_skip = lax.dynamic_update_slice_in_dim(
        jnp.zeros((wide_heads,), jnp.float32), d_skip, col_at * head_count, 0
    )
    shared = lax.psum((d_state_act, wide_step, wide_decay, wide_skip), ("row", "col"))
    d_state_full = shared[0]
    d_step_full = lax.dynamic_slice_in_dim(shared[1], col_at * head_count, head_count, 1)
    d_decay_full = lax.dynamic_slice_in_dim(shared[2], col_at * head_count, head_count, 0)
    d_skip_full = lax.dynamic_slice_in_dim(shared[3], col_at * head_count, head_count, 0)
    d_state_pre, grad_conv_st, grad_bias_st = state_back(d_state_full)
    d_step_arg = d_step_full * jax.nn.sigmoid(step_arg)
    grad_step_bias = jnp.sum(d_step_arg, axis=0)
    grad_decay = d_decay_full * decay_rate
    gate_low = d_gate_pre.astype(jnp.bfloat16)
    inner_low = d_inner_pre.astype(jnp.bfloat16)
    state_low = d_state_pre.astype(jnp.bfloat16)
    step_low = d_step_arg.astype(jnp.bfloat16)
    state_part = contract_last(
        lax.dynamic_slice_in_dim(state_low, member * state_share, state_share, 1),
        lax.dynamic_slice_in_dim(state_w, member * state_share, state_share, 1),
    )
    step_part = contract_last(
        lax.dynamic_slice_in_dim(step_low, row_at * half_heads, half_heads, 1),
        lax.dynamic_slice_in_dim(step_w, row_at * half_heads, half_heads, 1),
    )
    d_normed = (
        contract_last(gate_low, gate_w) + contract_last(inner_low, inner_w) + state_part + step_part
    )
    grad_gate_w = contract_first(normed, gate_low)
    grad_inner_w = contract_first(normed, inner_low)
    grad_state_w = contract_first(normed, state_low)
    grad_step_w = contract_first(normed, step_low)
    cot_plain = cotangent.astype(jnp.float32)
    d_half = lax.psum_scatter(d_normed, "row", scatter_dimension=1, tiled=True)
    d_half = lax.psum(d_half, "col")
    weighted_in = d_half * norm_gain[None, :]
    input_dot = lax.psum(jnp.sum(weighted_in * plain, axis=1), "row")
    grad_rows = (
        cot_plain
        + scaling[:, None] * weighted_in
        - plain * (scaling**3 * input_dot / model_width)[:, None]
    )
    grad_norm = jnp.sum(d_half * plain * scaling[:, None], axis=0)
    big = (
        lax.psum_scatter(
            grad_gate_w.reshape(model_width, head_count, channels),
            "dp",
            scatter_dimension=0,
            tiled=True,
        ),
        lax.psum_scatter(
            grad_inner_w.reshape(model_width, head_count, channels),
            "dp",
            scatter_dimension=0,
            tiled=True,
        ),
        lax.psum_scatter(grad_state_w, "dp", scatter_dimension=0, tiled=True),
        lax.psum_scatter(grad_step_w, "dp", scatter_dimension=0, tiled=True),
        lax.psum_scatter(
            grad_out.reshape(model_width, head_count, channels),
            "dp",
            scatter_dimension=0,
            tiled=True,
        ),
    )
    small = lax.psum(
        (
            grad_norm,
            d_conv_in.reshape(conv_inner.shape),
            d_bias_in.reshape(bias_inner.shape),
            grad_conv_st,
            grad_bias_st,
            grad_step_bias,
            grad_decay,
            d_skip_full,
            grad_gate_gain.reshape(gate_norm.shape),
        ),
        "dp",
    )
    return (
        output,
        grad_rows,
        small[0],
        big[0],
        big[1],
        big[2],
        big[3],
        small[1],
        small[2],
        small[3],
        small[4],
        small[5],
        small[6],
        small[7],
        small[8],
        big[4],
    )


def solution(mesh):
    return jax.shard_map(
        per_device,
        mesh=mesh,
        in_specs=(
            P("dp", "row"),
            P("dp", None),
            P("dp", "row"),
            P("row"),
            P("dp", "col", "row"),
            P("dp", "col", "row"),
            P("dp", None),
            P("dp", "col"),
            P(None, "col", "row"),
            P("col", "row"),
            P(),
            P(),
            P("col"),
            P("col"),
            P("col"),
            P("col", "row"),
            P("dp", "col", "row"),
        ),
        out_specs=(
            P("dp", "row"),
            P("dp", "row"),
            P("row"),
            P("dp", "col", "row"),
            P("dp", "col", "row"),
            P("dp", None),
            P("dp", "col"),
            P(None, "col", "row"),
            P("col", "row"),
            P(),
            P(),
            P("col"),
            P("col"),
            P("col"),
            P("col", "row"),
            P("dp", "col", "row"),
        ),
        check_vma=False,
    )
```

profile of v0, /device:TPU:0, one launch (start us, length us, event | category | flops | bytes accessed | tf_op | source)
XLA Modules:
  0.0 1333.0 jit_solution(18420000439808059908)
XLA Ops:
  23.6 10.2 all_gather.26
  33.9 14.0 %all_gather.27 = bf16[1536,256]{1,0:T(8,128)(2,1)} all-gather(bf16[384,256]{1,0:T(8,128)(2,1)S(1)} %convert_element_type.83), channel_id=1, replica_groups=mesh['dp'=4,'row'=2,'col'=4] {'dp'}, dimensions={0}, use_global_device_ids=true | all-gather | bytes 983040 | tf_op jit(solution)/shard_map/all_gather | solution.py:143
  50.5 11.6 all-gather.7.cloned.1.call-done
  62.1 5.8 fusion.157
  68.0 4.5 fusion.88
  78.2 5.2 broadcast_multiply_fusion
  84.9 4.6 reduce-window.14
  90.1 4.8 fusion.158
  110.1 54.1 %while.72 = (s32[]{:T(128)}, f32[12,32,128]{2,1,0:T(8,128)S(1)}, f32[8,12,32,128]{3,2,1,0:T(8,128)}, f32[8,12]{1,0:T(8,128)}, f32[8,12,1,1]{1,3,2,0:T(1,128)}, /...) while((s32[]{:T(128)}, f32[12,32,128]{2,1,0:T(8,128)S(1)}, ...), condition=%wide.region_7.8_spmd.clone, body=%wide.region_6.7_spmd.clone.sunk | while | flops 196635 | bytes 985236 | solution.py:75
  164.2 6.1 fusion.159
  172.3 57.1 %while.70 = (s32[]{:T(128)}, f32[8,256,12,32]{1,3,2,0:T(8,128)}, f32[8,256,12,32]{1,3,2,0:T(8,128)S(1)}, s32[8,256]{1,0:T(8,128)}, f32[8,256,12]{1,2,0:T(8,128)}...) while((s32[]{:T(128)}, f32[8,256,12,32]{1,3,2,0:T(8,128)}, ...), condition=%wide.region_5.6_spmd.clone, body=%wide.region_4.5_spmd.clone.sunk | while | flops 405995520 | bytes 1766501 | solution.py:55
  175.2 4.2 fusion.232
  182.3 4.2 fusion.232
  189.4 4.2 fusion.232
  196.5 4.2 fusion.232
  203.6 4.2 fusion.232
  210.7 4.2 fusion.232
  217.8 4.2 fusion.232
  224.9 4.2 fusion.232
  229.5 4.8 add_bitcast_fusion.1
  236.3 9.7 multiply_reduce_fusion.9
  246.0 17.5 %psum.127 = f32[2048]{0:T(1024)S(1)} all-reduce(f32[2048]{0:T(1024)S(1)} %get-tuple-element.940), channel_id=1, replica_groups=mesh['dp'=4,'row'=2,'col'=4] {'row','col'}, use_global_device_ids=true, to_apply=%region_9.10 | all-reduce | flops 2048 | bytes 16384 | tf_op jit(solution)/shard_map/psum | solution.py:192
  263.6 8.1 fusion.84
  271.6 14.0 %psum.128 = f32[2048]{0:T(1024)S(1)} all-reduce(f32[2048]{0:T(1024)S(1)} %get-tuple-element.834), channel_id=1, replica_groups=mesh['dp'=4,'row'=2,'col'=4] {'row','col'}, use_global_device_ids=true, to_apply=%region_12.13 | all-reduce | flops 2048 | bytes 16384 | tf_op jit(solution)/shard_map/psum | solution.py:206
  285.8 4.3 fusion.86
  304.5 114.0 %while.71 = (s32[]{:T(128)}, f32[8,256,12]{1,2,0:T(8,128)S(1)}, f32[8,256,128]{2,1,0:T(8,128)}, f32[8,256,128]{2,1,0:T(8,128)}, f32[8,256,12,32]{1,3,2,0:T(8,128...) while((s32[]{:T(128)}, f32[8,256,12]{1,2,0:T(8,128)S(1)}, ...), condition=%wide.region_20.21_spmd.clone, body=%wide.region_16.20_spmd.clone.sunk | while | flops 917897216 | bytes 6503601 | solution.py:55
  308.7 4.5 fusion.243
  322.9 4.5 fusion.243
  337.1 4.5 fusion.243
  351.4 4.5 fusion.243
  365.6 4.5 fusion.243
  379.9 4.5 fusion.243
  394.1 4.5 fusion.243
  408.4 4.5 fusion.243
  419.8 36.3 %while.73 = (s32[]{:T(128)}, f32[12,32,128]{2,1,0:T(8,128)S(1)}, f32[8,12]{1,0:T(8,128)S(1)}, f32[8,12,32,128]{3,2,1,0:T(8,128)}, f32[8,12,32,128]{3,2,1,0:T(8,1...) while((s32[]{:T(128)}, f32[12,32,128]{2,1,0:T(8,128)S(1)}, ...), condition=%wide.region_15.16_spmd.clone, body=%wide.region_13.15_spmd.clone.sunk | while | flops 294928 | bytes 1180264 | solution.py:75
  456.1 8.1 fusion.117
  464.3 7.7 fusion.120
  472.0 5.2 multiply_reduce_fusion.6
  484.5 19.9 %reduce-window.16 = f32[8,12,2,128]{3,1,2,0:T(8,128)S(1)} reduce-window(f32[8,12,2,128]{3,1,2,0:T(8,128)S(1)} %copy.159, f32[]{:T(128)} %constant.213.clone.1), window={size=1x1x1x128 pad=0_0x0_0x0_0x0_127}, to_apply=%region_26.27 | reduce-window | flops 3121152 | bytes 196612 | tf_op jit(solution)/shard_map/reduce-window.2
  511.3 7.8 convolution_bitcast_fusion.2
  523.5 9.5 multiply_reduce_fusion.5
  535.4 6.3 fusion.161
  541.8 6.5 fusion.160
  548.2 31.2 %all-reduce.34.cloned.1.call-done = (f32[2048,256]{1,0:T(8,128)}, f32[2048,48]{0,1:T(8,128)}) async-done(((f32[2048,256]{1,0:T(8,128)}, f32[2048,48]{0,1:T(8,128)}), (f32[2048,256]{1,0:T(8,128)}, f32[2048,48]{0,1:T(8,128)})) %all-reduce.34.cloned.1.call-update) | async-done | bytes 2490384 | tf_op jit(solution)/shard_map/psum | solution.py:223
  580.6 4.2 multiply_reduce_fusion.13
  587.2 6.3 fusion.126
  593.6 17.8 %fusion.60 = f32[2048,1536]{1,0:T(8,128)} fusion(f32[2048,1536]{1,0:T(8,128)} %fusion.126, f32[2048,1536]{1,0:T(8,128)} %fusion.161, f32[2048,1536,1]{1,0,2:T(8,128)} %fusion.160, bf16[2048,12]{0,1:T(8,128)(2,1)S(1)} %get-tuple-element.937, s32[]{:T(128)S(6)} %select_n.96, bf16[1536,12]{0,1:T(8,128)(2,1)S(1)} %copy-done.50), kind=kOutput, calls=%fused_computation.77 | convolution fusion | flops 47185920 | bytes 50390016 | tf_op jit(solution)/shard_map/dot_general | solution.py:88
  616.5 210.1 %reduce-scatter.22.cloned.1.call-done = f32[192,2048]{1,0:T(8,128)} async-done(((f32[1536,2048]{1,0:T(8,128)}), f32[192,2048]{1,0:T(8,128)}) %reduce-scatter.22.cloned.1.call-update) | async-done | bytes 1572880
  835.9 15.8 %reduce-scatter.10.cloned.1.call-done = f32[2048,768]{1,0:T(8,128)} async-done(((f32[2048,1536]{1,0:T(8,128)}), f32[2048,768]{1,0:T(8,128)}) %reduce-scatter.10.cloned.1.call-update) | async-done | bytes 6291472 | tf_op jit(solution)/shard_map/reduce_scatter | solution.py:252
  851.7 4.3 fusion.164
  856.2 6.1 fusion.163
  862.3 7.6 fusion.68
  870.0 7.3 fusion.162
  877.4 7.3 fusion.165
  885.5 18.0 %all-reduce.26 = (f32[48]{0:T(128)S(1)}, f32[48]{0:T(128)S(1)}) all-reduce(f32[48]{0:T(128)S(1)} %dynamic_update_slice.85, f32[48]{0:T(128)S(1)} %dynamic_update_slice.86), channel_id=1, replica_groups=mesh['dp'=4,'row'=2,'col'=4] {'row','col'}, use_global_device_ids=true, to_apply=%region_56.57 | all-reduce | flops 96 | bytes 768 | tf_op jit(solution)/shard_map/psum | solution.py:223
  903.7 15.4 %all-gather.15.cloned.1.call-done = bf16[2048,768]{0,1:T(8,128)(2,1)} async-done(((bf16[2048,192]{0,1:T(8,128)(2,1)}), bf16[2048,768]{0,1:T(8,128)(2,1)}) %all-gather.15.cloned.1.call-update) | async-done | bytes 3145744 | tf_op jit(solution)/shard_map/all_gather | solution.py:200
  919.0 4.6 copy.163
  923.6 219.5 %all-reduce.32.cloned.1.call-done = f32[2048,768]{1,0:T(8,128)} async-done(((f32[2048,768]{1,0:T(8,128)}), f32[2048,768]{1,0:T(8,128)}) %all-reduce.32.cloned.1.call-update) | async-done | bytes 6291472 | tf_op jit(solution)/shard_map/psum | solution.py:253
  1147.3 17.6 %all-reduce.28 = (f32[768]{0:T(1024)}, f32[4,12,32]{2,1,0:T(8,128)S(1)}, f32[12,32]{1,0:T(8,128)}, f32[4,256]{1,0:T(4,128)}, f32[256]{0:T(256)}, /*index=5*/f32[...) all-reduce(f32[768]{0:T(1024)S(1)} %get-tuple-element.831, ...), channel_id=1, replica_groups=mesh['dp'=4,'row'=2,'col'=4] {'dp'}, use_global_device_ids=true, to_apply=%region_34.35 | all-reduce | flops 4388 | bytes 35104 | tf_op jit(solution)/shard_map/psum | solution.py:284
  1168.0 6.2 fusion.65
  1174.2 29.1 %reduce-scatter.16.cloned.1.call-done = f32[384,256]{1,0:T(8,128)} async-done(((f32[1536,256]{1,0:T(8,128)}), f32[384,256]{1,0:T(8,128)}) %reduce-scatter.16.cloned.1.call-update) | async-done | bytes 393232 | tf_op jit(solution)/shard_map/reduce_scatter | solution.py:275
  1203.2 41.0 %reduce-scatter.12.cloned.1.call-done = f32[384,12,32]{0,2,1:T(8,128)} async-done(((f32[1536,12,32]{0,2,1:T(8,128)}), f32[384,12,32]{0,2,1:T(8,128)}) %reduce-scatter.12.cloned.1.call-update) | async-done | bytes 589840 | tf_op jit(solution)/shard_map/reduce_scatter | solution.py:263
  1244.3 40.9 %reduce-scatter.14.cloned.1.call-done = f32[384,12,32]{0,2,1:T(8,128)} async-done(((f32[1536,12,32]{0,2,1:T(8,128)}), f32[384,12,32]{0,2,1:T(8,128)}) %reduce-scatter.14.cloned.1.call-update) | async-done | bytes 589840 | tf_op jit(solution)/shard_map/reduce_scatter | solution.py:269
  1285.2 40.9 %reduce-scatter.20.cloned.1.call-done = f32[384,12,32]{0,2,1:T(8,128)} async-done(((f32[1536,12,32]{0,2,1:T(8,128)}), f32[384,12,32]{0,2,1:T(8,128)}) %reduce-scatter.20.cloned.1.call-update) | async-done | bytes 589840 | tf_op jit(solution)/shard_map/reduce_scatter | solution.py:277
  (581 shorter events, 299.2 us)
Async XLA Ops:
  7.2 7.9 copy-start
  7.2 7.9 copy-start.61
  7.2 43.3 %all-gather.9.cloned.1.call-start = ((), (), s32[]{:S(2)}) async-start(), calls=%async_computation.8 | async-start | bytes 1474560 | tf_op jit(solution)/shard_map/all_gather | solution.py:142
  9.2 52.9 %all-gather.7.cloned.1.call-start = ((), (), s32[]{:S(2)}) async-start(), calls=%async_computation.7 | async-start | bytes 9437184 | tf_op jit(solution)/shard_map/all_gather | solution.py:139
  17.6 16.2 %copy-start.48 = (f32[384,256]{1,0:T(8,128)S(1)}, f32[384,256]{1,0:T(8,128)}, u32[]{:S(2)}) copy-start(f32[384,256]{1,0:T(8,128)} %param.31) | copy-start | bytes 1179652
  17.7 218.7 %all-gather.11.cloned.1.call-start = ((), (), s32[]{:S(2)}) async-start(), calls=%async_computation.9 | async-start | bytes 1474560 | tf_op jit(solution)/shard_map/all_gather | solution.py:141
  19.4 28.5 %copy-start.90 = (f32[4,256]{1,0:T(4,128)S(1)}, f32[4,256]{1,0:T(4,128)}, u32[]{:S(2)}) copy-start(f32[4,256]{1,0:T(4,128)} %param.35) | copy-start | bytes 12292
  19.4 30.5 %copy-start.59 = (f32[12,32]{1,0:T(8,128)S(1)}, f32[12,32]{1,0:T(8,128)}, u32[]{:S(2)}) copy-start(f32[12,32]{1,0:T(8,128)} %param.40) | copy-start | bytes 4612
  19.4 244.1 %all-gather.13.cloned.1.call-start = ((), (), s32[]{:S(2)}) async-start(), calls=%async_computation.10 | async-start | bytes 1474560 | tf_op jit(solution)/shard_map/all_gather | solution.py:145
  20.2 243.3 %all-gather.17.cloned.1.call-start = ((), (), s32[]{:S(2)}) async-start(), calls=%async_computation.12 | async-start | bytes 9437184 | tf_op jit(solution)/shard_map/all_gather | solution.py:201
  20.8 558.6 %all-reduce.34.cloned.1.call-start = ((), (), s32[]{:S(2)}) async-start(), calls=%async_computation.21 | async-start | bytes 4980736 | tf_op jit(solution)/shard_map/psum | solution.py:223
  22.1 45.9 %copy-start.51 = (s32[8,256]{1,0:T(8,128)}, s32[8,256]{1,0:T(8,128)S(1)}, u32[]{:S(2)}) copy-start(s32[8,256]{1,0:T(8,128)S(1)} %reshape_squeeze.2) | copy-start | bytes 24580
  22.6 45.4 %copy-start.45 = (f32[2048]{0:T(1024)}, f32[2048]{0:T(1024)S(1)}, u32[]{:S(2)}) copy-start(f32[2048]{0:T(1024)S(1)} %get-tuple-element.976) | copy-start | bytes 24580
  22.7 45.3 %copy-start.70 = (f32[384]{0:T(512)}, f32[384]{0:T(512)S(1)}, u32[]{:S(2)}) copy-start(f32[384]{0:T(512)S(1)} %mul.739) | copy-start | bytes 4612
  22.8 45.2 %copy-start.72 = (f32[384]{0:T(512)}, f32[384]{0:T(512)S(1)}, u32[]{:S(2)}) copy-start(f32[384]{0:T(512)S(1)} %mul.734) | copy-start | bytes 4612
  22.9 45.1 %copy-start.74 = (f32[384]{0:T(512)}, f32[384]{0:T(512)S(1)}, u32[]{:S(2)}) copy-start(f32[384]{0:T(512)S(1)} %mul.729) | copy-start | bytes 4612
  23.0 45.1 %copy-start.76 = (f32[384]{0:T(512)}, f32[384]{0:T(512)S(1)}, u32[]{:S(2)}) copy-start(f32[384]{0:T(512)S(1)} %mul.721) | copy-start | bytes 4612
  90.0 13.3 copy-start.23
  90.1 10.7 copy-start.38
  90.1 6.2 copy-start.46
  90.1 6.2 copy-start.78
  90.1 6.2 copy-start.80
  90.1 6.2 copy-start.82
  90.1 6.2 copy-start.84
  90.1 6.2 copy-start.94
  172.3 57.2 %copy-start.28 = (f32[8,256,12]{1,2,0:T(8,128)S(1)}, f32[8,256,12]{1,2,0:T(8,128)}, u32[]{:S(2)}) copy-start(f32[8,256,12]{1,2,0:T(8,128)} %get-tuple-element.970) | copy-start | bytes 294916
  236.3 27.2 %copy-start.86 = (f32[384]{0:T(512)S(1)}, f32[384]{0:T(512)}, u32[]{:S(2)}) copy-start(f32[384]{0:T(512)} %mul.783) | copy-start | bytes 4612
  246.0 39.7 %copy-start.11 = (f32[2048,12,32]{0,2,1:T(8,128)}, f32[2048,12,32]{0,2,1:T(8,128)S(1)}, u32[]{:S(2)}) copy-start(f32[2048,12,32]{0,2,1:T(8,128)S(1)} %get-tuple-element.941) | copy-start | bytes 9437188
  263.5 22.2 %copy-start.54 = (f32[2048]{0:T(1024)}, f32[2048]{0:T(1024)S(1)}, u32[]{:S(2)}) copy-start(f32[2048]{0:T(1024)S(1)} %add_rsqrt_fusion) | copy-start | bytes 24580
  304.5 115.3 %copy-start.98 = (f32[8]{0:T(128)S(1)}, f32[8]{0:T(128)}, u32[]{:S(2)}) copy-start(f32[8]{0:T(128)} %get-tuple-element.1435) | copy-start | bytes 100
  419.8 44.4 %copy-start.27 = (f32[8,256,12]{1,2,0:T(8,128)S(1)}, f32[8,256,12]{1,2,0:T(8,128)}, u32[]{:S(2)}) copy-start(f32[8,256,12]{1,2,0:T(8,128)} %copy-done.26) | copy-start | bytes 294916
  456.1 8.1 copy-start.3
  456.1 8.1 copy-start.13
  456.1 15.9 %copy-start.16 = (f32[8,256,12,32]{1,3,2,0:T(8,128)S(1)}, f32[8,256,12,32]{1,3,2,0:T(8,128)}, u32[]{:S(2)}) copy-start(f32[8,256,12,32]{1,3,2,0:T(8,128)} %get-tuple-element.586) | copy-start | bytes 9437188
  464.2 7.8 copy-start.7
  464.2 7.8 copy-start.9
  484.4 23.7 %copy-start.89 = (f32[12]{0:T(128)S(1)}, f32[12]{0:T(128)}, u32[]{:S(2)}) copy-start(f32[12]{0:T(128)} %exponential_negate_fusion) | copy-start | bytes 148
  504.9 6.4 copy-start.12
  511.2 315.3 %reduce-scatter.22.cloned.1.call-start = ((), (), s32[]{:S(2)}) async-start(), calls=%async_computation.20 | async-start | bytes 14155776
  519.1 332.6 %reduce-scatter.10.cloned.1.call-start = ((), (), s32[]{:S(2)}) async-start(), calls=%async_computation.13 | async-start | bytes 18874368 | tf_op jit(solution)/shard_map/reduce_scatter | solution.py:252
  523.5 9.6 copy-start.71
  523.5 9.6 copy-start.73
  523.5 9.6 copy-start.75
  535.4 6.3 copy-start.21
  535.4 6.3 copy-start.30
  535.4 6.3 copy-start.99
  541.7 37.7 %copy-start.36 = (f32[2,8,8,256]{3,1,2,0:T(8,128)S(1)}, f32[2,8,8,256]{3,1,2,0:T(8,128)}, u32[]{:S(2)}) copy-start(f32[2,8,8,256]{3,1,2,0:T(8,128)} %copy-done.35) | copy-start | bytes 393220
  541.7 37.7 %copy-start.39 = (f32[2048,12]{0,1:T(8,128)S(1)}, f32[2048,12]{0,1:T(8,128)}, u32[]{:S(2)}) copy-start(f32[2048,12]{0,1:T(8,128)} %get-tuple-element.981) | copy-start | bytes 294916
  541.8 38.8 %copy-start.20 = (f32[2048,256]{1,0:T(8,128)S(1)}, f32[2048,256]{1,0:T(8,128)}, u32[]{:S(2)}) copy-start(f32[2048,256]{1,0:T(8,128)} %copy-done.19) | copy-start | bytes 6291460
  587.2 6.3 copy-start.25
  587.2 6.3 copy-start.50
  611.4 307.6 %all-gather.15.cloned.1.call-start = ((), (), s32[]{:S(2)}) async-start(), calls=%async_computation.11 | async-start | bytes 3932160 | tf_op jit(solution)/shard_map/all_gather | solution.py:200
  835.9 307.2 %all-reduce.32.cloned.1.call-start = ((), (), s32[]{:S(2)}) async-start(), calls=%async_computation.14 | async-start | bytes 12582912 | tf_op jit(solution)/shard_map/psum | solution.py:253
  851.7 322.5 %reduce-scatter.18.cloned.1.call-start = ((), (), s32[]{:S(2)}) async-start(), calls=%async_computation.18 | async-start | bytes 122880 | tf_op jit(solution)/shard_map/reduce_scatter | solution.py:276
  856.1 347.1 %reduce-scatter.16.cloned.1.call-start = ((), (), s32[]{:S(2)}) async-start(), calls=%async_computation.17 | async-start | bytes 1966080 | tf_op jit(solution)/shard_map/reduce_scatter | solution.py:275
  862.3 382.0 %reduce-scatter.12.cloned.1.call-start = ((), (), s32[]{:S(2)}) async-start(), calls=%async_computation.15 | async-start | bytes 2949120 | tf_op jit(solution)/shard_map/reduce_scatter | solution.py:263
  870.0 415.2 %reduce-scatter.14.cloned.1.call-start = ((), (), s32[]{:S(2)}) async-start(), calls=%async_computation.16 | async-start | bytes 2949120 | tf_op jit(solution)/shard_map/reduce_scatter | solution.py:269
  877.3 448.8 %reduce-scatter.20.cloned.1.call-start = ((), (), s32[]{:S(2)}) async-start(), calls=%async_computation.19 | async-start | bytes 2949120 | tf_op jit(solution)/shard_map/reduce_scatter | solution.py:277
  877.4 7.6 copy-start.93
  877.4 7.7 copy-start.95
  877.4 26.2 %copy-start.97 = (f32[12]{0:T(128)S(1)}, f32[12]{0:T(128)}, u32[]{:S(2)}) copy-start(f32[12]{0:T(128)} %param.38) | copy-start | bytes 148
  903.6 239.5 %copy-start.53 = (f32[2048]{0:T(1024)S(1)}, f32[2048]{0:T(1024)}, u32[]{:S(2)}) copy-start(f32[2048]{0:T(1024)} %copy-done.52) | copy-start | bytes 24580
  903.7 239.5 %copy-start.62 = (f32[768]{0:T(1024)S(1)}, f32[768]{0:T(1024)}, u32[]{:S(2)}) copy-start(f32[768]{0:T(1024)} %param.28) | copy-start | bytes 9220
  923.6 244.3 %copy-start.58 = (f32[2048]{0:T(1024)S(1)}, f32[2048]{0:T(1024)}, u32[]{:S(2)}) copy-start(f32[2048]{0:T(1024)} %copy-done.57) | copy-start | bytes 24580
  (58 other events, 166.0 us)
Sparse Core Ops, SparseCore 0:
  10.4 32.6 all-gather.8
  45.3 16.8 all-gather.6
  64.5 28.7 all-gather.10
  95.5 27.5 all-gather.12
  124.5 16.7 all-gather.16
  511.4 68.0 all-reduce.33
  581.8 244.6 reduce-scatter.21
  829.0 22.6 reduce-scatter.9
  853.9 65.0 all-gather.14
  921.4 221.7 all-reduce.31
  1146.6 22.1 reduce-scatter.17
  1172.3 30.9 reduce-scatter.15
  1206.9 37.3 reduce-scatter.11
  1247.8 37.3 reduce-scatter.13
  1288.7 37.3 reduce-scatter.19
where the time goes:
time: 1350 us; the launch traced here: 1330 us
  waiting for transfers between devices  656 us (49%)
  matrix products  274 us (20%)
  other arithmetic  165 us (12%)
  local copies, waits for them, and re-layouts  124 us (9%)
  blocking collectives  96.5 us (7%)
  between operations  15.6 us (1%)
    psum x1, waiting for transfers between devices, per_device(): d_half = lax.psum(d_half, 'col')  219 us
    unnamed x16, waiting for transfers between devices  211 us
    dot_general x24, matrix products, intra_block(): return jnp.einsum('hts,shp->thp', mixing, driven_block, precision=HIGHEST)  95.9 us
    dot_general x5, matrix products, contract_last(): lax.dot_general(left, right, (((1,), (1,)), ((), ())), preferred_element_...  44.8 us
    reduce_scatter x1, waiting for transfers between devices, per_device(): lax.psum_scatter(grad_gate_w.reshape(model_width, head_count, channels),...  41 us
    reduce_scatter x1, waiting for transfers between devices, per_device(): lax.psum_scatter(grad_inner_w.reshape(model_width, head_count, channels),...  40.9 us
    reduce_scatter x1, waiting for transfers between devices, per_device(): lax.psum_scatter(grad_out.reshape(model_width, head_count, channels), 'dp...  40.9 us
    dot_general x5, matrix products, contract_first(): lax.dot_general(left, right, (((0,), (0,)), ((), ())), preferred_element_...  32.7 us
  transfers between devices with their start and end apart: 15, of which 10 were waited for; matrix products, arithmetic and copies ran while one was open for 24% of the time, Pallas kernels for 0%

commit v1 on v0

v1 whole, which is shorter than its diff:
```python
import functools

import jax
import jax.numpy as jnp
from jax import lax
from jax.experimental import pallas as pl
from jax.experimental.pallas import tpu as pltpu
from jax.sharding import PartitionSpec as P

H = 48
P_SIZE = 64
BLOCK_LEN = 256
EPSILON = 1e-05
NEG = -1e30
STEP_ROWS = 16
F32 = jnp.float32
BF16 = jnp.bfloat16
HIGHEST = lax.Precision.HIGHEST


def dot_nn(left, right, precision=None):
    return lax.dot_general(
        left, right, (((1,), (0,)), ((), ())), preferred_element_type=F32, precision=precision
    )


def dot_nt(left, right, precision=None):
    return lax.dot_general(
        left, right, (((1,), (1,)), ((), ())), preferred_element_type=F32, precision=precision
    )


def dot_tn(left, right):
    return lax.dot_general(left, right, (((0,), (0,)), ((), ())), preferred_element_type=F32)


def sigmoid(values):
    return 0.5 * jnp.tanh(0.5 * values) + 0.5


def softplus(values):
    return jnp.maximum(values, 0.0) + jnp.log1p(jnp.exp(-jnp.abs(values)))


def lane_fold(values):
    total = values[:, :128]
    for at in range(128, values.shape[1], 128):
        total = total + values[:, at : at + 128]
    return total


def columns_of(rows):
    padded = jnp.concatenate([rows, jnp.zeros((128 - rows.shape[0], rows.shape[1]), F32)], axis=0)
    return padded.T


def block_rows(dims, step_pre, hrow, aux):
    q = step_pre.shape[1]
    step_arg = step_pre + hrow[:, 0:1]
    step = softplus(step_arg)
    log_decay = step * hrow[:, 1:2]
    source = lax.broadcasted_iota(jnp.int32, (q, q), 0)
    target = lax.broadcasted_iota(jnp.int32, (q, q), 1)
    upper = (source <= target).astype(F32)
    cumul = dot_nn(log_decay, upper, HIGHEST)
    last = cumul[:, q - 1 : q]
    cols = columns_of(jnp.concatenate([cumul, aux], axis=0))
    return step_arg, step, cumul, last, cols


def forward_kernel(
    dims,
    x_own,
    x_sib,
    c_own,
    c_sib,
    weights,
    gain_own,
    gain_sib,
    aux_ref,
    conv_ref,
    chan_ref,
    hrow_ref,
    normed_own,
    normed_sib,
    pre_out,
    arg_out,
    gate_out,
    step_out,
    mixed_out,
    dng_out,
    state_out,
    stats_out,
    out_own,
    out_sib,
    prev,
    state,
    act_scr,
):
    nh, pc, ns, width = dims
    inner = nh * pc
    conv_rows = inner + 2 * ns
    gate_at = conv_rows + STEP_ROWS
    out_at = gate_at + inner
    half = x_own.shape[1]
    q = x_own.shape[0]
    row_at = lax.axis_index("row")
    own_at = pl.multiple_of(row_at * half, 128)
    sib_at = pl.multiple_of((1 - row_at) * half, 128)

    @pl.when(pl.program_id(0) == 0)
    def _():
        prev[...] = jnp.zeros_like(prev)
        state[...] = jnp.zeros_like(state)

    xo = x_own[...].astype(F32)
    xs = x_sib[...].astype(F32)
    squares = jnp.sum(xo * xo, axis=1, keepdims=True) + jnp.sum(xs * xs, axis=1, keepdims=True)
    scaling = lax.rsqrt(squares / width + EPSILON)
    no = (xo * scaling * gain_own[...]).astype(BF16)
    nsib = (xs * scaling * gain_sib[...]).astype(BF16)
    normed_own[...] = no
    normed_sib[...] = nsib
    pre = dot_nt(weights[0:out_at, pl.ds(own_at, half)], no) + dot_nt(
        weights[0:out_at, pl.ds(sib_at, half)], nsib
    )
    values = pre[0:conv_rows]
    step_pre = pre[conv_rows:gate_at]
    gate = pre[gate_at:out_at]
    pre_out[...] = values
    step_out[...] = step_pre
    gate_out[...] = gate
    aux = aux_ref[...]
    conv = conv_ref[...]
    joined = jnp.concatenate([prev[...], values], axis=1)
    arg = conv[:, 4:5] + conv[:, 3:4] * values
    for offset in range(1, 4):
        arg = arg + conv[:, 3 - offset : 4 - offset] * (
            aux[offset - 1 : offset] * joined[:, 128 - offset : 128 - offset + q]
        )
    prev[...] = values[:, q - 128 :]
    arg_out[...] = arg
    act = arg * sigmoid(arg)
    act_scr[...] = act[0:inner]
    in_low = act[inner : inner + ns].astype(BF16)
    out_low = act[inner + ns :].astype(BF16)

    _, step, cumul, last, cols = block_rows(dims, step_pre, hrow_ref[...], aux)
    source = lax.broadcasted_iota(jnp.int32, (q, q), 0)
    target = lax.broadcasted_iota(jnp.int32, (q, q), 1)
    seg_col = cols[:, STEP_ROWS + 3 : STEP_ROWS + 4]
    bias = jnp.where((source <= target) & (seg_col == aux[3:4]), 0.0, NEG)
    pairs = dot_tn(in_low, out_low)
    entering = state[...]
    state_out[0] = entering
    from_state = dot_nn(entering.astype(BF16), out_low)
    reach = aux[4:5] * jnp.exp(cumul)
    tails = aux[5:6] * jnp.exp(last - cumul)
    keep = aux[6:7, 0:1] * jnp.exp(last)
    hq = q // 2
    gain = chan_ref[...]
    squares_row = jnp.zeros((1, q), F32)
    tail_parts = []
    for h in range(nh):
        lo = h * pc
        x_h = act_scr[lo : lo + pc]
        u_h = (x_h * step[h : h + 1]).astype(BF16)
        tail_parts.append((x_h * (step[h : h + 1] * tails[h : h + 1])).astype(BF16))
        col = cols[:, h : h + 1]
        row = cumul[h : h + 1]
        top = (jnp.exp((row - col[:hq]) + bias[:hq]) * pairs[:hq]).astype(BF16)
        low = (jnp.exp((row[:, hq:] - col[hq:]) + bias[hq:, hq:]) * pairs[hq:, hq:]).astype(BF16)
        y_top = dot_nn(u_h[:, :hq], top)
        y_low = dot_nn(u_h[:, hq:], low)
        y_h = jnp.concatenate([y_top[:, :hq], y_top[:, hq:] + y_low], axis=1)
        y_h = y_h + from_state[lo : lo + pc] * reach[h : h + 1]
        mixed_out[lo : lo + pc] = y_h + gain[lo : lo + pc, 1:2] * x_h
    contrib = dot_nt(jnp.concatenate(tail_parts, axis=0), in_low)
    for h in range(nh):
        lo = h * pc
        state[lo : lo + pc] = keep[h : h + 1] * entering[lo : lo + pc] + contrib[lo : lo + pc]
    gated = mixed_out[...] * (gate * sigmoid(gate))
    squares_row = jnp.sum(gated * gated, axis=0, keepdims=True)
    weighted = gated * gain[:, 0:1]
    low = weighted.astype(BF16)
    out_own[...] = dot_tn(low, weights[out_at:, pl.ds(own_at, half)]).astype(BF16)
    out_sib[...] = dot_tn(low, weights[out_at:, pl.ds(sib_at, half)]).astype(BF16)
    dng = dot_nt(weights[out_at:, pl.ds(own_at, half)], c_own[...]) + dot_nt(
        weights[out_at:, pl.ds(sib_at, half)], c_sib[...]
    )
    dng_out[...] = dng
    dot_row = jnp.sum(dng * weighted, axis=0, keepdims=True)
    stats_out[...] = jnp.concatenate([squares_row, dot_row, jnp.zeros((6, q), F32)], axis=0)


def backward_kernel(
    dims,
    normed_own,
    normed_sib,
    c_own,
    c_sib,
    weights,
    aux_ref,
    conv_ref,
    chan_ref,
    hrow_ref,
    pre_ref,
    arg_ref,
    gate_ref,
    step_ref,
    mixed_ref,
    dng_ref,
    state_ref,
    stats_ref,
    dn_own,
    dn_sib,
    grad_w,
    conv_grad,
    chan_grad,
    head_grad,
    after,
    d_state,
    acc_w,
    acc_conv,
    acc_chan,
    acc_head,
    du_scr,
    low_scr,
):
    nh, pc, ns, width = dims
    inner = nh * pc
    conv_rows = inner + 2 * ns
    gate_at = conv_rows + STEP_ROWS
    out_at = gate_at + inner
    half = c_own.shape[1]
    q = c_own.shape[0]
    inner_width = H * P_SIZE
    row_at = lax.axis_index("row")
    own_at = pl.multiple_of(row_at * half, 128)
    sib_at = pl.multiple_of((1 - row_at) * half, 128)

    @pl.when(pl.program_id(0) == 0)
    def _():
        after[...] = jnp.zeros_like(after)
        d_state[...] = jnp.zeros_like(d_state)
        acc_w[...] = jnp.zeros_like(acc_w)
        acc_conv[...] = jnp.zeros_like(acc_conv)
        acc_chan[...] = jnp.zeros_like(acc_chan)
        acc_head[...] = jnp.zeros_like(acc_head)

    aux = aux_ref[...]
    conv = conv_ref[...]
    chan = chan_ref[...]
    hrow = hrow_ref[...]
    stats = stats_ref[...]
    gate_scale = lax.rsqrt(stats[0:1] / inner_width + EPSILON)
    pull = gate_scale * gate_scale * gate_scale * stats[1:2] / inner_width
    gate = gate_ref[...]
    sig = sigmoid(gate)
    silu = gate * sig
    mixed = mixed_ref[...]
    gated = mixed * silu
    dng_scaled = dng_ref[...] * gate_scale
    d_gated = chan[:, 0:1] * dng_scaled - gated * pull
    acc_chan[0] += lane_fold(dng_scaled * gated)
    normed_gate = (gated * (gate_scale * chan[:, 0:1])).astype(BF16)
    acc_w[out_at:, pl.ds(own_at, half)] += dot_nn(normed_gate, c_own[...])
    acc_w[out_at:, pl.ds(sib_at, half)] += dot_nn(normed_gate, c_sib[...])
    grad_mixed = d_gated * silu
    low_scr[gate_at:out_at] = (d_gated * mixed * (sig * (1.0 + gate * (1.0 - sig)))).astype(BF16)

    arg = arg_ref[...]
    sig_arg = sigmoid(arg)
    act = arg * sig_arg
    act_slope = sig_arg * (1.0 + arg * (1.0 - sig_arg))
    x_all = act[0:inner]
    in_low = act[inner : inner + ns].astype(BF16)
    out_low = act[inner + ns :].astype(BF16)
    step_arg, step, cumul, last, cols = block_rows(dims, step_ref[...], hrow, aux)
    t_at = lax.broadcasted_iota(jnp.int32, (q, q), 0)
    s_at = lax.broadcasted_iota(jnp.int32, (q, q), 1)
    seg_col = cols[:, STEP_ROWS + 3 : STEP_ROWS + 4]
    bias = jnp.where((s_at <= t_at) & (seg_col == aux[3:4]), 0.0, NEG)
    pairs = dot_tn(out_low, in_low)
    reach = aux[4:5] * jnp.exp(cumul)
    tails = aux[5:6] * jnp.exp(last - cumul)
    keep = aux[6:7, 0:1] * jnp.exp(last)
    entering = state_ref[0]
    d_next = d_state[...]
    from_next = dot_nn(d_next.astype(BF16), in_low)
    hq = q // 2
    acc_chan[1] += lane_fold(grad_mixed * x_all)
    d_pairs_top = jnp.zeros((hq, hq), F32)
    d_pairs_low = jnp.zeros((hq, q), F32)
    reach_parts, tail_parts = [], []
    row_sums, col_sums, x_sums, tail_sums, carry_sums = [], [], [], [], []
    for h in range(nh):
        lo = h * pc
        x_h = x_all[lo : lo + pc]
        u_h = x_h * step[h : h + 1]
        u_low = u_h.astype(BF16)
        g_h = grad_mixed[lo : lo + pc]
        g_low = g_h.astype(BF16)
        col = cols[:, h : h + 1]
        row = cumul[h : h + 1]
        reach_parts.append((g_h * reach[h : h + 1]).astype(BF16))
        tail_parts.append((u_h * tails[h : h + 1]).astype(BF16))
        e_top = jnp.exp((col[:hq] - row[:, :hq]) + bias[:hq, :hq])
        e_low = jnp.exp((col[hq:] - row) + bias[hq:])
        m_top = (e_top * pairs[:hq, :hq]).astype(BF16)
        m_low = (e_low * pairs[hq:]).astype(BF16)
        dm_top = dot_tn(g_low[:, :hq], u_low[:, :hq])
        dm_low = dot_tn(g_low[:, hq:], u_low)
        d_pairs_top = d_pairs_top + dm_top * e_top
        d_pairs_low = d_pairs_low + dm_low * e_low
        du_top = dot_nn(g_low[:, :hq], m_top)
        du_low = dot_nn(g_low[:, hq:], m_low)
        du_local = jnp.concatenate([du_top + du_low[:, :hq], du_low[:, hq:]], axis=1)
        du_next = from_next[lo : lo + pc] * tails[h : h + 1]
        du = du_local + du_next
        du_scr[lo : lo + pc] = du * step[h : h + 1] + chan[lo : lo + pc, 1:2] * g_h
        u_round = u_low.astype(F32)
        y_h = mixed[lo : lo + pc] - chan[lo : lo + pc, 1:2] * x_h
        row_sums.append(jnp.sum(g_low.astype(F32) * y_h, axis=0, keepdims=True))
        next_sum = jnp.sum(u_round * du_next, axis=0, keepdims=True)
        col_sums.append(jnp.sum(u_round * du_local, axis=0, keepdims=True) + next_sum)
        tail_sums.append(next_sum)
        x_sums.append(jnp.sum(x_h * du, axis=0, keepdims=True))
        flow = jnp.sum(entering[lo : lo + pc] * d_next[lo : lo + pc], axis=0, keepdims=True)
        carry_sums.append(flow)
    pad_rows = [jnp.zeros((STEP_ROWS - nh, q), F32)]
    row_sum = jnp.concatenate(row_sums + pad_rows, axis=0)
    col_sum = jnp.concatenate(col_sums + pad_rows, axis=0)
    tail_sum = jnp.concatenate(tail_sums + pad_rows, axis=0)
    x_sum = jnp.concatenate(x_sums + pad_rows, axis=0)
    carry = jnp.concatenate(carry_sums + [jnp.zeros((STEP_ROWS - nh, ns), F32)], axis=0)
    d_last = jnp.sum(tail_sum, axis=1, keepdims=True) + keep * jnp.sum(
        carry, axis=1, keepdims=True
    )
    later = (t_at >= s_at).astype(F32)
    d_log = dot_nn(row_sum - col_sum, later, HIGHEST) + d_last
    d_step = x_sum + hrow[:, 1:2] * d_log
    d_step_arg = d_step * sigmoid(step_arg)
    acc_head[0] += lane_fold(d_step_arg)
    acc_head[1] += lane_fold(step * d_log)
    low_scr[conv_rows:gate_at] = d_step_arg.astype(BF16)

    g_reach = jnp.concatenate(reach_parts, axis=0)
    u_tail = jnp.concatenate(tail_parts, axis=0)
    d_top_low = d_pairs_top.astype(BF16)
    d_low_low = d_pairs_low.astype(BF16)
    d_out = dot_tn(entering.astype(BF16), g_reach)
    d_out = d_out + jnp.concatenate(
        [dot_nt(in_low[:, :hq], d_top_low), dot_nt(in_low, d_low_low)], axis=1
    )
    d_in = dot_tn(d_next.astype(BF16), u_tail) + dot_nn(out_low[:, hq:], d_low_low)
    d_in_top = dot_nn(out_low[:, :hq], d_top_low)
    d_in = jnp.concatenate([d_in[:, :hq] + d_in_top, d_in[:, hq:]], axis=1)
    d_enter = dot_nt(g_reach, out_low)
    for h in range(nh):
        lo = h * pc
        d_state[lo : lo + pc] = keep[h : h + 1] * d_next[lo : lo + pc] + d_enter[lo : lo + pc]

    err = jnp.concatenate([du_scr[...], d_in, d_out], axis=0) * act_slope
    values = pre_ref[...]
    d_pre = conv[:, 3:4] * err
    acc_conv[3] += lane_fold(err * values)
    acc_conv[4] += lane_fold(err)
    for offset in range(1, 4):
        masked = err * aux[offset - 1 : offset]
        joined = jnp.concatenate([masked, after[offset - 1]], axis=1)
        shifted = joined[:, offset : offset + q]
        after[offset - 1] = masked[:, :128]
        d_pre = d_pre + conv[:, 3 - offset : 4 - offset] * shifted
        acc_conv[3 - offset] += lane_fold(shifted * values)
    low_scr[0:conv_rows] = d_pre.astype(BF16)
    low = low_scr[...]
    dn_own[...] = dot_tn(low, weights[0:out_at, pl.ds(own_at, half)]).astype(BF16)
    dn_sib[...] = dot_tn(low, weights[0:out_at, pl.ds(sib_at, half)]).astype(BF16)
    acc_w[0:out_at, pl.ds(own_at, half)] += dot_nn(low, normed_own[...])
    acc_w[0:out_at, pl.ds(sib_at, half)] += dot_nn(low, normed_sib[...])

    @pl.when(pl.program_id(0) == pl.num_programs(0) - 1)
    def _():
        grad_w[...] = acc_w[...].astype(BF16)

        def gather_columns(ref, count):
            lanes = lax.broadcasted_iota(jnp.int32, ref.shape[1:], 1)
            total = jnp.zeros(ref.shape[1:], F32)
            for at in range(count):
                total = jnp.where(lanes == at, jnp.sum(ref[at], axis=1, keepdims=True), total)
            return total

        conv_grad[...] = gather_columns(acc_conv, 5)
        chan_grad[...] = gather_columns(acc_chan, 2)
        head_grad[...] = gather_columns(acc_head, 2)


def per_device(
    inputs,
    segments,
    cotangent,
    norm_gain,
    gate_proj,
    inner_proj,
    state_proj,
    step_proj,
    conv_inner,
    bias_inner,
    conv_state,
    bias_state,
    step_bias,
    decay_log,
    skip_gain,
    gate_norm,
    out_proj,
):
    length, half = inputs.shape
    row_count = lax.axis_size("row")
    col_count = lax.axis_size("col")
    col_at = lax.axis_index("col")
    width = half * row_count
    share, nh, pc = gate_proj.shape
    inner = nh * pc
    state_width = state_proj.shape[1]
    ns = state_width // 2
    conv_rows = inner + state_width
    gate_at = conv_rows + STEP_ROWS
    out_at = gate_at + inner
    rows = out_at + inner
    q = BLOCK_LEN
    blocks = length // q
    swap = [(0, 1), (1, 0)]
    dims = (nh, pc, ns, width)

    def channel_rows(w):
        return jnp.transpose(w, (1, 2, 0)).reshape(inner, share)

    stacked = jnp.concatenate(
        [
            channel_rows(inner_proj),
            state_proj.T,
            jnp.pad(step_proj.T, ((0, STEP_ROWS - nh), (0, 0))),
            channel_rows(gate_proj),
            channel_rows(out_proj),
        ],
        axis=0,
    ).astype(BF16)
    weights = lax.all_gather(stacked, "dp", axis=1, tiled=True)
    x_sib = lax.ppermute(inputs, "row", swap)
    c_sib = lax.ppermute(cotangent, "row", swap)
    gain_own = norm_gain[None, :]
    gain_sib = lax.ppermute(gain_own, "row", swap)

    seg = segments[0]
    seg_blocks = seg.reshape(blocks, q)
    last_seg = seg_blocks[:, -1]
    before_seg = jnp.concatenate([jnp.full((1,), -1, seg.dtype), last_seg[:-1]])
    shift_masks = [
        (jnp.pad(seg, (offset, 0), constant_values=-1)[:length] == seg).astype(F32)
        for offset in range(1, 4)
    ]
    flags = [
        seg.astype(F32),
        (seg_blocks == before_seg[:, None]).astype(F32).reshape(length),
        (seg_blocks == last_seg[:, None]).astype(F32).reshape(length),
        jnp.repeat((last_seg == before_seg).astype(F32), q),
        jnp.zeros((length,), F32),
    ]
    aux = jnp.stack(shift_masks + flags, axis=0)
    conv_cols = jnp.concatenate(
        [conv_inner.reshape(4, inner), conv_state], axis=1
    )
    bias_row = jnp.concatenate([bias_inner.reshape(inner), bias_state])[None]
    conv_par = jnp.concatenate([conv_cols, bias_row, jnp.zeros((3, conv_rows), F32)], axis=0).T
    chan_par = jnp.concatenate(
        [
            gate_norm.reshape(1, inner),
            jnp.repeat(skip_gain, pc)[None],
            jnp.zeros((6, inner), F32),
        ],
        axis=0,
    ).T
    decay_rate = -jnp.exp(decay_log)
    head_par = jnp.pad(
        jnp.stack([step_bias, decay_rate], axis=1), ((0, STEP_ROWS - nh), (0, 6))
    )

    def token_block(order):
        return pl.BlockSpec((q, half), lambda i: (order(i), 0))

    def lane_block(count, order):
        return pl.BlockSpec((count, q), lambda i: (0, order(i)))

    def whole(*shape):
        return pl.BlockSpec(shape, lambda i: (0,) * len(shape), pipeline_mode=pl.Buffered(1))

    def up(i):
        return i

    def down(i):
        return blocks - 1 - i

    sds = jax.ShapeDtypeStruct
    forward = pl.pallas_call(
        functools.partial(forward_kernel, dims),
        name="forward",
        grid=(blocks,),
        in_specs=[
            token_block(up),
            token_block(up),
            token_block(up),
            token_block(up),
            whole(rows, width),
            whole(1, half),
            whole(1, half),
            lane_block(8, up),
            whole(conv_rows, 8),
            whole(inner, 8),
            whole(STEP_ROWS, 8),
        ],
        out_specs=[
            token_block(up),
            token_block(up),
            lane_block(conv_rows, up),
            lane_block(conv_rows, up),
            lane_block(inner, up),
            lane_block(STEP_ROWS, up),
            lane_block(inner, up),
            lane_block(inner, up),
            pl.BlockSpec((1, inner, ns), lambda i: (i, 0, 0)),
            lane_block(8, up),
            token_block(up),
            token_block(up),
        ],
        out_shape=[
            sds((length, half), BF16),
            sds((length, half), BF16),
            sds((conv_rows, length), F32),
            sds((conv_rows, length), F32),
            sds((inner, length), F32),
            sds((STEP_ROWS, length), F32),
            sds((inner, length), F32),
            sds((inner, length), F32),
            sds((blocks, inner, ns), F32),
            sds((8, length), F32),
            sds((length, half), BF16),
            sds((length, half), BF16),
        ],
        scratch_shapes=[
            pltpu.VMEM((conv_rows, 128), F32),
            pltpu.VMEM((inner, ns), F32),
            pltpu.VMEM((inner, q), F32),
        ],
        compiler_params=pltpu.CompilerParams(vmem_limit_bytes=56 << 20),
        cost_estimate=pl.CostEstimate(
            flops=2 * length * width * (out_at + 2 * inner),
            bytes_accessed=50 << 20,
            transcendentals=nh * length * q,
        ),
    )
    (
        normed_own,
        normed_sib,
        pre_vals,
        arg_vals,
        gate_vals,
        step_vals,
        mixed_vals,
        dng_vals,
        states,
        stats,
        out_own,
        out_sib,
    ) = forward(
        inputs,
        x_sib,
        cotangent,
        c_sib,
        weights,
        gain_own,
        gain_sib,
        aux,
        conv_par,
        chan_par,
        head_par,
    )
    stats = lax.psum(stats, ("row", "col"))

    out_recv = lax.ppermute(out_sib, "row", swap)
    out_pair = (out_own.astype(F32) + out_recv.astype(F32)).astype(BF16)
    out_sum = lax.psum(out_pair, "col")
    gate_scale = lax.rsqrt(stats[0] / (H * P_SIZE) + EPSILON)
    plain = inputs.astype(F32)
    output = (plain + gate_scale[:, None] * out_sum.astype(F32)).astype(BF16)

    backward = pl.pallas_call(
        functools.partial(backward_kernel, dims),
        name="backward",
        grid=(blocks,),
        in_specs=[
            token_block(down),
            token_block(down),
            token_block(down),
            token_block(down),
            whole(rows, width),
            lane_block(8, down),
            whole(conv_rows, 8),
            whole(inner, 8),
            whole(STEP_ROWS, 8),
            lane_block(conv_rows, down),
            lane_block(conv_rows, down),
            lane_block(inner, down),
            lane_block(STEP_ROWS, down),
            lane_block(inner, down),
            lane_block(inner, down),
            pl.BlockSpec((1, inner, ns), lambda i: (down(i), 0, 0)),
            lane_block(8, down),
        ],
        out_specs=[
            token_block(down),
            token_block(down),
            whole(rows, width),
            whole(conv_rows, 128),
            whole(inner, 128),
            whole(STEP_ROWS, 128),
        ],
        out_shape=[
            sds((length, half), BF16),
            sds((length, half), BF16),
            sds((rows, width), BF16),
            sds((conv_rows, 128), F32),
            sds((inner, 128), F32),
            sds((STEP_ROWS, 128), F32),
        ],
        scratch_shapes=[
            pltpu.VMEM((3, conv_rows, 128), F32),
            pltpu.VMEM((inner, ns), F32),
            pltpu.VMEM((rows, width), F32),
            pltpu.VMEM((5, conv_rows, 128), F32),
            pltpu.VMEM((2, inner, 128), F32),
            pltpu.VMEM((2, STEP_ROWS, 128), F32),
            pltpu.VMEM((inner, q), F32),
            pltpu.VMEM((out_at, q), BF16),
        ],
        compiler_params=pltpu.CompilerParams(vmem_limit_bytes=60 << 20),
        cost_estimate=pl.CostEstimate(
            flops=4 * length * width * (out_at + inner),
            bytes_accessed=60 << 20,
            transcendentals=nh * length * q,
        ),
    )
    dn_own, dn_sib, grad_w, conv_grad, chan_grad, head_grad = backward(
        normed_own,
        normed_sib,
        cotangent,
        c_sib,
        weights,
        aux,
        conv_par,
        chan_par,
        head_par,
        pre_vals,
        arg_vals,
        gate_vals,
        step_vals,
        mixed_vals,
        dng_vals,
        states,
        stats,
    )

    dn_recv = lax.ppermute(dn_sib, "row", swap)
    dn_pair = (dn_own.astype(F32) + dn_recv.astype(F32)).astype(BF16)
    d_half = lax.psum(dn_pair, "col").astype(F32)
    x_sib_plain = x_sib.astype(F32)
    squares = jnp.sum(plain * plain, axis=1) + jnp.sum(x_sib_plain * x_sib_plain, axis=1)
    scaling = lax.rsqrt(squares / width + EPSILON)
    weighted = d_half * gain_own
    dot_own = jnp.sum(weighted * plain, axis=1)
    input_dot = dot_own + lax.ppermute(dot_own, "row", swap)
    grad_inputs = (
        cotangent.astype(F32)
        + scaling[:, None] * weighted
        - plain * (scaling**3 * input_dot / width)[:, None]
    )
    grad_norm = jnp.sum(d_half * plain * scaling[:, None], axis=0)

    grads = lax.psum_scatter(grad_w, "dp", scatter_dimension=1, tiled=True).astype(F32)
    head_wide = head_grad[:nh, :2].T
    skip_part = jnp.sum(chan_grad[:, 1].reshape(nh, pc), axis=1)[None]
    heads = jnp.concatenate([head_wide, skip_part], axis=0)

    def widen(part):
        wide = jnp.zeros((col_count,) + part.shape, F32)
        return lax.dynamic_update_slice_in_dim(wide, part[None], col_at, 0)

    step_wide = widen(grads[conv_rows : conv_rows + nh])
    head_all = widen(heads)
    grad_norm, conv_sum, gate_gain_sum, head_all = lax.psum(
        (grad_norm, conv_grad[:, :5].T, chan_grad[:, 0], head_all), "dp"
    )
    state_sum, step_wide, conv_state_sum, head_all = lax.psum(
        (grads[inner:conv_rows], step_wide, conv_sum[:, inner:], head_all), ("row", "col")
    )

    def take(wide):
        return lax.dynamic_slice_in_dim(wide, col_at, 1, 0)[0]

    step_grad = take(step_wide)
    head_own = take(head_all)

    def feature_rows(w):
        return jnp.transpose(w.reshape(nh, pc, share), (2, 0, 1))

    return (
        output,
        grad_inputs,
        grad_norm,
        feature_rows(grads[gate_at:out_at]),
        feature_rows(grads[0:inner]),
        state_sum.T,
        step_grad.T,
        conv_sum[:4, :inner].reshape(4, nh, pc),
        conv_sum[4, :inner].reshape(nh, pc),
        conv_state_sum[:4],
        conv_state_sum[4],
        head_own[0],
        head_own[1] * decay_rate,
        head_own[2],
        gate_gain_sum.reshape(nh, pc),
        feature_rows(grads[out_at:]),
    )


def solution(mesh):
    return jax.shard_map(
        per_device,
        mesh=mesh,
        in_specs=(
            P("dp", "row"),
            P("dp", None),
            P("dp", "row"),
            P("row"),
            P("dp", "col", "row"),
            P("dp", "col", "row"),
            P("dp", None),
            P("dp", "col"),
            P(None, "col", "row"),
            P("col", "row"),
            P(),
            P(),
            P("col"),
            P("col"),
            P("col"),
            P("col", "row"),
            P("dp", "col", "row"),
        ),
        out_specs=(
            P("dp", "row"),
            P("dp", "row"),
            P("row"),
            P("dp", "col", "row"),
            P("dp", "col", "row"),
            P("dp", None),
            P("dp", "col"),
            P(None, "col", "row"),
            P("col", "row"),
            P(),
            P(),
            P("col"),
            P("col"),
            P("col"),
            P("col", "row"),
            P("dp", "col", "row"),
        ),
        check_vma=False,
    )
```

time: 1350 us -> 659 us (0.49); the launches traced: 1330 us -> 658 us
  matrix products: 274 us -> 0 us
  waiting for transfers between devices: 656 us -> 417 us
  other arithmetic: 165 us -> 31.4 us
  Pallas kernels: 0 us -> 105 us
  local copies, waits for them, and re-layouts: 124 us -> 34.6 us
  blocking collectives: 96.5 us -> 52 us
    dot_general x77 -> x0, matrix products: 274 us -> none  [the longest x24 95.9 us: intra_block(): return jnp.einsum('hts,shp->thp', mixing, driven_block, precision=HIGHEST)]
    reduce_scatter x6 -> x0, waiting for transfers between devices: 168 us -> none  [the longest x1 41 us: per_device(): lax.psum_scatter(grad_gate_w.reshape(model_width, head_count, channels),...]
    unnamed x16 -> x6, waiting for transfers between devices: 211 us -> 45.8 us
    pallas_call x0 -> x2, Pallas kernels: none -> 105 us  [the longest x1 64.4 us: per_device(): backward(normed_own, normed_sib, cotangent, c_sib, weights, aux, conv_par...]
    psum x2 -> x3, waiting for transfers between devices: 251 us -> 316 us  [the longest x1 223 us: per_device(): out_sum = lax.psum(out_pair, 'col')]
    reduce_sum x14 -> x3, other arithmetic: 31 us -> 3.39 us  [the longest x1 2.59 us: per_device(): jnp.sum(x_sib_plain * x_sib_plain, axis=1)]
    mul x22 -> x1, other arithmetic: 26.8 us -> 0.52 us  [per_device(): head_own[1] * decay_rate]
    dynamic_update_slice x32 -> x1, other arithmetic: 25.9 us -> 0.01 us  [widen(): return lax.dynamic_update_slice_in_dim(wide, part[None], col_at, 0)]
  transfers between devices with their start and end apart: 15 -> 11, of which waited for: 10 -> 9; matrix products, arithmetic and copies ran while one was open for 24% -> 5% of each run, Pallas kernels for 0% -> 0%
where the time goes in v1:
time: 659 us; the launch traced here: 658 us
  waiting for transfers between devices  417 us (63%)
  Pallas kernels  105 us (16%)
  blocking collectives  52 us (8%)
  local copies, waits for them, and re-layouts  34.6 us (5%)
  other arithmetic  31.4 us (5%)
  between operations  14.2 us (2%)
    psum x1, waiting for transfers between devices, per_device(): out_sum = lax.psum(out_pair, 'col')  223 us
    pallas_call x1, Pallas kernels, per_device(): backward(normed_own, normed_sib, cotangent, c_sib, weights, aux, conv_par...  64.4 us
    psum x1, waiting for transfers between devices, per_device(): stats = lax.psum(stats, ('row', 'col'))  53.5 us
    all_gather x1, waiting for transfers between devices, per_device(): weights = lax.all_gather(stacked, 'dp', axis=1, tiled=True)  46.2 us
    unnamed x6, waiting for transfers between devices  45.8 us
    pallas_call x1, Pallas kernels, per_device(): forward(inputs, x_sib, cotangent, c_sib, weights, gain_own, gain_sib, aux...  40.6 us
    psum x1, waiting for transfers between devices, per_device(): lax.psum((grads[inner:conv_rows], step_wide, conv_sum[:, inner:], head_al...  39.1 us
    psum x1, blocking collectives, per_device(): lax.psum((grads[inner:conv_rows], step_wide, conv_sum[:, inner:], head_al...  28.5 us
  transfers between devices with their start and end apart: 11, of which 9 were waited for; matrix products, arithmetic and copies ran while one was open for 5% of the time, Pallas kernels for 0%

profile of v1, /device:TPU:0, one launch (start us, length us, event | category | flops | bytes accessed | tf_op | source)
XLA Modules:
  0.0 657.8 jit_solution(8396621101727284298)
XLA Ops:
  7.3 1.3 convert.28
  8.6 0.7 constant_dynamic-update-slice_fusion.2
  9.3 1.2 copy.71
  10.5 0.7 convert_bitcast_fusion
  11.3 1.1 convert.31
  12.4 1.1 convert.32
  13.5 0.7 bitcast_dynamic-update-slice_fusion
  14.2 0.6 pad_dynamic-update-slice_fusion
  14.8 0.7 constant_dynamic-update-slice_fusion.1
  15.5 0.7 constant_dynamic-update-slice_fusion
  16.3 0.5 collective-permute-start
  16.9 0.5 collective-permute-start.2
  17.4 0.5 broadcast.66
  18.0 0.7 fusion.22
  19.0 0.1 copy.84
  20.3 0.9 copy.75
  21.2 0.8 copy.76
  22.0 0.1 copy.77
  22.1 0.6 pad.25.hrow_ref
  22.7 0.7 stack.37.aux_ref
  23.4 2.4 collective-permute-done.2.gain_sib
  25.9 0.1 collective-permute-done.x_sib
  26.0 1.0 collective-permute-done.1.c_sib
  27.0 46.2 %all-gather.2.cloned.1.call-done.weights = bf16[1424,1536]{1,0:T(8,128)(2,1)} async-done(((bf16[1424,384]{1,0:T(8,128)(2,1)}), bf16[1424,1536]{1,0:T(8,128)(2,1)}) %all-gather.2.cloned.1.call-update) | async-done | bytes 4374544 | tf_op jit(solution)/shard_map/all_gather | solution.py:449
  73.2 40.6 %forward.1 = (bf16[2048,768]{1,0:T(8,128)(2,1)}, bf16[2048,768]{1,0:T(8,128)(2,1)}, f32[640,2048]{1,0:T(8,128)}, f32[640,2048]{1,0:T(8,128)}, f32[384,2048]{1,0:...) custom-call(bf16[2048,768]{1,0:T(8,128)(2,1)} %x_own.1, ...), custom_call_target="tpu_custom_call" | custom-call | flops 11374952448 | bytes 52428800 | tf_op jit(solution)/shard_map/forward/pallas_call | solution.py:575
  113.8 0.2 reduce-scatter.4.cloned.1.call-start
  114.1 53.5 %all-reduce.13.cloned.1.call-done.stats_ref = f32[8,2048]{1,0:T(8,128)} async-done(((f32[8,2048]{1,0:T(8,128)}), f32[8,2048]{1,0:T(8,128)}) %all-reduce.13.cloned.1.call-update) | async-done | bytes 65552 | tf_op jit(solution)/shard_map/psum | solution.py:588
  167.6 64.4 %backward.1 = (bf16[2048,768]{1,0:T(8,128)(2,1)}, bf16[2048,768]{1,0:T(8,128)(2,1)}, bf16[1424,1536]{1,0:T(8,128)(2,1)}, f32[640,128]{1,0:T(8,128)}, f32[384,128]{1,0:T(8,128)}, /*index=5*/f32[16,128]{1,0:T(8,128)}) custom-call(bf16[2048,768]{1,0:T(8,128)(2,1)} %get-tuple-element.37.normed_own, bf16[2048,768]{1,0:T(8,128)(2,1)} %get-tuple-element.38.normed_sib, ...), custom_call_target="tpu_custom_call" | custom-call | flops 17918066688 | bytes 62914560 | tf_op jit(solution)/shard_map/backward/pallas_call | solution.py:653
  232.0 6.5 copy.82
  238.7 0.5 collective-permute-start.4
  239.2 5.5 collective-permute-done.3
  244.7 4.4 add_convert_fusion.1
  249.1 45.8 %reduce-scatter.4.cloned.1.call-done = bf16[384,1424]{1,0:T(8,128)(2,1)} async-done(((bf16[1536,1424]{1,0:T(8,128)(2,1)}), bf16[384,1424]{1,0:T(8,128)(2,1)}) %reduce-scatter.4.cloned.1.call-update) | async-done | bytes 1093648
  294.8 2.2 copy.83
  297.0 0.1 convert_element_type.78
  297.2 0.9 slice_bitcast_fusion
  298.2 0.3 all-reduce.17.cloned.1.call-start
  298.5 5.3 add_convert_fusion
  303.8 1.9 copy-done.1
  305.7 0.7 fusion.4
  306.4 2.6 multiply_reduce_fusion
  309.0 0.3 slice_reduce_fusion.1
  309.3 0.1 reduce_sum.49
  309.6 1.0 slice_bitcast_fusion.1
  310.6 0.9 fusion.15
  311.5 2.4 fusion.21
  313.9 39.1 %all-reduce.15.cloned.1.call-done = (f32[384,256]{0,1:T(8,128)}, f32[4,12,384]{2,1,0:T(8,128)}) async-done(((f32[384,256]{0,1:T(8,128)}, f32[4,12,384]{2,1,0:T(8,128)}), (f32[384,256]{0,1:T(8,128)}, f32[4,12,384]{2,1,0:T(8,128)})) %all-reduce.15.cloned.1.call-update) | async-done | bytes 466960 | tf_op jit(solution)/shard_map/psum | solution.py:703
  353.0 1.9 copy.79
  354.9 1.3 dynamic-slice_bitcast_fusion
  356.3 223.4 %all-reduce.17.cloned.1.call-done = (bf16[2048,768]{1,0:T(8,128)(2,1)}, bf16[2048,768]{1,0:T(8,128)(2,1)}) async-done(((bf16[2048,768]{1,0:T(8,128)(2,1)}, bf16[2048,768]{1,0:T(8,128)(2,1)}), (bf16[2048,768]{1,0:T(8,128)(2,1)}, bf16[2048,768]{1,0:T(8,128)(2,1)})) %all-reduce.17.cloned.1.call-update) | async-done | bytes 6291472 | tf_op jit(solution)/shard_map/psum | solution.py:592
  579.7 4.2 fusion.7
  583.9 23.4 %all-reduce.7 = (f32[768]{0:T(1024)}, f32[5,640]{0,1:T(8,128)}, f32[4,3,12]{2,1,0:T(4,128)S(1)}, f32[12,32]{1,0:T(8,128)}) all-reduce(f32[768]{0:T(1024)S(1)} %get-tuple-element.116, f32[5,640]{0,1:T(8,128)S(1)} %slice_bitcast_fusion.1, f32[4,3,12]{2,1,0:T(4,128)S(1)} %fusion.19, ...), channel_id=1, replica_groups=mesh['dp'=4,'row'=2,'col'=4] {'dp'}, use_global_device_ids=true, to_apply=%region_7.8 | all-reduce | flops 4496 | bytes 35968 | tf_op jit(solution)/shard_map/psum | solution.py:700
  607.3 1.2 slice_reduce_fusion
  608.5 0.9 slice.109
  609.4 28.5 %all-reduce.5 = (f32[5,256]{0,1:T(8,128)S(1)}, f32[4,3,12]{2,1,0:T(4,128)S(1)}) all-reduce(f32[5,256]{0,1:T(8,128)S(1)} %slice.109, f32[4,3,12]{2,1,0:T(4,128)S(1)} %get-tuple-element.126), channel_id=1, replica_groups=mesh['dp'=4,'row'=2,'col'=4] {'row','col'}, use_global_device_ids=true, to_apply=%region_12.13 | all-reduce | flops 1424 | bytes 11392 | tf_op jit(solution)/shard_map/psum | solution.py:703
  638.0 0.5 slice_bitcast_fusion.4
  638.5 0.5 bitcast_multiply_fusion
  639.0 1.1 collective-permute-start.5
  640.1 0.7 slice_reduce_fusion.3
  640.9 0.9 slice.107
  641.8 0.7 copy.80
  642.6 0.7 reshape_squeeze.10
  643.2 0.7 copy.81
  643.9 7.3 %fusion.2 = (f32[2048,768]{1,0:T(8,128)}, bf16[2048,768]{1,0:T(8,128)(2,1)}) fusion(bf16[2048,768]{1,0:T(8,128)(2,1)} %get-tuple-element.129, bf16[2048,768]{1,0:T(8,128)(2,1)S(1)} %copy-done.1, bf16[2048,768]{1,0:T(8,128)(2,1)} %c_own.3, f32[2048]{0:T(1024)S(1)} %fusion.13, f32[768]{0:T(1024)S(1)} %copy-done.7, f32[2048]{0:T(1024)S(1)} %add_rsqrt_fusion, ...), kind=kLoop, calls=%fused_computation.8 | loop fusion | flops 18874368 | bytes 22047744 | tf_op jit(solution)/shard_map/sub | solution.py:683
  (92 shorter events, 2.2 us)
Async XLA Ops:
  7.2 9.1 %copy-start = (bf16[2048,768]{1,0:T(8,128)(2,1)S(1)}, bf16[2048,768]{1,0:T(8,128)(2,1)}, u32[]{:S(2)}) copy-start(bf16[2048,768]{1,0:T(8,128)(2,1)} %x_own.1) | copy-start | bytes 9437188
  7.2 9.7 %copy-start.7 = (f32[768]{0:T(1024)S(1)}, f32[768]{0:T(1024)}, u32[]{:S(2)}) copy-start(f32[768]{0:T(1024)} %param.20) | copy-start | bytes 9220
  7.2 10.8 %copy-start.6 = (s32[1,2048]{1,0:T(1,128)S(1)}, s32[1,2048]{1,0:T(1,128)}, u32[]{:S(2)}) copy-start(s32[1,2048]{1,0:T(1,128)} %param.18) | copy-start | bytes 24580
  7.2 12.0 %copy-start.9 = (f32[12,32]{1,0:T(8,128)S(1)}, f32[12,32]{1,0:T(8,128)}, u32[]{:S(2)}) copy-start(f32[12,32]{1,0:T(8,128)} %param.26) | copy-start | bytes 4612
  7.2 12.1 %copy-start.14 = (f32[256]{0:T(256)S(1)}, f32[256]{0:T(256)}, u32[]{:S(2)}) copy-start(f32[256]{0:T(256)} %param.28) | copy-start | bytes 3076
  7.2 12.1 %copy-start.8 = (f32[4,12,32]{2,0,1:T(4,128)S(1)}, f32[4,12,32]{2,0,1:T(4,128)}, u32[]{:S(2)}) copy-start(f32[4,12,32]{2,0,1:T(4,128)} %param.25) | copy-start | bytes 18436
  7.2 66.0 %all-gather.2.cloned.1.call-start = ((), (), s32[]{:S(2)}) async-start(), calls=%async_computation.1 | async-start | bytes 5468160 | tf_op jit(solution)/shard_map/all_gather | solution.py:449
  8.5 10.9 %copy-start.15 = (f32[12]{0:T(128)S(1)}, f32[12]{0:T(128)}, u32[]{:S(2)}) copy-start(f32[12]{0:T(128)} %param.31) | copy-start | bytes 148
  8.6 11.0 %copy-start.10 = (f32[12,32]{1,0:T(8,128)S(1)}, f32[12,32]{1,0:T(8,128)}, u32[]{:S(2)}) copy-start(f32[12,32]{1,0:T(8,128)} %param.32) | copy-start | bytes 4612
  8.6 11.3 %copy-start.18 = (f32[12]{0:T(128)S(1)}, f32[12]{0:T(128)}, u32[]{:S(2)}) copy-start(f32[12]{0:T(128)} %param.30) | copy-start | bytes 148
  8.6 11.5 %copy-start.12 = (f32[4,256]{1,0:T(4,128)S(1)}, f32[4,256]{1,0:T(4,128)}, u32[]{:S(2)}) copy-start(f32[4,256]{1,0:T(4,128)} %param.27) | copy-start | bytes 12292
  8.6 11.6 %copy-start.16 = (f32[12]{0:T(128)S(1)}, f32[12]{0:T(128)}, u32[]{:S(2)}) copy-start(f32[12]{0:T(128)} %param.29) | copy-start | bytes 148
  16.3 151.3 %all-reduce.13.cloned.1.call-start = ((), (), s32[]{:S(2)}) async-start(), calls=%async_computation.2 | async-start | bytes 131072 | tf_op jit(solution)/shard_map/psum | solution.py:588
  16.3 9.6 %collective-permute-start = (bf16[2048,768]{1,0:T(8,128)(2,1)S(1)}, bf16[2048,768]{1,0:T(8,128)(2,1)}, u32[]{:S(2)}, u32[]{:S(2)}) collective-permute-start(bf16[2048,768]{1,0:T(8,128)(2,1)S(1)} %copy-done), channel_id=1, source_target_pairs={{0,4},{4,0},{1,5},{5,1},{2,6},{6,2},{3,7},{7,3},{8,12},{12,8},{9,1... | collective-permute-start | bytes 9437192 | tf_op jit(solution)/shard_map/ppermute | solution.py:450
  16.9 10.1 %collective-permute-start.1 = (bf16[2048,768]{1,0:T(8,128)(2,1)}, bf16[2048,768]{1,0:T(8,128)(2,1)}, u32[]{:S(2)}, u32[]{:S(2)}) collective-permute-start(bf16[2048,768]{1,0:T(8,128)(2,1)} %c_own.3), channel_id=1, source_target_pairs={{0,4},{4,0},{1,5},{5,1},{2,6},{6,2},{3,7},{7,3},{8,12},{12,8},{9,1... | collective-permute-start | bytes 9437192 | tf_op jit(solution)/shard_map/ppermute | solution.py:451
  16.9 56.3 %copy-start.13 = (f32[1,768]{1,0:T(1,128)}, f32[1,768]{1,0:T(1,128)S(1)}, u32[]{:S(2)}) copy-start(f32[1,768]{1,0:T(1,128)S(1)} %broadcast_in_dim.38.gain_own) | copy-start | bytes 9220
  16.9 8.9 %collective-permute-start.2 = (f32[1,768]{1,0:T(1,128)S(1)}, f32[1,768]{1,0:T(1,128)S(1)}, u32[]{:S(2)}, u32[]{:S(2)}) collective-permute-start(f32[1,768]{1,0:T(1,128)S(1)} %broadcast_in_dim.38.gain_own), channel_id=1, source_target_pairs={{0,4},{4,0},{1,5},{5,1},{2,6},{6,2},{3,7},{7,3},{8,12},{12,8},{9,1... | collective-permute-start | bytes 9224 | tf_op jit(solution)/shard_map/ppermute | solution.py:453
  25.9 47.4 %copy-start.17 = (f32[1,768]{1,0:T(1,128)}, f32[1,768]{1,0:T(1,128)S(1)}, u32[]{:S(2)}) copy-start(f32[1,768]{1,0:T(1,128)S(1)} %collective-permute-done.2.gain_sib) | copy-start | bytes 9220
  113.8 181.0 %reduce-scatter.4.cloned.1.call-start = ((), (), s32[]{:S(2)}) async-start(), calls=%async_computation.3 | async-start | bytes 5898240
  238.5 6.1 copy-start.3
  238.6 114.4 %all-reduce.15.cloned.1.call-start = ((), (), s32[]{:S(2)}) async-start(), calls=%async_computation.4 | async-start | bytes 983040 | tf_op jit(solution)/shard_map/psum | solution.py:703
  238.6 6.1 collective-permute-start.3
  238.7 59.8 %collective-permute-start.4 = (bf16[2048,768]{1,0:T(8,128)(2,1)}, bf16[2048,768]{1,0:T(8,128)(2,1)}, u32[]{:S(2)}, u32[]{:S(2)}) collective-permute-start(bf16[2048,768]{1,0:T(8,128)(2,1)} %get-tuple-element.47), channel_id=1, source_target_pairs={{0,4},{4,0},{1,5},{5,1},{2,6},{6,2},{3,7},{7,3},{8,12},{12,8},{9,1... | collective-permute-start | bytes 9437192 | tf_op jit(solution)/shard_map/ppermute | solution.py:673
  297.0 6.7 %copy-start.2 = (bf16[1424,384]{1,0:T(8,128)(2,1)}, bf16[1424,384]{1,0:T(8,128)(2,1)S(1)}, u32[]{:S(2)}) copy-start(bf16[1424,384]{1,0:T(8,128)(2,1)S(1)} %copy.83) | copy-start | bytes 3280900
  297.2 0.9 copy-start.5
  298.2 281.5 %all-reduce.17.cloned.1.call-start = ((), (), s32[]{:S(2)}) async-start(), calls=%async_computation.5 | async-start | bytes 12582912 | tf_op jit(solution)/shard_map/psum | solution.py:592
  303.8 1.9 copy-start.1
  305.7 3.3 copy-start.4
  305.7 3.8 copy-start.11
  639.0 4.9 collective-permute-start.5
Sparse Core Ops, SparseCore 0:
  16.4 56.7 all-gather.1
  113.9 53.5 all-reduce.12
  238.7 56.0 reduce-scatter.3
  298.3 54.6 all-reduce.14
  355.8 223.8 all-reduce.16

commit v2 on v1

--- a/solution.py
+++ b/solution.py
@@ -68,15 +68,205 @@
     return step_arg, step, cumul, last, cols
 
 
+MESH = pl.DeviceIdType.MESH
+
+
+def send(src, dst, sems, at, **device):
+    return pltpu.make_async_remote_copy(
+        src_ref=src,
+        dst_ref=dst,
+        send_sem=sems[0].at[at],
+        recv_sem=sems[1].at[at],
+        device_id=device,
+        device_id_type=MESH,
+    )
+
+
+def group_peers(row_count, col_count):
+    row_at, col_at = lax.axis_index("row"), lax.axis_index("col")
+    return [
+        dict(row=lax.rem(row_at + j, row_count), col=lax.rem(col_at + k, col_count))
+        for k in range(col_count)
+        for j in range(row_count)
+        if (j, k) != (0, 0)
+    ]
+
+
+def greet(peers):
+    barrier = pltpu.get_barrier_semaphore()
+    for peer in peers:
+        pl.semaphore_signal(barrier, inc=1, device_id=peer, device_id_type=MESH)
+    pl.semaphore_wait(barrier, len(peers))
+
+
+def add_low(left, right):
+    return (left.astype(F32) + right.astype(F32)).astype(BF16)
+
+
+class Chain:
+    def __init__(self, own, sib, bufs, sems, result, q, place):
+        self.place = place
+        self.own, self.sib, self.result, self.q = own, sib, result, q
+        self.first, self.pair, self.cross = bufs
+        self.sems = sems
+        self.row_at, self.col_at = lax.axis_index("row"), lax.axis_index("col")
+        self.is_outer = (self.col_at == 0) | (self.col_at == 3)
+        self.inward = 1 + lax.div(self.col_at, 2)
+        self.outward = 3 * lax.div(self.col_at, 2)
+
+    def exchange(self, b):
+        return send(
+            self.sib.at[b], self.first.at[b], self.sems[0], b, row=1 - self.row_at
+        )
+
+    def to_inner(self, b):
+        return send(self.first.at[b], self.pair.at[b], self.sems[1], b, col=self.inward)
+
+    def across(self, b):
+        return send(self.pair.at[b], self.cross.at[b], self.sems[2], b, col=3 - self.col_at)
+
+    def rows(self, b):
+        return self.result.at[pl.ds(pl.multiple_of(self.place(b) * self.q, self.q), self.q)]
+
+    def to_outer(self, b):
+        return send(self.cross.at[b], self.rows(b), self.sems[3], b, col=self.outward)
+
+    def keep(self, b):
+        return pltpu.make_async_copy(self.cross.at[b], self.rows(b), self.sems[4].at[b])
+
+    def stage_first(self, b):
+        self.exchange(b).wait_recv()
+        self.first[b] = add_low(self.own[b], self.first[b])
+
+        @pl.when(self.is_outer)
+        def _():
+            self.to_inner(b).start()
+
+    def stage_pair(self, b):
+        @pl.when(~self.is_outer)
+        def _():
+            self.to_inner(b).wait_recv()
+            self.pair[b] = add_low(self.first[b], self.pair[b])
+            self.across(b).start()
+
+    def stage_cross(self, b):
+        @pl.when(~self.is_outer)
+        def _():
+            self.across(b).wait_recv()
+            self.cross[b] = add_low(self.pair[b], self.cross[b])
+            self.keep(b).start()
+            self.to_outer(b).start()
+
+    def progress(self, i):
+        for lag, stage in ((1, self.stage_first), (2, self.stage_pair), (3, self.stage_cross)):
+
+            @pl.when(i >= lag)
+            def _():
+                stage(i - lag)
+
+    def drain(self, blocks):
+        for extra in range(3):
+            for lag, stage in ((1, self.stage_first), (2, self.stage_pair), (3, self.stage_cross)):
+                if lag > extra:
+                    stage(blocks + extra - lag)
+
+        def finish(b, _):
+            self.exchange(b).wait_send()
+
+            @pl.when(self.is_outer)
+            def _():
+                self.to_inner(b).wait_send()
+                self.to_outer(b).wait_recv()
+
+            @pl.when(~self.is_outer)
+            def _():
+                self.across(b).wait_send()
+                self.to_outer(b).wait_send()
+                self.keep(b).wait()
+
+            return 0
+
+        lax.fori_loop(0, blocks, finish, 0)
+
+
+def chain_scratch(blocks, q, half):
+    dma = pltpu.SemaphoreType.DMA
+    buffers = [pltpu.VMEM((blocks, q, half), BF16) for _ in range(5)]
+    return buffers + [dma((blocks,)) for _ in range(9)]
+
+
+def chain_of(refs, result, q, place):
+    own, sib, first, pair, cross = refs[:5]
+    sems = [tuple(refs[5 + 2 * k : 7 + 2 * k]) for k in range(4)] + [refs[13]]
+    return Chain(own, sib, (first, pair, cross), sems, result, q, place)
+
+
+class Gather:
+    def __init__(self, mine, whole, sems, groups):
+        self.mine, self.whole, self.groups = mine, whole, groups
+        self.sems = sems
+        at = lax.axis_index("dp")
+        self.at = at
+        self.near = at + 1 - 2 * lax.rem(at, 2)
+        self.far = lax.rem(at + 2, 4)
+        self.share = mine.shape[1]
+
+    def part(self, shard, lo, hi):
+        return self.whole.at[
+            lo:hi, pl.ds(pl.multiple_of(shard * self.share, 128), self.share)
+        ]
+
+    def direct(self, g, to_near):
+        lo, _, hi = self.groups[g]
+        return send(
+            self.mine.at[lo:hi],
+            self.part(self.at, lo, hi),
+            self.sems[0 if to_near else 1],
+            g,
+            dp=self.near if to_near else self.far,
+        )
+
+    def onward(self, g, from_near):
+        lo, mid, hi = self.groups[g]
+        lo, hi = (lo, mid) if from_near else (mid, hi)
+        part = self.part(self.near if from_near else self.far, lo, hi)
+        return send(
+            part,
+            part,
+            self.sems[2 if from_near else 3],
+            g,
+            dp=self.far if from_near else self.near,
+        )
+
+    def start(self):
+        for g in range(len(self.groups)):
+            self.direct(g, True).start()
+            self.direct(g, False).start()
+
+    def take(self, g):
+        self.direct(g, True).wait_recv()
+        self.onward(g, True).start()
+        self.direct(g, False).wait_recv()
+        self.onward(g, False).start()
+        self.onward(g, True).wait_recv()
+        self.onward(g, False).wait_recv()
+
+    def finish(self):
+        for g in range(len(self.groups)):
+            for which in (True, False):
+                self.direct(g, which).wait_send()
+                self.onward(g, which).wait_send()
+
+
 def forward_kernel(
     dims,
+    mesh_dims,
     x_own,
-    x_sib,
     c_own,
-    c_sib,
-    weights,
+    x_any,
+    c_any,
+    weights_in,
     gain_own,
-    gain_sib,
     aux_ref,
     conv_ref,
     chan_ref,
@@ -91,45 +281,103 @@
     dng_out,
     state_out,
     stats_out,
-    out_own,
-    out_sib,
+    out_total,
+    c_out,
+    w_out,
     prev,
     state,
     act_scr,
+    x_scr,
+    c_scr,
+    gain_sib,
+    stats_scr,
+    swap_sems,
+    local_sems,
+    stat_sems,
+    *rest,
 ):
     nh, pc, ns, width = dims
+    row_count, col_count, gathers = mesh_dims
+    step_at = pl.program_id(0)
+    blocks = x_scr.shape[0]
     inner = nh * pc
     conv_rows = inner + 2 * ns
     gate_at = conv_rows + STEP_ROWS
     out_at = gate_at + inner
     half = x_own.shape[1]
     q = x_own.shape[0]
-    row_at = lax.axis_index("row")
+    row_at, col_at = lax.axis_index("row"), lax.axis_index("col")
     own_at = pl.multiple_of(row_at * half, 128)
     sib_at = pl.multiple_of((1 - row_at) * half, 128)
-
-    @pl.when(pl.program_id(0) == 0)
+    sib = dict(row=1 - row_at)
+    me = row_at * col_count + col_at
+    peers = group_peers(row_count, col_count)
+    chain = chain_of(rest[:14], out_total, q, lambda b: b)
+
+    def token_rows(ref, b):
+        return ref.at[pl.ds(pl.multiple_of(b * q, q), q)]
+
+    def swap(which, b):
+        src, dst = ((x_any, x_scr), (c_any, c_scr))[which]
+        sems = (swap_sems.at[2 * which], swap_sems.at[2 * which + 1])
+        return send(token_rows(src, b), dst.at[b], sems, b, **sib)
+
+    gain_swap = send(
+        gain_own, gain_sib, (swap_sems.at[0], swap_sems.at[1]), blocks, **sib
+    )
+
+    def keep_cot(b):
+        return pltpu.make_async_copy(c_scr.at[b], token_rows(c_out, b), local_sems.at[b])
+
+    def stat_copy(k):
+        return send(
+            stats_scr.at[me], stats_scr.at[me], (stat_sems.at[0], stat_sems.at[1]), k, **peers[k]
+        )
+
+    if gathers:
+        weights = rest[14]
+        bounds = ((0, 336, gate_at), (gate_at, gate_at + 192, out_at), (out_at, out_at + 192, out_at + inner))
+        gather = Gather(weights_in, weights, [tuple(rest[15 + 2 * k : 17 + 2 * k]) for k in range(4)], bounds)
+        others = [dict(dp=gather.near), dict(dp=gather.far)]
+        keep_weights = pltpu.make_async_copy(weights, w_out, local_sems.at[blocks])
+    else:
+        weights, gather, others = weights_in, None, []
+
+    @pl.when(step_at == 0)
     def _():
+        greet(peers + others)
+        if gathers:
+            gather.start()
+        gain_swap.start()
+        for b in range(blocks):
+            swap(0, b).start()
+            swap(1, b).start()
         prev[...] = jnp.zeros_like(prev)
         state[...] = jnp.zeros_like(state)
-
+        if gathers:
+            share = weights_in.shape[1]
+            mine_at = pl.multiple_of(lax.axis_index("dp") * share, 128)
+            weights[:, pl.ds(mine_at, share)] = weights_in[...]
+        gain_swap.wait_recv()
+        if gathers:
+            gather.take(0)
+
+    swap(0, step_at).wait_recv()
     xo = x_own[...].astype(F32)
-    xs = x_sib[...].astype(F32)
+    xs = x_scr[step_at].astype(F32)
     squares = jnp.sum(xo * xo, axis=1, keepdims=True) + jnp.sum(xs * xs, axis=1, keepdims=True)
     scaling = lax.rsqrt(squares / width + EPSILON)
     no = (xo * scaling * gain_own[...]).astype(BF16)
     nsib = (xs * scaling * gain_sib[...]).astype(BF16)
     normed_own[...] = no
     normed_sib[...] = nsib
-    pre = dot_nt(weights[0:out_at, pl.ds(own_at, half)], no) + dot_nt(
-        weights[0:out_at, pl.ds(sib_at, half)], nsib
+    pre = dot_nt(weights[0:gate_at, pl.ds(own_at, half)], no) + dot_nt(
+        weights[0:gate_at, pl.ds(sib_at, half)], nsib
     )
     values = pre[0:conv_rows]
     step_pre = pre[conv_rows:gate_at]
-    gate = pre[gate_at:out_at]
     pre_out[...] = values
     step_out[...] = step_pre
-    gate_out[...] = gate
     aux = aux_ref[...]
     conv = conv_ref[...]
     joined = jnp.concatenate([prev[...], values], axis=1)
@@ -175,26 +423,69 @@
         y_h = jnp.concatenate([y_top[:, :hq], y_top[:, hq:] + y_low], axis=1)
         y_h = y_h + from_state[lo : lo + pc] * reach[h : h + 1]
         mixed_out[lo : lo + pc] = y_h + gain[lo : lo + pc, 1:2] * x_h
+    chain.progress(step_at)
     contrib = dot_nt(jnp.concatenate(tail_parts, axis=0), in_low)
     for h in range(nh):
         lo = h * pc
         state[lo : lo + pc] = keep[h : h + 1] * entering[lo : lo + pc] + contrib[lo : lo + pc]
+    if gathers:
+
+        @pl.when(step_at == 0)
+        def _():
+            gather.take(1)
+
+    gate = dot_nt(weights[gate_at:out_at, pl.ds(own_at, half)], no) + dot_nt(
+        weights[gate_at:out_at, pl.ds(sib_at, half)], nsib
+    )
+    gate_out[...] = gate
     gated = mixed_out[...] * (gate * sigmoid(gate))
     squares_row = jnp.sum(gated * gated, axis=0, keepdims=True)
     weighted = gated * gain[:, 0:1]
     low = weighted.astype(BF16)
-    out_own[...] = dot_tn(low, weights[out_at:, pl.ds(own_at, half)]).astype(BF16)
-    out_sib[...] = dot_tn(low, weights[out_at:, pl.ds(sib_at, half)]).astype(BF16)
+    if gathers:
+
+        @pl.when(step_at == 0)
+        def _():
+            gather.take(2)
+            keep_weights.start()
+
+    chain.sib[step_at] = dot_tn(low, weights[out_at:, pl.ds(sib_at, half)]).astype(BF16)
+    chain.exchange(step_at).start()
+    chain.own[step_at] = dot_tn(low, weights[out_at:, pl.ds(own_at, half)]).astype(BF16)
+    swap(1, step_at).wait_recv()
+    keep_cot(step_at).start()
     dng = dot_nt(weights[out_at:, pl.ds(own_at, half)], c_own[...]) + dot_nt(
-        weights[out_at:, pl.ds(sib_at, half)], c_sib[...]
+        weights[out_at:, pl.ds(sib_at, half)], c_scr[step_at]
     )
     dng_out[...] = dng
     dot_row = jnp.sum(dng * weighted, axis=0, keepdims=True)
-    stats_out[...] = jnp.concatenate([squares_row, dot_row, jnp.zeros((6, q), F32)], axis=0)
+    stats_scr[me, pl.ds(step_at, 1)] = squares_row
+    stats_scr[me, pl.ds(blocks + step_at, 1)] = dot_row
+
+    @pl.when(step_at == blocks - 1)
+    def _():
+        for k in range(len(peers)):
+            stat_copy(k).start()
+        chain.drain(blocks)
+        for k in range(len(peers)):
+            stat_copy(k).wait()
+        total = stats_scr[0]
+        for k in range(1, len(peers) + 1):
+            total = total + stats_scr[k]
+        stats_out[...] = total
+        gain_swap.wait_send()
+        for b in range(blocks):
+            swap(0, b).wait_send()
+            swap(1, b).wait_send()
+            keep_cot(b).wait()
+        if gathers:
+            gather.finish()
+            keep_weights.wait()
 
 
 def backward_kernel(
     dims,
+    mesh_dims,
     normed_own,
     normed_sib,
     c_own,
@@ -212,8 +503,7 @@
     dng_ref,
     state_ref,
     stats_ref,
-    dn_own,
-    dn_sib,
+    dn_total,
     grad_w,
     conv_grad,
     chan_grad,
@@ -226,8 +516,12 @@
     acc_head,
     du_scr,
     low_scr,
+    *rest,
 ):
     nh, pc, ns, width = dims
+    row_count, col_count, _ = mesh_dims
+    step_at = pl.program_id(0)
+    blocks = stats_ref.shape[0] // 2
     inner = nh * pc
     conv_rows = inner + 2 * ns
     gate_at = conv_rows + STEP_ROWS
@@ -239,8 +533,14 @@
     own_at = pl.multiple_of(row_at * half, 128)
     sib_at = pl.multiple_of((1 - row_at) * half, 128)
 
-    @pl.when(pl.program_id(0) == 0)
+    chain = chain_of(rest, dn_total, q, lambda b: blocks - 1 - b)
+    block_at = blocks - 1 - step_at
+
+    @pl.when(step_at == 0)
     def _():
+        greet(
+            [dict(row=1 - row_at), dict(col=lax.rem(chain.col_at + 1, col_count)), dict(col=lax.rem(chain.col_at + 3, col_count))]
+        )
         after[...] = jnp.zeros_like(after)
         d_state[...] = jnp.zeros_like(d_state)
         acc_w[...] = jnp.zeros_like(acc_w)
@@ -252,9 +552,9 @@
     conv = conv_ref[...]
     chan = chan_ref[...]
     hrow = hrow_ref[...]
-    stats = stats_ref[...]
-    gate_scale = lax.rsqrt(stats[0:1] / inner_width + EPSILON)
-    pull = gate_scale * gate_scale * gate_scale * stats[1:2] / inner_width
+    gate_scale = lax.rsqrt(stats_ref[pl.ds(block_at, 1)] / inner_width + EPSILON)
+    gate_dot = stats_ref[pl.ds(blocks + block_at, 1)]
+    pull = gate_scale * gate_scale * gate_scale * gate_dot / inner_width
     gate = gate_ref[...]
     sig = sigmoid(gate)
     silu = gate * sig
@@ -328,6 +628,7 @@
         x_sums.append(jnp.sum(x_h * du, axis=0, keepdims=True))
         flow = jnp.sum(entering[lo : lo + pc] * d_next[lo : lo + pc], axis=0, keepdims=True)
         carry_sums.append(flow)
+    chain.progress(step_at)
     pad_rows = [jnp.zeros((STEP_ROWS - nh, q), F32)]
     row_sum = jnp.concatenate(row_sums + pad_rows, axis=0)
     col_sum = jnp.concatenate(col_sums + pad_rows, axis=0)
@@ -375,8 +676,9 @@
         acc_conv[3 - offset] += lane_fold(shifted * values)
     low_scr[0:conv_rows] = d_pre.astype(BF16)
     low = low_scr[...]
-    dn_own[...] = dot_tn(low, weights[0:out_at, pl.ds(own_at, half)]).astype(BF16)
-    dn_sib[...] = dot_tn(low, weights[0:out_at, pl.ds(sib_at, half)]).astype(BF16)
+    chain.sib[step_at] = dot_tn(low, weights[0:out_at, pl.ds(sib_at, half)]).astype(BF16)
+    chain.exchange(step_at).start()
+    chain.own[step_at] = dot_tn(low, weights[0:out_at, pl.ds(own_at, half)]).astype(BF16)
     acc_w[0:out_at, pl.ds(own_at, half)] += dot_nn(low, normed_own[...])
     acc_w[0:out_at, pl.ds(sib_at, half)] += dot_nn(low, normed_sib[...])
 
@@ -394,6 +696,7 @@
         conv_grad[...] = gather_columns(acc_conv, 5)
         chan_grad[...] = gather_columns(acc_chan, 2)
         head_grad[...] = gather_columns(acc_head, 2)
+        chain.drain(blocks)
 
 
 def per_device(
@@ -446,11 +749,12 @@
         ],
         axis=0,
     ).astype(BF16)
-    weights = lax.all_gather(stacked, "dp", axis=1, tiled=True)
-    x_sib = lax.ppermute(inputs, "row", swap)
-    c_sib = lax.ppermute(cotangent, "row", swap)
+    gathers = lax.axis_size("dp") == 4 and share % 128 == 0
+    if not gathers:
+        stacked = lax.all_gather(stacked, "dp", axis=1, tiled=True)
     gain_own = norm_gain[None, :]
-    gain_sib = lax.ppermute(gain_own, "row", swap)
+    mesh_dims = (row_count, col_count, gathers)
+    group = row_count * col_count
 
     seg = segments[0]
     seg_blocks = seg.reshape(blocks, q)
@@ -503,16 +807,15 @@
 
     sds = jax.ShapeDtypeStruct
     forward = pl.pallas_call(
-        functools.partial(forward_kernel, dims),
+        functools.partial(forward_kernel, dims, mesh_dims),
         name="forward",
         grid=(blocks,),
         in_specs=[
             token_block(up),
             token_block(up),
-            token_block(up),
-            token_block(up),
-            whole(rows, width),
-            whole(1, half),
+            pl.BlockSpec(memory_space=pl.ANY),
+            pl.BlockSpec(memory_space=pl.ANY),
+            whole(*stacked.shape),
             whole(1, half),
             lane_block(8, up),
             whole(conv_rows, 8),
@@ -529,9 +832,10 @@
             lane_block(inner, up),
             lane_block(inner, up),
             pl.BlockSpec((1, inner, ns), lambda i: (i, 0, 0)),
-            lane_block(8, up),
-            token_block(up),
-            token_block(up),
+            whole(2 * blocks, q),
+            pl.BlockSpec(memory_space=pl.ANY),
+            pl.BlockSpec(memory_space=pl.ANY),
+            pl.BlockSpec(memory_space=pl.ANY),
         ],
         out_shape=[
             sds((length, half), BF16),
@@ -543,16 +847,32 @@
             sds((inner, length), F32),
             sds((inner, length), F32),
             sds((blocks, inner, ns), F32),
-            sds((8, length), F32),
+            sds((2 * blocks, q), F32),
             sds((length, half), BF16),
             sds((length, half), BF16),
+            sds((rows, width) if gathers else (16, 128), BF16),
         ],
         scratch_shapes=[
             pltpu.VMEM((conv_rows, 128), F32),
             pltpu.VMEM((inner, ns), F32),
             pltpu.VMEM((inner, q), F32),
-        ],
-        compiler_params=pltpu.CompilerParams(vmem_limit_bytes=56 << 20),
+            pltpu.VMEM((blocks, q, half), BF16),
+            pltpu.VMEM((blocks, q, half), BF16),
+            pltpu.VMEM((1, half), F32),
+            pltpu.VMEM((group, 2 * blocks, q), F32),
+            pltpu.SemaphoreType.DMA((4, blocks + 1)),
+            pltpu.SemaphoreType.DMA((blocks + 1,)),
+            pltpu.SemaphoreType.DMA((2, group - 1)),
+        ]
+        + chain_scratch(blocks, q, half)
+        + (
+            [pltpu.VMEM((rows, width), BF16)] + [pltpu.SemaphoreType.DMA((3,)) for _ in range(8)]
+            if gathers
+            else []
+        ),
+        compiler_params=pltpu.CompilerParams(
+            vmem_limit_bytes=60 << 20, collective_id=1, has_side_effects=True
+        ),
         cost_estimate=pl.CostEstimate(
             flops=2 * length * width * (out_at + 2 * inner),
             bytes_accessed=50 << 20,
@@ -570,32 +890,29 @@
         dng_vals,
         states,
         stats,
-        out_own,
-        out_sib,
+        out_sum,
+        c_sib,
+        weights,
     ) = forward(
         inputs,
-        x_sib,
         cotangent,
-        c_sib,
-        weights,
+        inputs,
+        cotangent,
+        stacked,
         gain_own,
-        gain_sib,
         aux,
         conv_par,
         chan_par,
         head_par,
     )
-    stats = lax.psum(stats, ("row", "col"))
-
-    out_recv = lax.ppermute(out_sib, "row", swap)
-    out_pair = (out_own.astype(F32) + out_recv.astype(F32)).astype(BF16)
-    out_sum = lax.psum(out_pair, "col")
-    gate_scale = lax.rsqrt(stats[0] / (H * P_SIZE) + EPSILON)
+    if not gathers:
+        weights = stacked
+    gate_scale = lax.rsqrt(stats[:blocks].reshape(length) / (H * P_SIZE) + EPSILON)
     plain = inputs.astype(F32)
     output = (plain + gate_scale[:, None] * out_sum.astype(F32)).astype(BF16)
 
     backward = pl.pallas_call(
-        functools.partial(backward_kernel, dims),
+        functools.partial(backward_kernel, dims, mesh_dims),
         name="backward",
         grid=(blocks,),
         in_specs=[
@@ -615,18 +932,16 @@
             lane_block(inner, down),
             lane_block(inner, down),
             pl.BlockSpec((1, inner, ns), lambda i: (down(i), 0, 0)),
-            lane_block(8, down),
+            whole(2 * blocks, q),
         ],
         out_specs=[
-            token_block(down),
-            token_block(down),
+            pl.BlockSpec(memory_space=pl.ANY),
             whole(rows, width),
             whole(conv_rows, 128),
             whole(inner, 128),
             whole(STEP_ROWS, 128),
         ],
         out_shape=[
-            sds((length, half), BF16),
             sds((length, half), BF16),
             sds((rows, width), BF16),
             sds((conv_rows, 128), F32),
@@ -642,15 +957,18 @@
             pltpu.VMEM((2, STEP_ROWS, 128), F32),
             pltpu.VMEM((inner, q), F32),
             pltpu.VMEM((out_at, q), BF16),
-        ],
-        compiler_params=pltpu.CompilerParams(vmem_limit_bytes=60 << 20),
+        ]
+        + chain_scratch(blocks, q, half),
+        compiler_params=pltpu.CompilerParams(
+            vmem_limit_bytes=60 << 20, collective_id=2, has_side_effects=True
+        ),
         cost_estimate=pl.CostEstimate(
             flops=4 * length * width * (out_at + inner),
             bytes_accessed=60 << 20,
             transcendentals=nh * length * q,
         ),
     )
-    dn_own, dn_sib, grad_w, conv_grad, chan_grad, head_grad = backward(
+    dn_total, grad_w, conv_grad, chan_grad, head_grad = backward(
         normed_own,
         normed_sib,
         cotangent,
@@ -670,15 +988,12 @@
         stats,
     )
 
-    dn_recv = lax.ppermute(dn_sib, "row", swap)
-    dn_pair = (dn_own.astype(F32) + dn_recv.astype(F32)).astype(BF16)
-    d_half = lax.psum(dn_pair, "col").astype(F32)
-    x_sib_plain = x_sib.astype(F32)
-    squares = jnp.sum(plain * plain, axis=1) + jnp.sum(x_sib_plain * x_sib_plain, axis=1)
-    scaling = lax.rsqrt(squares / width + EPSILON)
+    d_half = dn_total.astype(F32)
     weighted = d_half * gain_own
-    dot_own = jnp.sum(weighted * plain, axis=1)
-    input_dot = dot_own + lax.ppermute(dot_own, "row", swap)
+    sums = jnp.stack([jnp.sum(weighted * plain, axis=1), jnp.sum(plain * plain, axis=1)])
+    sums = sums + lax.ppermute(sums, "row", swap)
+    input_dot = sums[0]
+    scaling = lax.rsqrt(sums[1] / width + EPSILON)
     grad_inputs = (
         cotangent.astype(F32)
         + scaling[:, None] * weighted

time: 659 us -> 436 us (0.66)
  waiting for transfers between devices: 417 us -> 52.6 us
  Pallas kernels: 105 us -> 255 us
  other arithmetic: 31.4 us -> 20.2 us
  blocking collectives: 52 us -> 60.9 us
    psum x2 -> x0, waiting for transfers between devices: 277 us -> none  [the longest x1 223 us: per_device(): out_sum = lax.psum(out_pair, 'col')]
    pallas_call x1, Pallas kernels: 40.6 us -> 147 us  [per_device(): forward(inputs, cotangent, inputs, cotangent, stacked, gain_own, aux, con...]
    all_gather x1 -> x0, waiting for transfers between devices: 46.2 us -> none  [per_device(): weights = lax.all_gather(stacked, 'dp', axis=1, tiled=True)]
    unnamed x6 -> x3, waiting for transfers between devices: 45.8 us -> 0.03 us
    pallas_call x1, Pallas kernels: 64.4 us -> 108 us  [per_device(): backward(normed_own, normed_sib, cotangent, c_sib, weights, aux, conv_par...]
    psum x1, waiting for transfers between devices: 39.1 us -> 52.6 us  [per_device(): lax.psum((grads[inner:conv_rows], step_wide, conv_sum[:, inner:], head_al...]
    convert_element_type x2 -> x0, other arithmetic: 9.67 us -> none  [the longest x1 5.3 us: per_device(): dn_pair = (dn_own.astype(F32) + dn_recv.astype(F32)).astype(BF16)]
    ppermute x6 -> x1, waiting for transfers between devices: 9.07 us -> 0.01 us  [per_device(): sums = sums + lax.ppermute(sums, 'row', swap)]
  transfers between devices with their start and end apart: 11 -> 3, of which waited for: 9 -> 1; matrix products, arithmetic and copies ran while one was open for 5% -> 4% of each run, Pallas kernels for 0% -> 0%
where the time goes in v2:
time: 436 us; the launch traced here: 435 us
  Pallas kernels  255 us (58%)
  blocking collectives  60.9 us (14%)
  waiting for transfers between devices  52.6 us (12%)
  local copies, waits for them, and re-layouts  31.1 us (7%)
  other arithmetic  20.2 us (5%)
  between operations  14.4 us (3%)
    pallas_call x1, Pallas kernels, per_device(): forward(inputs, cotangent, inputs, cotangent, stacked, gain_own, aux, con...  147 us
    pallas_call x1, Pallas kernels, per_device(): backward(normed_own, normed_sib, cotangent, c_sib, weights, aux, conv_par...  108 us
    psum x1, waiting for transfers between devices, per_device(): lax.psum((grads[inner:conv_rows], step_wide, conv_sum[:, inner:], head_al...  52.6 us
    psum x1, blocking collectives, per_device(): lax.psum((grads[inner:conv_rows], step_wide, conv_sum[:, inner:], head_al...  31 us
    psum x1, blocking collectives, per_device(): lax.psum((grad_norm, conv_grad[:, :5].T, chan_grad[:, 0], head_all), 'dp')  29.9 us
    unnamed x43, local copies, waits for them, and re-layouts  17.4 us
  transfers between devices with their start and end apart: 3, of which 1 were waited for; matrix products, arithmetic and copies ran while one was open for 4% of the time, Pallas kernels for 0%

profile of v2, /device:TPU:0, one launch (start us, length us, event | category | flops | bytes accessed | tf_op | source)
XLA Modules:
  0.0 434.6 jit_solution(7503429878878621566)
XLA Ops:
  7.3 0.5 broadcast.81
  7.8 1.4 fusion.23
  9.2 0.1 slice.108
  9.3 0.1 slice.109
  9.4 0.1 copy.84
  9.5 0.1 pad_add_fusion
  9.6 0.1 broadcast_bitcast_fusion.2
  9.6 0.1 copy.85
  9.7 0.1 compare_convert_fusion.2
  10.0 0.9 fusion.16
  10.9 0.7 copy.74
  11.6 0.1 reshape.122
  11.7 0.8 reshape.123
  12.5 0.7 pad_maximum_fusion.1
  13.2 0.1 pad.38.clone
  13.3 0.8 maximum_maximum_fusion
  14.0 0.9 copy.75
  14.9 0.7 broadcast_in_dim.42
  15.6 0.1 broadcast_in_dim_reshape.3
  15.7 0.8 reshape.124
  16.5 0.1 pad.34.clone
  16.6 0.1 maximum_maximum_fusion.1
  16.6 0.8 copy.76
  17.5 0.7 fusion.20
  18.1 0.7 pad_maximum_fusion.2
  18.8 0.1 copy.77
  18.9 0.6 pad.25.hrow_ref
  19.5 1.1 convert.28
  20.6 1.2 copy.71
  21.8 0.7 convert_bitcast_fusion
  22.7 0.6 broadcast_in_dim.38.gain_own
  23.5 0.9 stack.46.aux_ref
  24.3 0.1 copy-done.5
  24.4 146.8 %forward.1 = (bf16[2048,768]{1,0:T(8,128)(2,1)}, bf16[2048,768]{1,0:T(8,128)(2,1)}, f32[640,2048]{1,0:T(8,128)}, f32[640,2048]{1,0:T(8,128)}, f32[384,2048]{1,0:...) custom-call(bf16[2048,768]{1,0:T(8,128)(2,1)} %x_any.1, ...), custom_call_target="tpu_custom_call" | custom-call | flops 11374952448 | bytes 52428800 | tf_op jit(solution)/shard_map/forward/pallas_call | solution.py:896
  171.2 108.1 %backward.1 = (bf16[2048,768]{1,0:T(8,128)(2,1)}, bf16[1424,1536]{1,0:T(8,128)(2,1)}, f32[640,128]{1,0:T(8,128)}, f32[384,128]{1,0:T(8,128)}, f32[16,128]{1,0:T(8,128)}) custom-call(bf16[2048,768]{1,0:T(8,128)(2,1)} %get-tuple-element.36.normed_own, bf16[2048,768]{1,0:T(8,128)(2,1)} %get-tuple-element.37.normed_sib, bf16[2048,768]{1,0:T(8,128)(2,1)} %c_own.3, ...), custom_call_target="tpu_custom_call" | custom-call | flops 17918066688 | bytes 62914560 | tf_op jit(solution)/shard_map/backward/pallas_call | solution.py:971
  279.4 6.5 %copy.82 = bf16[1424,1536]{0,1:T(8,128)(2,1)} copy(bf16[1424,1536]{1,0:T(8,128)(2,1)} %get-tuple-element.48) | data formatting | bytes 8749056
  285.9 0.3 all-reduce.10.cloned.1.call-start
  286.2 1.6 copy-done
  287.8 3.4 fusion.4
  291.4 0.3 slice_reduce_fusion.1
  291.6 0.1 reshape_squeeze.11
  291.7 0.6 reduce_sum.39
  292.3 0.1 copy.78
  292.4 1.0 slice_bitcast_fusion.1
  293.5 0.7 fusion.19
  294.1 0.1 reshape.128
  294.3 7.4 %fusion.7 = (f32[768]{0:T(1024)S(1)}, f32[2048,768]{1,0:T(8,128)}, bf16[2048,768]{1,0:T(8,128)(2,1)}) fusion(bf16[2048,768]{1,0:T(8,128)(2,1)S(1)} %copy-done, bf16[2048,768]{1,0:T(8,128)(2,1)} %get-tuple-element.47, f32[2048]{0:T(1024)S(1)} %bitcast.97, f32[2048]{0:T(1024)S(1)} %fusion.13, f32[768]{0:T(1024)S(1)} %copy-done.7, bf16[2048,768]{1,0:T(8,128)(2,1)} %c_own.3, ...), kind=kLoop, calls=%fused_computation.13 | loop fusion | flops 23592192 | bytes 22050816 | tf_op jit(solution)/shard_map/reduce_sum | solution.py:1002
  301.7 29.9 %all-reduce.7 = (f32[768]{0:T(1024)}, f32[5,640]{0,1:T(8,128)S(1)}, f32[4,3,12]{2,1,0:T(4,128)S(1)}, f32[12,32]{1,0:T(8,128)}) all-reduce(f32[768]{0:T(1024)S(1)} %get-tuple-element.128, f32[5,640]{0,1:T(8,128)S(1)} %slice_bitcast_fusion.1, f32[4,3,12]{2,1,0:T(4,128)S(1)} %fusion.19, ...), channel_id=1, replica_groups=mesh['dp'=4,'row'=2,'col'=4] {'dp'}, use_global_device_ids=true, to_apply=%region_3.4 | all-reduce | flops 4496 | bytes 35968 | tf_op jit(solution)/shard_map/psum | solution.py:1015
  331.7 31.0 %all-reduce.5 = (f32[5,256]{0,1:T(8,128)S(1)}, f32[4,3,12]{2,1,0:T(4,128)S(1)}) all-reduce(f32[5,256]{0,1:T(8,128)S(1)} %slice.118, f32[4,3,12]{2,1,0:T(4,128)S(1)} %get-tuple-element.126), channel_id=1, replica_groups=mesh['dp'=4,'row'=2,'col'=4] {'row','col'}, use_global_device_ids=true, to_apply=%region_8.9 | all-reduce | flops 1424 | bytes 11392 | tf_op jit(solution)/shard_map/psum | solution.py:1018
  362.7 0.7 copy.81
  363.4 0.7 copy.80
  364.1 0.2 slice_reduce_fusion
  364.3 0.7 reshape_squeeze.10
  365.0 0.7 slice_reduce_fusion.3
  365.8 0.5 slice_bitcast_fusion.4
  366.3 0.5 bitcast_multiply_fusion
  366.8 2.2 copy.83
  369.0 0.1 convert_element_type.50
  369.2 0.8 slice_bitcast_fusion
  370.0 0.6 copy-done.4
  370.6 1.2 fusion.22
  371.9 52.6 %all-reduce.10.cloned.1.call-done = (f32[384,256]{0,1:T(8,128)}, f32[4,12,384]{2,1,0:T(8,128)}) async-done(((f32[384,256]{0,1:T(8,128)}, f32[4,12,384]{2,1,0:T(8,128)}), (f32[384,256]{0,1:T(8,128)}, f32[4,12,384]{2,1,0:T(8,128)})) %all-reduce.10.cloned.1.call-update) | async-done | bytes 466960 | tf_op jit(solution)/shard_map/psum | solution.py:1018
  424.5 1.9 copy.79
  426.4 1.3 dynamic-slice_bitcast_fusion
  (56 shorter events, 0.8 us)
Async XLA Ops:
  7.2 16.1 %copy-start.6 = (s32[1,2048]{1,0:T(1,128)S(1)}, s32[1,2048]{1,0:T(1,128)}, u32[]{:S(2)}) copy-start(s32[1,2048]{1,0:T(1,128)} %param.18) | copy-start | bytes 24580
  7.2 15.4 %copy-start.2 = (f32[384,12,32]{0,2,1:T(8,128)S(1)}, f32[384,12,32]{0,2,1:T(8,128)}, u32[]{:S(2)}) copy-start(f32[384,12,32]{0,2,1:T(8,128)} %param.21) | copy-start | bytes 1769476
  7.2 15.4 %copy-start.3 = (f32[384,12,32]{0,2,1:T(8,128)S(1)}, f32[384,12,32]{0,2,1:T(8,128)}, u32[]{:S(2)}) copy-start(f32[384,12,32]{0,2,1:T(8,128)} %param.33) | copy-start | bytes 1769476
  7.2 15.4 %copy-start.7 = (f32[768]{0:T(1024)S(1)}, f32[768]{0:T(1024)}, u32[]{:S(2)}) copy-start(f32[768]{0:T(1024)} %param.20) | copy-start | bytes 9220
  7.2 359.6 %reduce-scatter.4.cloned.1.call-start = ((), (), s32[]{:S(2)}) async-start(), calls=%async_computation.1 | async-start | bytes 5898240
  23.4 1.0 copy-start.5
  285.9 1.9 copy-start
  285.9 138.5 %all-reduce.10.cloned.1.call-start = ((), (), s32[]{:S(2)}) async-start(), calls=%async_computation.2 | async-start | bytes 983040 | tf_op jit(solution)/shard_map/psum | solution.py:1018
  287.8 3.6 copy-start.1
  287.8 4.5 %copy-start.8 = (f32[16,128]{1,0:T(8,128)S(1)}, f32[16,128]{1,0:T(8,128)}, u32[]{:S(2)}) copy-start(f32[16,128]{1,0:T(8,128)} %get-tuple-element.50) | copy-start | bytes 24580
  287.8 4.6 %copy-start.9 = (f32[16,256]{1,0:T(8,128)S(1)}, f32[16,256]{1,0:T(8,128)}, u32[]{:S(2)}) copy-start(f32[16,256]{1,0:T(8,128)} %get-tuple-element.34.stats_ref) | copy-start | bytes 49156
  291.3 2.9 collective-permute-start
  294.3 72.0 %copy-start.10 = (f32[12]{0:T(128)S(1)}, f32[12]{0:T(128)}, u32[]{:S(2)}) copy-start(f32[12]{0:T(128)} %param.30) | copy-start | bytes 148
  370.0 0.6 copy-start.4
Sparse Core Ops, SparseCore 0:
  286.1 65.4 reduce-scatter.3
  370.7 53.6 all-reduce.9

commit v3 on v2

--- a/solution.py
+++ b/solution.py
@@ -52,6 +52,23 @@
 def columns_of(rows):
     padded = jnp.concatenate([rows, jnp.zeros((128 - rows.shape[0], rows.shape[1]), F32)], axis=0)
     return padded.T
+
+
+def rows_of(ref):
+    lanes = lax.broadcasted_iota(jnp.int32, ref.shape[1:], 1)
+    total = jnp.zeros(ref.shape[1:], F32)
+    for at in range(ref.shape[0]):
+        total = jnp.where(lanes == at, jnp.sum(ref[at], axis=1, keepdims=True), total)
+    if total.shape[0] % 128:
+        total = jnp.concatenate([total, jnp.zeros((128 - total.shape[0], 128), F32)], axis=0)
+    return total.T[0:8]
+
+
+def load_columns(par_rows, head_rows, conv_scr, head_scr):
+    conv_scr[...] = columns_of(par_rows[...])
+    heads = columns_of(head_rows[...])[0:STEP_ROWS]
+    lanes = lax.broadcasted_iota(jnp.int32, heads.shape, 1)
+    head_scr[...] = jnp.where(lanes == 1, -jnp.exp(heads), heads)
 
 
 def block_rows(dims, step_pre, hrow, aux):
@@ -96,7 +113,10 @@
     barrier = pltpu.get_barrier_semaphore()
     for peer in peers:
         pl.semaphore_signal(barrier, inc=1, device_id=peer, device_id_type=MESH)
-    pl.semaphore_wait(barrier, len(peers))
+
+
+def greeted(peers):
+    pl.semaphore_wait(pltpu.get_barrier_semaphore(), len(peers))
 
 
 def add_low(left, right):
@@ -164,12 +184,12 @@
             def _():
                 stage(i - lag)
 
-    def drain(self, blocks):
-        for extra in range(3):
-            for lag, stage in ((1, self.stage_first), (2, self.stage_pair), (3, self.stage_cross)):
-                if lag > extra:
-                    stage(blocks + extra - lag)
-
+    def drain(self, blocks, extra):
+        for lag, stage in ((1, self.stage_first), (2, self.stage_pair), (3, self.stage_cross)):
+            if lag > extra:
+                stage(blocks + extra - lag)
+
+    def finish(self, blocks):
         def finish(b, _):
             self.exchange(b).wait_send()
 
@@ -258,6 +278,75 @@
                 self.onward(g, which).wait_send()
 
 
+class Reduce:
+    def __init__(self, acc, stage, split, rows, bufs, sems):
+        self.acc, self.stage = acc, stage
+        self.halves = ((0, split), (split, rows))
+        self.bufs, self.sems = bufs, sems
+        at = lax.axis_index("dp")
+        self.at = at
+        self.near = at + 1 - 2 * lax.rem(at, 2)
+        self.far = lax.rem(at + 2, 4)
+        self.share = acc.shape[1] // 4
+
+    def cols(self, shard):
+        return pl.ds(pl.multiple_of(shard * self.share, 128), self.share)
+
+    def first(self, half, slot):
+        lo, hi = self.halves[half]
+        to = (self.near, self.far)[half]
+        shard = to if slot == 0 else 3 - self.at
+        return send(
+            self.stage.at[lo:hi, self.cols(shard)],
+            self.bufs[half].at[slot],
+            self.sems[half],
+            slot,
+            dp=to,
+        )
+
+    def second(self, half):
+        return send(
+            self.bufs[half].at[1],
+            self.bufs[2 + half],
+            self.sems[half],
+            2,
+            dp=(self.far, self.near)[half],
+        )
+
+    def start(self):
+        for slot in (1, 0):
+            for half in range(2):
+                self.first(half, slot).start()
+
+    def middle(self):
+        for half in range(2):
+            lo, hi = self.halves[half]
+            other = (self.far, self.near)[half]
+            self.first(half, 1).wait_recv()
+            self.bufs[half][1] = (
+                self.acc[lo:hi, self.cols(other)] + self.bufs[half][1].astype(F32)
+            ).astype(BF16)
+            self.second(half).start()
+
+    def end(self):
+        for half in range(2):
+            lo, hi = self.halves[half]
+            self.first(half, 0).wait_recv()
+            self.second(half).wait_recv()
+            mine = self.cols(self.at)
+            self.acc[lo:hi, mine] = (
+                self.acc[lo:hi, mine]
+                + self.bufs[half][0].astype(F32)
+                + self.bufs[2 + half][...].astype(F32)
+            )
+
+    def finish(self):
+        for half in range(2):
+            self.first(half, 0).wait_send()
+            self.first(half, 1).wait_send()
+            self.second(half).wait_send()
+
+
 def forward_kernel(
     dims,
     mesh_dims,
@@ -265,12 +354,56 @@
     c_own,
     x_any,
     c_any,
-    weights_in,
     gain_own,
-    aux_ref,
-    conv_ref,
-    chan_ref,
-    hrow_ref,
+    seg_ref,
+    par_rows,
+    head_rows,
+    *refs,
+):
+    gathers = mesh_dims[2]
+    count = 5 if gathers else 1
+    forward_body(
+        dims,
+        mesh_dims,
+        x_own,
+        c_own,
+        x_any,
+        c_any,
+        gain_own,
+        seg_ref,
+        par_rows,
+        head_rows,
+        refs[:count],
+        *refs[count:],
+    )
+
+
+def stack_weights(mine, parts, gate_at, out_at):
+    inner_w, state_w, step_w, gate_w, out_w = parts
+    inner, share = inner_w.shape
+    nh = step_w.shape[0]
+    conv_rows = gate_at - STEP_ROWS
+    mine[0:inner] = inner_w[...].astype(BF16)
+    mine[inner:conv_rows] = state_w[...].T.astype(BF16)
+    mine[conv_rows:gate_at] = jnp.concatenate(
+        [step_w[...], jnp.zeros((STEP_ROWS - nh, share), F32)], axis=0
+    ).astype(BF16)
+    mine[gate_at:out_at] = gate_w[...].astype(BF16)
+    mine[out_at:] = out_w[...].astype(BF16)
+
+
+def forward_body(
+    dims,
+    mesh_dims,
+    x_own,
+    c_own,
+    x_any,
+    c_any,
+    gain_own,
+    seg_ref,
+    par_rows,
+    head_rows,
+    weight_parts,
     normed_own,
     normed_sib,
     pre_out,
@@ -280,13 +413,18 @@
     mixed_out,
     dng_out,
     state_out,
+    aux_out,
+    scale_out,
     stats_out,
     out_total,
     c_out,
     w_out,
     prev,
+    prev_seg,
     state,
     act_scr,
+    conv_scr,
+    head_scr,
     x_scr,
     c_scr,
     gain_sib,
@@ -335,17 +473,25 @@
         )
 
     if gathers:
-        weights = rest[14]
-        bounds = ((0, 336, gate_at), (gate_at, gate_at + 192, out_at), (out_at, out_at + 192, out_at + inner))
-        gather = Gather(weights_in, weights, [tuple(rest[15 + 2 * k : 17 + 2 * k]) for k in range(4)], bounds)
+        weights, mine = rest[14:16]
+        bounds = (
+            (0, 336, gate_at),
+            (gate_at, gate_at + inner // 2, out_at),
+            (out_at, out_at + inner // 2, out_at + inner),
+        )
+        sems = [tuple(rest[16 + 2 * k : 18 + 2 * k]) for k in range(4)]
+        gather = Gather(mine, weights, sems, bounds)
         others = [dict(dp=gather.near), dict(dp=gather.far)]
         keep_weights = pltpu.make_async_copy(weights, w_out, local_sems.at[blocks])
     else:
-        weights, gather, others = weights_in, None, []
+        weights, gather, others = weight_parts[0], None, []
 
     @pl.when(step_at == 0)
     def _():
         greet(peers + others)
+        if gathers:
+            stack_weights(mine, weight_parts, gate_at, out_at)
+        greeted(peers + others)
         if gathers:
             gather.start()
         gain_swap.start()
@@ -353,11 +499,13 @@
             swap(0, b).start()
             swap(1, b).start()
         prev[...] = jnp.zeros_like(prev)
+        prev_seg[...] = jnp.full_like(prev_seg, -1.0)
         state[...] = jnp.zeros_like(state)
+        load_columns(par_rows, head_rows, conv_scr, head_scr)
         if gathers:
-            share = weights_in.shape[1]
+            share = mine.shape[1]
             mine_at = pl.multiple_of(lax.axis_index("dp") * share, 128)
-            weights[:, pl.ds(mine_at, share)] = weights_in[...]
+            weights[:, pl.ds(mine_at, share)] = mine[...]
         gain_swap.wait_recv()
         if gathers:
             gather.take(0)
@@ -367,6 +515,7 @@
     xs = x_scr[step_at].astype(F32)
     squares = jnp.sum(xo * xo, axis=1, keepdims=True) + jnp.sum(xs * xs, axis=1, keepdims=True)
     scaling = lax.rsqrt(squares / width + EPSILON)
+    scale_out[...] = jnp.broadcast_to(scaling, (q, 128))
     no = (xo * scaling * gain_own[...]).astype(BF16)
     nsib = (xs * scaling * gain_sib[...]).astype(BF16)
     normed_own[...] = no
@@ -378,8 +527,28 @@
     step_pre = pre[conv_rows:gate_at]
     pre_out[...] = values
     step_out[...] = step_pre
-    aux = aux_ref[...]
-    conv = conv_ref[...]
+    seg = seg_ref[...].astype(F32)
+    seg_before = prev_seg[...]
+    seg_joined = jnp.concatenate([seg_before, seg], axis=1)
+    before, final = seg_before[:, 127:128], seg[:, q - 1 : q]
+    aux = jnp.concatenate(
+        [
+            (seg_joined[:, 128 - offset : 128 - offset + q] == seg).astype(F32)
+            for offset in range(1, 4)
+        ]
+        + [
+            seg,
+            (seg == before).astype(F32),
+            (seg == final).astype(F32),
+            jnp.broadcast_to((before == final).astype(F32), (1, q)),
+            jnp.zeros((1, q), F32),
+        ],
+        axis=0,
+    )
+    prev_seg[...] = seg[:, q - 128 :]
+    aux_out[...] = aux
+    conv = conv_scr[...]
+    head = head_scr[...]
     joined = jnp.concatenate([prev[...], values], axis=1)
     arg = conv[:, 4:5] + conv[:, 3:4] * values
     for offset in range(1, 4):
@@ -393,7 +562,7 @@
     in_low = act[inner : inner + ns].astype(BF16)
     out_low = act[inner + ns :].astype(BF16)
 
-    _, step, cumul, last, cols = block_rows(dims, step_pre, hrow_ref[...], aux)
+    _, step, cumul, last, cols = block_rows(dims, step_pre, head, aux)
     source = lax.broadcasted_iota(jnp.int32, (q, q), 0)
     target = lax.broadcasted_iota(jnp.int32, (q, q), 1)
     seg_col = cols[:, STEP_ROWS + 3 : STEP_ROWS + 4]
@@ -406,8 +575,7 @@
     tails = aux[5:6] * jnp.exp(last - cumul)
     keep = aux[6:7, 0:1] * jnp.exp(last)
     hq = q // 2
-    gain = chan_ref[...]
-    squares_row = jnp.zeros((1, q), F32)
+    gain = conv[0:inner, 5:6]
     tail_parts = []
     for h in range(nh):
         lo = h * pc
@@ -422,7 +590,7 @@
         y_low = dot_nn(u_h[:, hq:], low)
         y_h = jnp.concatenate([y_top[:, :hq], y_top[:, hq:] + y_low], axis=1)
         y_h = y_h + from_state[lo : lo + pc] * reach[h : h + 1]
-        mixed_out[lo : lo + pc] = y_h + gain[lo : lo + pc, 1:2] * x_h
+        mixed_out[lo : lo + pc] = y_h + head[h : h + 1, 2:3] * x_h
     chain.progress(step_at)
     contrib = dot_nt(jnp.concatenate(tail_parts, axis=0), in_low)
     for h in range(nh):
@@ -440,7 +608,7 @@
     gate_out[...] = gate
     gated = mixed_out[...] * (gate * sigmoid(gate))
     squares_row = jnp.sum(gated * gated, axis=0, keepdims=True)
-    weighted = gated * gain[:, 0:1]
+    weighted = gated * gain
     low = weighted.astype(BF16)
     if gathers:
 
@@ -466,7 +634,9 @@
     def _():
         for k in range(len(peers)):
             stat_copy(k).start()
-        chain.drain(blocks)
+        for extra in range(3):
+            chain.drain(blocks, extra)
+        chain.finish(blocks)
         for k in range(len(peers)):
             stat_copy(k).wait()
         total = stats_scr[0]
@@ -492,9 +662,9 @@
     c_sib,
     weights,
     aux_ref,
-    conv_ref,
-    chan_ref,
-    hrow_ref,
+    par_rows,
+    head_rows,
+    gain_own,
     pre_ref,
     arg_ref,
     gate_ref,
@@ -504,22 +674,34 @@
     state_ref,
     stats_ref,
     dn_total,
-    grad_w,
-    conv_grad,
-    chan_grad,
-    head_grad,
-    after,
-    d_state,
-    acc_w,
-    acc_conv,
-    acc_chan,
-    acc_head,
-    du_scr,
-    low_scr,
-    *rest,
+    dot_out,
+    vec_out,
+    *refs,
 ):
+    gathers = mesh_dims[2]
+    grad_outs, refs = (refs[:5], refs[5:]) if gathers else (refs[:1], refs[1:])
+    (
+        after,
+        d_state,
+        acc_w,
+        acc_conv,
+        acc_chan,
+        acc_head,
+        acc_norm,
+        acc_dot,
+        du_scr,
+        low_scr,
+        conv_scr,
+        head_scr,
+        stage,
+        group_vec,
+        dp_vec,
+        group_sems,
+        dp_sems,
+    ) = refs[:17]
+    rest = refs[17:]
     nh, pc, ns, width = dims
-    row_count, col_count, _ = mesh_dims
+    row_count, col_count = mesh_dims[:2]
     step_at = pl.program_id(0)
     blocks = stats_ref.shape[0] // 2
     inner = nh * pc
@@ -533,25 +715,33 @@
     own_at = pl.multiple_of(row_at * half, 128)
     sib_at = pl.multiple_of((1 - row_at) * half, 128)
 
-    chain = chain_of(rest, dn_total, q, lambda b: blocks - 1 - b)
+    chain = chain_of(rest[:14], dn_total, q, lambda b: blocks - 1 - b)
     block_at = blocks - 1 - step_at
+    col_at = chain.col_at
+    group = row_count * col_count
+    me = row_at * col_count + col_at
+    peers = group_peers(row_count, col_count)
+    dp_at = lax.axis_index("dp")
+    friends = [dict(dp=lax.rem(dp_at + k, 4)) for k in range(1, 4)] if gathers else []
 
     @pl.when(step_at == 0)
     def _():
-        greet(
-            [dict(row=1 - row_at), dict(col=lax.rem(chain.col_at + 1, col_count)), dict(col=lax.rem(chain.col_at + 3, col_count))]
-        )
+        greet(peers + friends)
+        load_columns(par_rows, head_rows, conv_scr, head_scr)
+        acc_norm[...] = jnp.zeros_like(acc_norm)
+        acc_dot[...] = jnp.zeros_like(acc_dot)
         after[...] = jnp.zeros_like(after)
         d_state[...] = jnp.zeros_like(d_state)
         acc_w[...] = jnp.zeros_like(acc_w)
         acc_conv[...] = jnp.zeros_like(acc_conv)
         acc_chan[...] = jnp.zeros_like(acc_chan)
         acc_head[...] = jnp.zeros_like(acc_head)
+        greeted(peers + friends)
 
     aux = aux_ref[...]
-    conv = conv_ref[...]
-    chan = chan_ref[...]
-    hrow = hrow_ref[...]
+    conv = conv_scr[...]
+    gain = conv[0:inner, 5:6]
+    hrow = head_scr[...]
     gate_scale = lax.rsqrt(stats_ref[pl.ds(block_at, 1)] / inner_width + EPSILON)
     gate_dot = stats_ref[pl.ds(blocks + block_at, 1)]
     pull = gate_scale * gate_scale * gate_scale * gate_dot / inner_width
@@ -561,9 +751,9 @@
     mixed = mixed_ref[...]
     gated = mixed * silu
     dng_scaled = dng_ref[...] * gate_scale
-    d_gated = chan[:, 0:1] * dng_scaled - gated * pull
+    d_gated = gain * dng_scaled - gated * pull
     acc_chan[0] += lane_fold(dng_scaled * gated)
-    normed_gate = (gated * (gate_scale * chan[:, 0:1])).astype(BF16)
+    normed_gate = (gated * (gate_scale * gain)).astype(BF16)
     acc_w[out_at:, pl.ds(own_at, half)] += dot_nn(normed_gate, c_own[...])
     acc_w[out_at:, pl.ds(sib_at, half)] += dot_nn(normed_gate, c_sib[...])
     grad_mixed = d_gated * silu
@@ -618,9 +808,9 @@
         du_local = jnp.concatenate([du_top + du_low[:, :hq], du_low[:, hq:]], axis=1)
         du_next = from_next[lo : lo + pc] * tails[h : h + 1]
         du = du_local + du_next
-        du_scr[lo : lo + pc] = du * step[h : h + 1] + chan[lo : lo + pc, 1:2] * g_h
+        du_scr[lo : lo + pc] = du * step[h : h + 1] + hrow[h : h + 1, 2:3] * g_h
         u_round = u_low.astype(F32)
-        y_h = mixed[lo : lo + pc] - chan[lo : lo + pc, 1:2] * x_h
+        y_h = mixed[lo : lo + pc] - hrow[h : h + 1, 2:3] * x_h
         row_sums.append(jnp.sum(g_low.astype(F32) * y_h, axis=0, keepdims=True))
         next_sum = jnp.sum(u_round * du_next, axis=0, keepdims=True)
         col_sums.append(jnp.sum(u_round * du_local, axis=0, keepdims=True) + next_sum)
@@ -676,27 +866,165 @@
         acc_conv[3 - offset] += lane_fold(shifted * values)
     low_scr[0:conv_rows] = d_pre.astype(BF16)
     low = low_scr[...]
-    chain.sib[step_at] = dot_tn(low, weights[0:out_at, pl.ds(sib_at, half)]).astype(BF16)
+    dn_sib = dot_tn(low, weights[0:out_at, pl.ds(sib_at, half)])
+    chain.sib[step_at] = dn_sib.astype(BF16)
     chain.exchange(step_at).start()
-    chain.own[step_at] = dot_tn(low, weights[0:out_at, pl.ds(own_at, half)]).astype(BF16)
+    dn_own = dot_tn(low, weights[0:out_at, pl.ds(own_at, half)])
+    chain.own[step_at] = dn_own.astype(BF16)
+    token_dot = jnp.zeros((q, 1), F32)
+    for which, (part, seen) in enumerate(((dn_own, normed_own), (dn_sib, normed_sib))):
+        product = part * seen[...].astype(F32)
+        token_dot = token_dot + jnp.sum(product, axis=1, keepdims=True)
+        acc_norm[which] += jnp.sum(product.reshape(q // 8, 8, half), axis=0)
+    lanes = lax.broadcasted_iota(jnp.int32, acc_dot.shape, 1)
+    acc_dot[...] = jnp.where(lanes == block_at, token_dot, acc_dot[...])
     acc_w[0:out_at, pl.ds(own_at, half)] += dot_nn(low, normed_own[...])
     acc_w[0:out_at, pl.ds(sib_at, half)] += dot_nn(low, normed_sib[...])
 
-    @pl.when(pl.program_id(0) == pl.num_programs(0) - 1)
+    @pl.when(step_at == blocks - 1)
     def _():
-        grad_w[...] = acc_w[...].astype(BF16)
-
-        def gather_columns(ref, count):
-            lanes = lax.broadcasted_iota(jnp.int32, ref.shape[1:], 1)
-            total = jnp.zeros(ref.shape[1:], F32)
-            for at in range(count):
-                total = jnp.where(lanes == at, jnp.sum(ref[at], axis=1, keepdims=True), total)
-            return total
-
-        conv_grad[...] = gather_columns(acc_conv, 5)
-        chan_grad[...] = gather_columns(acc_chan, 2)
-        head_grad[...] = gather_columns(acc_head, 2)
-        chain.drain(blocks)
+        conv_vec = rows_of(acc_conv)
+        chan_vec = rows_of(acc_chan)
+        head_vec = rows_of(acc_head)
+        norm_vec = [jnp.sum(acc_norm[which], axis=0, keepdims=True) for which in range(2)]
+        lane = 256
+        zeros = jnp.zeros((1, 128), F32)
+        skip = chan_vec[1:2]
+        group_vec[me] = jnp.concatenate(
+            [
+                conv_vec[0:5, inner:],
+                skip[:, 0:lane],
+                jnp.concatenate([skip[:, lane:], head_vec[0:1]], axis=1),
+                jnp.concatenate([head_vec[1:2], zeros], axis=1),
+                acc_dot[...].T[0:blocks],
+            ]
+            + [vec[:, at : at + lane] for vec in norm_vec for at in range(0, half, lane)]
+            + [jnp.zeros((2, lane), F32)],
+            axis=0,
+        )
+
+        def group_copy(k):
+            return send(
+                group_vec.at[me],
+                group_vec.at[me],
+                (group_sems.at[0], group_sems.at[1]),
+                k,
+                **peers[k],
+            )
+
+        for k in range(group - 1):
+            group_copy(k).start()
+        stage[...] = acc_w[...].astype(BF16)
+        if gathers:
+            reduce = Reduce(
+                acc_w,
+                stage,
+                rest[14].shape[1],
+                out_at + inner,
+                rest[14:18],
+                (tuple(rest[18:20]), tuple(rest[20:22])),
+            )
+            reduce.start()
+        chain.drain(blocks, 0)
+        for k in range(group - 1):
+            group_copy(k).wait()
+        shared = group_vec[0]
+        for k in range(1, group):
+            shared = shared + group_vec[k]
+        by_row, by_head = jnp.zeros((6, lane), F32), jnp.zeros((3, lane), F32)
+        for k in range(group):
+            same = (k // col_count) == row_at
+            one = group_vec[k]
+            picked = jnp.concatenate([one[16:22], one[5:8]], axis=0)
+            near = jnp.where(same, picked[0:3], picked[3:6])
+            by_row = by_row + jnp.concatenate([near, near], axis=0)
+            by_head = by_head + jnp.where((k % col_count) == col_at, picked[6:9], 0.0)
+        dot_out[...] = shared[8:16]
+        norm_sum = jnp.concatenate([by_row[at : at + 1] for at in range(half // lane)], axis=1)
+        norm_sum = norm_sum / gain_own[...]
+        skip_sum = jnp.concatenate([by_head[0:1], by_head[1:2, 0:128]], axis=1)
+        dp_vec[0] = jnp.concatenate(
+            [
+                jnp.concatenate([conv_vec[0:5, 0:inner], shared[0:5]], axis=1),
+                jnp.concatenate([chan_vec[0:1], by_head[1:2, 128:], by_head[2:3, 0:128]], axis=1),
+                jnp.concatenate([skip_sum, norm_sum[:, 0:lane]], axis=1),
+                jnp.concatenate([norm_sum[:, lane:], zeros], axis=1),
+            ],
+            axis=0,
+        )
+
+        def dp_copy(k):
+            return send(
+                dp_vec.at[0], dp_vec.at[k], (dp_sems.at[0], dp_sems.at[1]), k - 1, **friends[k - 1]
+            )
+
+        if gathers:
+            for k in range(1, 4):
+                dp_copy(k).start()
+        chain.drain(blocks, 1)
+        if gathers:
+            reduce.middle()
+        chain.drain(blocks, 2)
+        if gathers:
+            for k in range(1, 4):
+                dp_copy(k).wait()
+            ordered = [lax.rem(dp_at - k + 4, 4) for k in range(4)]
+            total = dp_vec[ordered[0]]
+            for k in range(1, 4):
+                total = total + dp_vec[ordered[k]]
+            vec_out[...] = total
+            reduce.end()
+            mine = reduce.cols(dp_at)
+            step_scr, state_send, state_recv, state_all, step_sems, state_sems = rest[22:28]
+            slice_rows = 2 * ns // group
+            for k in range(group):
+                lo = inner + k * slice_rows
+                state_send[k] = acc_w[lo : lo + slice_rows, mine].astype(BF16)
+            step_scr[0] = acc_w[conv_rows:gate_at, mine]
+
+            def state_copy(phase, k):
+                peer = peers[k]
+                sems = (state_sems.at[2 * phase], state_sems.at[2 * phase + 1])
+                to = peer["row"] * col_count + peer["col"]
+                if phase == 0:
+                    return send(state_send.at[to], state_recv.at[me], sems, k, **peer)
+                return send(state_all.at[me], state_all.at[me], sems, k, **peer)
+
+            step_copy = send(
+                step_scr.at[0],
+                step_scr.at[1],
+                (step_sems.at[0], step_sems.at[1]),
+                0,
+                row=1 - row_at,
+            )
+            for k in range(group - 1):
+                state_copy(0, k).start()
+            step_copy.start()
+            g_inner, g_state, g_step, g_gate, g_out = grad_outs
+            g_inner[...] = acc_w[0:inner, mine]
+            g_gate[...] = acc_w[gate_at:out_at, mine]
+            g_out[...] = acc_w[out_at:, mine]
+            state_recv[me] = state_send[me]
+            for k in range(group - 1):
+                state_copy(0, k).wait()
+            summed = state_recv[0].astype(F32)
+            for k in range(1, group):
+                summed = summed + state_recv[k].astype(F32)
+            state_all[me] = summed.astype(BF16)
+            for k in range(group - 1):
+                state_copy(1, k).start()
+            step_copy.wait()
+            g_step[...] = step_scr[0] + step_scr[1]
+            reduce.finish()
+            chain.finish(blocks)
+            for k in range(group - 1):
+                state_copy(1, k).wait()
+            whole_state = jnp.concatenate([state_all[k].astype(F32) for k in range(group)], axis=0)
+            g_state[...] = whole_state.T
+        else:
+            vec_out[...] = dp_vec[0]
+            grad_outs[0][...] = stage[...]
+            chain.finish(blocks)
 
 
 def per_device(
@@ -739,55 +1067,38 @@
     def channel_rows(w):
         return jnp.transpose(w, (1, 2, 0)).reshape(inner, share)
 
-    stacked = jnp.concatenate(
-        [
-            channel_rows(inner_proj),
-            state_proj.T,
-            jnp.pad(step_proj.T, ((0, STEP_ROWS - nh), (0, 0))),
-            channel_rows(gate_proj),
-            channel_rows(out_proj),
-        ],
-        axis=0,
-    ).astype(BF16)
     gathers = lax.axis_size("dp") == 4 and share % 128 == 0
+    parts = [
+        channel_rows(inner_proj),
+        state_proj,
+        step_proj.T,
+        channel_rows(gate_proj),
+        channel_rows(out_proj),
+    ]
     if not gathers:
-        stacked = lax.all_gather(stacked, "dp", axis=1, tiled=True)
+        parts[1] = state_proj.T
+        parts[2] = jnp.pad(step_proj.T, ((0, STEP_ROWS - nh), (0, 0)))
+        stacked = jnp.concatenate(parts, axis=0).astype(BF16)
+        parts = [lax.all_gather(stacked, "dp", axis=1, tiled=True)]
     gain_own = norm_gain[None, :]
     mesh_dims = (row_count, col_count, gathers)
     group = row_count * col_count
 
-    seg = segments[0]
-    seg_blocks = seg.reshape(blocks, q)
-    last_seg = seg_blocks[:, -1]
-    before_seg = jnp.concatenate([jnp.full((1,), -1, seg.dtype), last_seg[:-1]])
-    shift_masks = [
-        (jnp.pad(seg, (offset, 0), constant_values=-1)[:length] == seg).astype(F32)
-        for offset in range(1, 4)
-    ]
-    flags = [
-        seg.astype(F32),
-        (seg_blocks == before_seg[:, None]).astype(F32).reshape(length),
-        (seg_blocks == last_seg[:, None]).astype(F32).reshape(length),
-        jnp.repeat((last_seg == before_seg).astype(F32), q),
-        jnp.zeros((length,), F32),
-    ]
-    aux = jnp.stack(shift_masks + flags, axis=0)
-    conv_cols = jnp.concatenate(
-        [conv_inner.reshape(4, inner), conv_state], axis=1
-    )
-    bias_row = jnp.concatenate([bias_inner.reshape(inner), bias_state])[None]
-    conv_par = jnp.concatenate([conv_cols, bias_row, jnp.zeros((3, conv_rows), F32)], axis=0).T
-    chan_par = jnp.concatenate(
+    chan_rows = jnp.concatenate(
         [
-            gate_norm.reshape(1, inner),
-            jnp.repeat(skip_gain, pc)[None],
-            jnp.zeros((6, inner), F32),
+            conv_inner,
+            bias_inner[None],
+            gate_norm[None],
+            jnp.zeros((2, nh, pc), F32),
         ],
         axis=0,
-    ).T
-    decay_rate = -jnp.exp(decay_log)
-    head_par = jnp.pad(
-        jnp.stack([step_bias, decay_rate], axis=1), ((0, STEP_ROWS - nh), (0, 6))
+    ).reshape(8, inner)
+    state_rows = jnp.concatenate(
+        [conv_state, bias_state[None], jnp.zeros((3, state_width), F32)], axis=0
+    )
+    par_rows = jnp.concatenate([chan_rows, state_rows], axis=1)
+    head_rows = jnp.pad(
+        jnp.stack([step_bias, decay_log, skip_gain]), ((0, 5), (0, 128 - nh))
     )
 
     def token_block(order):
@@ -815,13 +1126,12 @@
             token_block(up),
             pl.BlockSpec(memory_space=pl.ANY),
             pl.BlockSpec(memory_space=pl.ANY),
-            whole(*stacked.shape),
             whole(1, half),
-            lane_block(8, up),
-            whole(conv_rows, 8),
-            whole(inner, 8),
-            whole(STEP_ROWS, 8),
-        ],
+            lane_block(1, up),
+            whole(8, conv_rows),
+            whole(8, 128),
+        ]
+        + [whole(*part.shape) for part in parts],
         out_specs=[
             token_block(up),
             token_block(up),
@@ -832,6 +1142,8 @@
             lane_block(inner, up),
             lane_block(inner, up),
             pl.BlockSpec((1, inner, ns), lambda i: (i, 0, 0)),
+            lane_block(8, up),
+            pl.BlockSpec((q, 128), lambda i: (i, 0)),
             whole(2 * blocks, q),
             pl.BlockSpec(memory_space=pl.ANY),
             pl.BlockSpec(memory_space=pl.ANY),
@@ -847,6 +1159,8 @@
             sds((inner, length), F32),
             sds((inner, length), F32),
             sds((blocks, inner, ns), F32),
+            sds((8, length), F32),
+            sds((length, 128), F32),
             sds((2 * blocks, q), F32),
             sds((length, half), BF16),
             sds((length, half), BF16),
@@ -854,8 +1168,11 @@
         ],
         scratch_shapes=[
             pltpu.VMEM((conv_rows, 128), F32),
+            pltpu.VMEM((1, 128), F32),
             pltpu.VMEM((inner, ns), F32),
             pltpu.VMEM((inner, q), F32),
+            pltpu.VMEM((conv_rows, 128), F32),
+            pltpu.VMEM((STEP_ROWS, 128), F32),
             pltpu.VMEM((blocks, q, half), BF16),
             pltpu.VMEM((blocks, q, half), BF16),
             pltpu.VMEM((1, half), F32),
@@ -866,7 +1183,8 @@
         ]
         + chain_scratch(blocks, q, half)
         + (
-            [pltpu.VMEM((rows, width), BF16)] + [pltpu.SemaphoreType.DMA((3,)) for _ in range(8)]
+            [pltpu.VMEM((rows, width), BF16), pltpu.VMEM((rows, share), BF16)]
+            + [pltpu.SemaphoreType.DMA((3,)) for _ in range(8)]
             if gathers
             else []
         ),
@@ -889,6 +1207,8 @@
         mixed_vals,
         dng_vals,
         states,
+        aux,
+        scaling,
         stats,
         out_sum,
         c_sib,
@@ -898,19 +1218,48 @@
         cotangent,
         inputs,
         cotangent,
-        stacked,
         gain_own,
-        aux,
-        conv_par,
-        chan_par,
-        head_par,
+        segments,
+        par_rows,
+        head_rows,
+        *parts,
     )
     if not gathers:
-        weights = stacked
+        weights = parts[0]
     gate_scale = lax.rsqrt(stats[:blocks].reshape(length) / (H * P_SIZE) + EPSILON)
     plain = inputs.astype(F32)
     output = (plain + gate_scale[:, None] * out_sum.astype(F32)).astype(BF16)
 
+    dma = pltpu.SemaphoreType.DMA
+    split = 704
+    if gathers:
+        grad_shapes = [
+            sds((inner, share), F32),
+            sds((share, state_width), F32),
+            sds((STEP_ROWS, share), F32),
+            sds((inner, share), F32),
+            sds((inner, share), F32),
+        ]
+        slice_rows = state_width // group
+        reduce_scratch = [
+            pltpu.VMEM((2, split, share), BF16),
+            pltpu.VMEM((2, rows - split, share), BF16),
+            pltpu.VMEM((split, share), BF16),
+            pltpu.VMEM((rows - split, share), BF16),
+            dma((3,)),
+            dma((3,)),
+            dma((3,)),
+            dma((3,)),
+            pltpu.VMEM((2, STEP_ROWS, share), F32),
+            pltpu.VMEM((group, slice_rows, share), BF16),
+            pltpu.VMEM((group, slice_rows, share), BF16),
+            pltpu.VMEM((group, slice_rows, share), BF16),
+            dma((2, 1)),
+            dma((4, group - 1)),
+        ]
+    else:
+        grad_shapes = [sds((rows, width), BF16)]
+        reduce_scratch = []
     backward = pl.pallas_call(
         functools.partial(backward_kernel, dims, mesh_dims),
         name="backward",
@@ -922,9 +1271,9 @@
             token_block(down),
             whole(rows, width),
             lane_block(8, down),
-            whole(conv_rows, 8),
-            whole(inner, 8),
-            whole(STEP_ROWS, 8),
+            whole(8, conv_rows),
+            whole(8, 128),
+            whole(1, half),
             lane_block(conv_rows, down),
             lane_block(conv_rows, down),
             lane_block(inner, down),
@@ -936,18 +1285,16 @@
         ],
         out_specs=[
             pl.BlockSpec(memory_space=pl.ANY),
-            whole(rows, width),
-            whole(conv_rows, 128),
-            whole(inner, 128),
-            whole(STEP_ROWS, 128),
-        ],
+            whole(blocks, q),
+            whole(8, conv_rows),
+        ]
+        + [whole(*shape.shape) for shape in grad_shapes],
         out_shape=[
             sds((length, half), BF16),
-            sds((rows, width), BF16),
-            sds((conv_rows, 128), F32),
-            sds((inner, 128), F32),
-            sds((STEP_ROWS, 128), F32),
-        ],
+            sds((blocks, q), F32),
+            sds((8, conv_rows), F32),
+        ]
+        + grad_shapes,
         scratch_shapes=[
             pltpu.VMEM((3, conv_rows, 128), F32),
             pltpu.VMEM((inner, ns), F32),
@@ -955,10 +1302,20 @@
             pltpu.VMEM((5, conv_rows, 128), F32),
             pltpu.VMEM((2, inner, 128), F32),
             pltpu.VMEM((2, STEP_ROWS, 128), F32),
+            pltpu.VMEM((2, 8, half), F32),
+            pltpu.VMEM((q, 128), F32),
             pltpu.VMEM((inner, q), F32),
             pltpu.VMEM((out_at, q), BF16),
+            pltpu.VMEM((conv_rows, 128), F32),
+            pltpu.VMEM((STEP_ROWS, 128), F32),
+            pltpu.VMEM((rows, width), BF16),
+            pltpu.VMEM((group, 24, 256), F32),
+            pltpu.VMEM((4, 8, conv_rows), F32),
+            dma((2, group - 1)),
+            dma((2, 3)),
         ]
-        + chain_scratch(blocks, q, half),
+        + chain_scratch(blocks, q, half)
+        + reduce_scratch,
         compiler_params=pltpu.CompilerParams(
             vmem_limit_bytes=60 << 20, collective_id=2, has_side_effects=True
         ),
@@ -968,16 +1325,16 @@
             transcendentals=nh * length * q,
         ),
     )
-    dn_total, grad_w, conv_grad, chan_grad, head_grad = backward(
+    dn_total, token_dots, vectors, *grad_parts = backward(
         normed_own,
         normed_sib,
         cotangent,
         c_sib,
         weights,
         aux,
-        conv_par,
-        chan_par,
-        head_par,
+        par_rows,
+        head_rows,
+        gain_own,
         pre_vals,
         arg_vals,
         gate_vals,
@@ -988,63 +1345,45 @@
         stats,
     )
 
-    d_half = dn_total.astype(F32)
-    weighted = d_half * gain_own
-    sums = jnp.stack([jnp.sum(weighted * plain, axis=1), jnp.sum(plain * plain, axis=1)])
-    sums = sums + lax.ppermute(sums, "row", swap)
-    input_dot = sums[0]
-    scaling = lax.rsqrt(sums[1] / width + EPSILON)
+    scale = scaling[:, 0:1]
+    pull = token_dots.reshape(length)[:, None] * scale * scale / width
     grad_inputs = (
-        cotangent.astype(F32)
-        + scaling[:, None] * weighted
-        - plain * (scaling**3 * input_dot / width)[:, None]
-    )
-    grad_norm = jnp.sum(d_half * plain * scaling[:, None], axis=0)
-
-    grads = lax.psum_scatter(grad_w, "dp", scatter_dimension=1, tiled=True).astype(F32)
-    head_wide = head_grad[:nh, :2].T
-    skip_part = jnp.sum(chan_grad[:, 1].reshape(nh, pc), axis=1)[None]
-    heads = jnp.concatenate([head_wide, skip_part], axis=0)
-
-    def widen(part):
-        wide = jnp.zeros((col_count,) + part.shape, F32)
-        return lax.dynamic_update_slice_in_dim(wide, part[None], col_at, 0)
-
-    step_wide = widen(grads[conv_rows : conv_rows + nh])
-    head_all = widen(heads)
-    grad_norm, conv_sum, gate_gain_sum, head_all = lax.psum(
-        (grad_norm, conv_grad[:, :5].T, chan_grad[:, 0], head_all), "dp"
-    )
-    state_sum, step_wide, conv_state_sum, head_all = lax.psum(
-        (grads[inner:conv_rows], step_wide, conv_sum[:, inner:], head_all), ("row", "col")
-    )
-
-    def take(wide):
-        return lax.dynamic_slice_in_dim(wide, col_at, 1, 0)[0]
-
-    step_grad = take(step_wide)
-    head_own = take(head_all)
+        cotangent.astype(F32) + scale * (dn_total.astype(F32) * gain_own) - plain * pull
+    )
+    if gathers:
+        g_inner, g_state, g_step, g_gate, g_out = grad_parts
+    else:
+        grads = lax.psum_scatter(grad_parts[0], "dp", scatter_dimension=1, tiled=True)
+        grads = grads.astype(F32)
+        vectors = lax.psum(vectors, "dp")
+        g_inner = grads[0:inner]
+        g_state = lax.psum(grads[inner:conv_rows], ("row", "col")).T
+        g_step = lax.psum(grads[conv_rows:gate_at], "row")
+        g_gate = grads[gate_at:out_at]
+        g_out = grads[out_at:]
 
     def feature_rows(w):
         return jnp.transpose(w.reshape(nh, pc, share), (2, 0, 1))
 
+    channel_vecs = vectors[:, 0:inner].reshape(8, nh, pc)
+    grad_norm = jnp.concatenate([vectors[6, inner:], vectors[7, : half - 2 * ns]])
     return (
         output,
         grad_inputs,
         grad_norm,
-        feature_rows(grads[gate_at:out_at]),
-        feature_rows(grads[0:inner]),
-        state_sum.T,
-        step_grad.T,
-        conv_sum[:4, :inner].reshape(4, nh, pc),
-        conv_sum[4, :inner].reshape(nh, pc),
-        conv_state_sum[:4],
-        conv_state_sum[4],
-        head_own[0],
-        head_own[1] * decay_rate,
-        head_own[2],
-        gate_gain_sum.reshape(nh, pc),
-        feature_rows(grads[out_at:]),
+        feature_rows(g_gate),
+        feature_rows(g_inner),
+        g_state,
+        g_step[:nh].T,
+        channel_vecs[0:4],
+        channel_vecs[4],
+        vectors[0:4, inner:],
+        vectors[4, inner:],
+        vectors[5, inner : inner + nh],
+        -vectors[5, inner + 128 : inner + 128 + nh] * jnp.exp(decay_log),
+        jnp.sum(channel_vecs[6], axis=1),
+        channel_vecs[5],
+        feature_rows(g_out),
     )
 
 

time: 436 us -> 305 us (0.70)
  blocking collectives: 60.9 us -> 0 us
  waiting for transfers between devices: 52.6 us -> 0 us
  Pallas kernels: 255 us -> 277 us
  local copies, waits for them, and re-layouts: 31.1 us -> 13.9 us
  between operations: 14.4 us -> 0.82 us
  other arithmetic: 20.2 us -> 13.2 us
    psum x2 -> x0, blocking collectives: 60.9 us -> none  [the longest x1 31 us: per_device(): lax.psum((grads[inner:conv_rows], step_wide, conv_sum[:, inner:], head_al...]
    psum x1 -> x0, waiting for transfers between devices: 52.6 us -> none  [per_device(): lax.psum((grads[inner:conv_rows], step_wide, conv_sum[:, inner:], head_al...]
    pallas_call x2, Pallas kernels: 255 us -> 277 us  [the longest x1 149 us: per_device(): forward(inputs, cotangent, inputs, cotangent, gain_own, segments, par_row...]
    unnamed x43 -> x29, local copies, waits for them, and re-layouts: 17.4 us -> 5.68 us
    reduce_sum x3 -> x1, other arithmetic: 11.5 us -> 0.63 us  [per_device(): jnp.sum(channel_vecs[6], axis=1)]
    sub x0 -> x1, other arithmetic: none -> 8.19 us  [per_device(): cotangent.astype(F32) + scale * (dn_total.astype(F32) * gain_own)]
  transfers between devices with their start and end apart: 3 -> 0, of which waited for: 1 -> 0; matrix products, arithmetic and copies ran while one was open for 4% -> 0% of each run, Pallas kernels for 0% -> 0%
where the time goes in v3:
time: 305 us; the launch traced here: 304 us
  Pallas kernels  277 us (91%)
  local copies, waits for them, and re-layouts  13.9 us (5%)
  other arithmetic  13.2 us (4%)
    pallas_call x1, Pallas kernels, per_device(): forward(inputs, cotangent, inputs, cotangent, gain_own, segments, par_row...  149 us
    pallas_call x1, Pallas kernels, per_device(): backward(normed_own, normed_sib, cotangent, c_sib, weights, aux, par_rows...  128 us
    sub x1, other arithmetic, per_device(): cotangent.astype(F32) + scale * (dn_total.astype(F32) * gain_own)  8.19 us

profile of v3, /device:TPU:0, one launch (start us, length us, event | category | flops | bytes accessed | tf_op | source)
XLA Modules:
  0.0 304.5 jit_solution(7204319558953056548)
XLA Ops:
  0.6 0.7 copy.39
  1.4 0.1 concatenate.19
  1.5 0.8 concatenate.20
  2.2 0.8 concatenate.21
  3.0 1.3 maximum_maximum_fusion.par_rows
  4.3 1.3 select_maximum_fusion.head_rows
  5.6 1.3 broadcast_in_dim.15.gain_own
  6.9 149.0 %forward.1 = (bf16[2048,768]{1,0:T(8,128)(2,1)}, bf16[2048,768]{1,0:T(8,128)(2,1)}, f32[640,2048]{1,0:T(8,128)}, f32[640,2048]{1,0:T(8,128)}, f32[384,2048]{1,0:...) custom-call(bf16[2048,768]{1,0:T(8,128)(2,1)} %x_any.1, ...), custom_call_target="tpu_custom_call" | custom-call | flops 11374952448 | bytes 52428800 | tf_op jit(solution)/shard_map/forward/pallas_call | solution.py:1216
  155.9 0.0 copy-start
  155.9 0.0 copy-start.8
  155.9 0.0 copy-start.7
  155.9 127.6 %backward.1 = (bf16[2048,768]{1,0:T(8,128)(2,1)}, f32[8,256]{1,0:T(8,128)}, f32[8,640]{1,0:T(8,128)}, f32[384,384]{1,0:T(8,128)}, f32[384,256]{1,0:T(8,128)}, /*...) custom-call(bf16[2048,768]{1,0:T(8,128)(2,1)} %get-tuple-element.42.normed_own, ...), custom_call_target="tpu_custom_call" | custom-call | flops 17918066688 | bytes 62914560 | tf_op jit(solution)/shard_map/backward/pallas_call | solution.py:1328
  283.6 1.3 fusion.4
  284.9 0.7 slice.53
  285.6 0.6 pad_maximum_fusion
  286.2 0.7 copy.43
  286.9 0.4 copy.44
  287.3 0.0 copy-done
  287.3 0.6 slice_reduce_fusion
  287.9 0.0 copy-done.8
  288.0 0.0 copy-done.7
  288.0 0.0 copy-start.6
  288.0 0.0 copy-start.5
  288.0 0.0 copy-start.9
  288.0 0.0 copy-start.3
  288.0 0.0 copy-start.2
  288.0 0.0 copy-start.4
  288.0 0.0 copy-start.1
  288.0 8.2 %fusion.1 = (f32[2048,768]{1,0:T(8,128)}, bf16[2048,768]{1,0:T(8,128)(2,1)}) fusion(bf16[2048,768]{1,0:T(8,128)(2,1)} %x_any.1, bf16[2048,768]{1,0:T(8,128)(2,1)} %get-tuple-element.54, bf16[2048,768]{1,0:T(8,128)(2,1)} %c_own.3, f32[2048]{0:T(1024)S(1)} %get-tuple-element.111, f32[768]{0:T(1024)S(1)} %copy-done.7, f32[2048]{0:T(1024)S(1)} %get-tuple-element.110, ...), kind=kLoop, calls=%fused_computation.3 | loop fusion | flops 18874368 | bytes 22047744 | tf_op jit(solution)/shard_map/sub | solution.py:1351
  296.2 0.0 copy-done.6
  296.2 0.1 slice.56
  296.3 0.6 copy.41
  296.9 0.0 copy-done.5
  296.9 0.6 slice_bitcast_fusion
  297.6 0.1 squeeze.27
  297.7 0.6 reduce_sum.9
  298.3 0.7 squeeze.24
  299.0 0.7 squeeze.28
  299.6 0.6 slice.58
  300.2 0.0 copy-done.9
  300.2 0.5 bitcast_multiply_fusion
  300.8 0.5 slice_bitcast_fusion.1
  301.3 0.0 copy-done.3
  301.3 0.8 copy.49
  302.1 0.0 copy-done.2
  302.1 0.8 copy.50
  302.9 0.0 copy-done.4
  302.9 0.7 copy.51
  303.7 0.0 copy-done.1
  303.7 0.8 copy.52
  (6 shorter events, 0.0 us)
Async XLA Ops:
  155.9 131.4 %copy-start = (f32[2048,128]{1,0:T(8,128)S(1)}, f32[2048,128]{1,0:T(8,128)}, u32[]{:S(2)}) copy-start(f32[2048,128]{1,0:T(8,128)} %get-tuple-element.41) | copy-start | bytes 3145732
  155.9 132.0 %copy-start.8 = (f32[16,256]{1,0:T(8,128)S(1)}, f32[16,256]{1,0:T(8,128)}, u32[]{:S(2)}) copy-start(f32[16,256]{1,0:T(8,128)} %get-tuple-element.39.stats_ref) | copy-start | bytes 49156
  155.9 132.1 %copy-start.7 = (f32[768]{0:T(1024)S(1)}, f32[768]{0:T(1024)}, u32[]{:S(2)}) copy-start(f32[768]{0:T(1024)} %param.20) | copy-start | bytes 9220
  288.0 8.3 %copy-start.6 = (f32[8,640]{1,0:T(8,128)S(1)}, f32[8,640]{1,0:T(8,128)}, u32[]{:S(2)}) copy-start(f32[8,640]{1,0:T(8,128)} %get-tuple-element.56) | copy-start | bytes 61444
  288.0 9.0 %copy-start.5 = (f32[16,384]{1,0:T(8,128)S(1)}, f32[16,384]{1,0:T(8,128)}, u32[]{:S(2)}) copy-start(f32[16,384]{1,0:T(8,128)} %get-tuple-element.60) | copy-start | bytes 73732
  288.0 12.3 %copy-start.9 = (f32[12]{0:T(128)S(1)}, f32[12]{0:T(128)}, u32[]{:S(2)}) copy-start(f32[12]{0:T(128)} %param.30) | copy-start | bytes 148
  288.0 13.3 %copy-start.3 = (f32[384,384]{1,0:T(8,128)S(1)}, f32[384,384]{1,0:T(8,128)}, u32[]{:S(2)}) copy-start(f32[384,384]{1,0:T(8,128)} %get-tuple-element.57) | copy-start | bytes 1769476
  288.0 14.1 %copy-start.2 = (f32[384,384]{1,0:T(8,128)S(1)}, f32[384,384]{1,0:T(8,128)}, u32[]{:S(2)}) copy-start(f32[384,384]{1,0:T(8,128)} %get-tuple-element.58) | copy-start | bytes 1769476
  288.0 14.9 %copy-start.4 = (f32[384,256]{1,0:T(8,128)S(1)}, f32[384,256]{1,0:T(8,128)}, u32[]{:S(2)}) copy-start(f32[384,256]{1,0:T(8,128)} %get-tuple-element.140) | copy-start | bytes 1179652
  288.0 15.6 %copy-start.1 = (f32[384,384]{1,0:T(8,128)S(1)}, f32[384,384]{1,0:T(8,128)}, u32[]{:S(2)}) copy-start(f32[384,384]{1,0:T(8,128)} %get-tuple-element.61) | copy-start | bytes 1769476

commit v4 on v0

v4 whole, which is shorter than its diff:
```python
import functools
import types

import jax
import jax.numpy as jnp
from jax import lax
from jax.experimental import pallas as pl
from jax.experimental.pallas import tpu as pltpu
from jax.sharding import PartitionSpec as P

H = 48
P_SIZE = 64
BLOCK_LEN = 256
EPSILON = 1e-05
NEG = -1e30
STEP_ROWS = 16
UNITS = 2
UP_AT = (0.45, None, None, None, None, None, None, 0.8)
DOWN_AT = (None, None, None, 0.22, 0.35, 0.5, 0.65, 0.78)
TURN_AT = (0.3, 0.6, 0.9)
AHEAD = 5
MODEL = (2.4, 3.7, 10.0, 8.2, 8.0, 0.5)
FORWARD_AT = (2, 4)
STOPS = (1, 1, 2, 3, 4, 7, 7, 8, 10)
DEPTH = 2
VMEM_LIMIT = 63 << 20
F32 = jnp.float32
BF16 = jnp.bfloat16
HIGHEST = lax.Precision.HIGHEST


def dot_nn(left, right, precision=None):
    return lax.dot_general(
        left, right, (((1,), (0,)), ((), ())), preferred_element_type=F32, precision=precision
    )


def dot_nt(left, right, precision=None):
    return lax.dot_general(
        left, right, (((1,), (1,)), ((), ())), preferred_element_type=F32, precision=precision
    )


def dot_tn(left, right):
    return lax.dot_general(left, right, (((0,), (0,)), ((), ())), preferred_element_type=F32)


def sigmoid(values):
    return 0.5 * jnp.tanh(0.5 * values) + 0.5


def softplus(values):
    return jnp.maximum(values, 0.0) + jnp.log1p(jnp.exp(-jnp.abs(values)))


def lane_fold(values):
    total = values[:, :128]
    for at in range(128, values.shape[1], 128):
        total = total + values[:, at : at + 128]
    return total


def columns_of(rows):
    padded = jnp.concatenate([rows, jnp.zeros((128 - rows.shape[0], rows.shape[1]), F32)], axis=0)
    return padded.T


def rows_of(ref):
    lanes = lax.broadcasted_iota(jnp.int32, ref.shape[1:], 1)
    total = jnp.zeros(ref.shape[1:], F32)
    for at in range(ref.shape[0]):
        total = jnp.where(lanes == at, jnp.sum(ref[at], axis=1, keepdims=True), total)
    if total.shape[0] % 128:
        total = jnp.concatenate([total, jnp.zeros((128 - total.shape[0], 128), F32)], axis=0)
    return total.T[0:8]


def load_columns(par_rows, head_rows, conv_scr, head_scr):
    conv_scr[...] = columns_of(par_rows[...])
    heads = columns_of(head_rows[...])[0:STEP_ROWS]
    lanes = lax.broadcasted_iota(jnp.int32, heads.shape, 1)
    head_scr[...] = jnp.where(lanes == 1, -jnp.exp(heads), heads)


def block_rows(dims, step_pre, hrow, aux):
    q = step_pre.shape[1]
    step_arg = step_pre + hrow[:, 0:1]
    step = softplus(step_arg)
    log_decay = step * hrow[:, 1:2]
    source = lax.broadcasted_iota(jnp.int32, (q, q), 0)
    target = lax.broadcasted_iota(jnp.int32, (q, q), 1)
    upper = (source <= target).astype(F32)
    cumul = dot_nn(log_decay, upper, HIGHEST)
    last = cumul[:, q - 1 : q]
    cols = columns_of(jnp.concatenate([cumul, aux], axis=0))
    return step_arg, step, cumul, last, cols


MESH = pl.DeviceIdType.MESH


def send(src, dst, sems, at, **device):
    return pltpu.make_async_remote_copy(
        src_ref=src,
        dst_ref=dst,
        send_sem=sems[0].at[at],
        recv_sem=sems[1].at[at],
        device_id=device,
        device_id_type=MESH,
    )


def group_peers(row_count, col_count):
    row_at, col_at = lax.axis_index("row"), lax.axis_index("col")
    return [
        dict(row=lax.rem(row_at + j, row_count), col=lax.rem(col_at + k, col_count))
        for k in range(col_count)
        for j in range(row_count)
        if (j, k) != (0, 0)
    ]


def greet(peers):
    barrier = pltpu.get_barrier_semaphore()
    for peer in peers:
        pl.semaphore_signal(barrier, inc=1, device_id=peer, device_id_type=MESH)


def greeted(peers):
    pl.semaphore_wait(pltpu.get_barrier_semaphore(), len(peers))


def add_low(left, right):
    return left + right


class Chain:
    def __init__(self, r, total, turn, first_rows, second_rows):
        self.total, self.turn = total, turn
        self.own, self.sib = r.ch_own, r.ch_sib
        self.first, self.pair, self.cross = r.ch_first, r.ch_pair, r.ch_cross
        self.slots = self.first.shape[0]
        self.out_slots = self.own.shape[0]
        self.sems = [(r.cs_send.at[k], r.cs_recv.at[k]) for k in range(4)]
        self.keep_sems = r.cs_keep
        self.free = r.ch_free
        self.first_rows, self.second_rows = first_rows, second_rows
        self.row_at, self.col_at = lax.axis_index("row"), lax.axis_index("col")
        self.is_outer = (self.col_at == 0) | (self.col_at == 3)
        self.inward = 1 + lax.div(self.col_at, 2)
        self.outward = 3 * lax.div(self.col_at, 2)

    def slot(self, m):
        return lax.rem(m, self.slots)

    def out_slot(self, m):
        return lax.rem(m, self.out_slots)

    def exchange(self, m):
        return send(
            self.sib.at[self.out_slot(m)],
            self.first.at[self.slot(m)],
            self.sems[0],
            self.slot(m),
            row=1 - self.row_at,
        )

    def to_inner(self, m):
        at = self.slot(m)
        return send(self.first.at[at], self.pair.at[at], self.sems[1], at, col=self.inward)

    def across(self, m):
        at = self.slot(m)
        return send(self.pair.at[at], self.cross.at[at], self.sems[2], at, col=3 - self.col_at)

    def to_outer(self, m, rows):
        at = self.slot(m)
        return send(self.cross.at[at], rows, self.sems[3], at, col=self.outward)

    def keep(self, m, rows):
        at = self.slot(m)
        return pltpu.make_async_copy(self.cross.at[at], rows, self.keep_sems.at[at])

    def credit(self, which, m, **device):
        @pl.when(m < self.total - self.slots)
        def _():
            pl.semaphore_signal(
                self.free.at[which], inc=1, device_id=device, device_id_type=MESH
            )

    def spend(self, which, m):
        @pl.when(m >= self.slots)
        def _():
            pl.semaphore_wait(self.free.at[which], 1)

    def begin(self, m, sib_part):
        @pl.when(m >= self.out_slots)
        def _():
            self.exchange(m - self.out_slots).wait_send()

        self.sib[self.out_slot(m)] = sib_part
        self.spend(0, m)
        self.exchange(m).start()

    def put_own(self, m, own_part):
        self.own[self.out_slot(m)] = own_part

    def stage_first(self, m):
        at = self.slot(m)
        self.exchange(m).wait_recv()
        self.first[at] = add_low(self.own[self.out_slot(m)], self.first[at])

        @pl.when(self.is_outer & (m < DEPTH))
        def _():
            self.to_inner(m).start()

    def stage_pair(self, m):
        at = self.slot(m)

        @pl.when(self.is_outer)
        def _():
            self.to_inner(m).wait_send()

            @pl.when(m + DEPTH < self.total)
            def _():
                self.spend(1, m + DEPTH)
                self.to_inner(m + DEPTH).start()

        @pl.when(~self.is_outer)
        def _():
            self.to_inner(m).wait_recv()
            self.pair[at] = add_low(self.first[at], self.pair[at])
            self.spend(2, m)
            self.across(m).start()

        self.credit(0, m, row=1 - self.row_at)

    def stage_cross(self, m):
        at = self.slot(m)

        @pl.when(~self.is_outer)
        def _():
            self.across(m).wait()
            self.cross[at] = add_low(self.pair[at], self.cross[at])
            self.credit(1, m, col=self.outward)

            @pl.when(m < self.turn)
            def _():
                self.keep(m, self.first_rows(m)).start()
                self.to_outer(m, self.first_rows(m)).start()

            @pl.when(m >= self.turn)
            def _():
                self.keep(m, self.second_rows(m)).start()
                self.to_outer(m, self.second_rows(m)).start()

    def stage_done(self, m):
        rows = self.first_rows(0)

        @pl.when(self.is_outer)
        def _():
            self.to_outer(m, rows).wait_recv()

        @pl.when(~self.is_outer)
        def _():
            self.keep(m, rows).wait()
            self.to_outer(m, rows).wait_send()
            self.credit(2, m, col=3 - self.col_at)


class Plan:
    def __init__(self, blocks, units, slots, up_us, scan_us, gap, down_us, hop, lag):
        steps = 2 * blocks
        self.total = steps * units
        self.per_step = len(UP_AT)
        self.points = steps * self.per_step
        hop = hop / units
        mixed = blocks - AHEAD
        lengths = [up_us + scan_us] * mixed + [up_us] * AHEAD + [down_us] * blocks
        starts = [0.0]
        for step in range(1, steps):
            pause = gap if step == blocks else 0.0
            starts.append(starts[-1] + lengths[step - 1] + pause)
        times = []
        for step in range(steps):
            if step < blocks:
                times += [None if at is None else starts[step] + at * up_us for at in UP_AT]
            else:
                times += [
                    None if at is None else starts[step] + at * down_us for at in DOWN_AT
                ]
        for which, at in enumerate(TURN_AT):
            times[self.per_step * blocks + which] = starts[blocks] - gap * (1.0 - at)
        ends = [at + up_us for at in starts[:blocks]]
        ends += [at + down_us for at in starts[blocks:]]

        def point_after(when):
            fits = [p for p, at in enumerate(times) if at is not None and at >= when]
            return fits[0] if fits else self.points

        def exact(point, when):
            known = point < len(times) and times[point] is not None
            return times[point] if known else when

        self.pair, self.cross, self.done = [], [], []
        one = two = three = 0.0
        for m in range(self.total):
            ready = ends[m // units] + 2.0
            if m >= DEPTH:
                ready = max(ready, taken[m - DEPTH])
            else:
                taken = taken if m else []
            one = max(one, ready) + hop
            point = point_after(one + lag)
            if m + DEPTH < self.total:
                point = max(point, self.per_step * ((m + DEPTH) // units + 1))
            if m + slots < self.total:
                point = min(point, self.per_step * ((m + slots) // units + 1) - 1)
            point = min(point, self.points)
            self.pair.append(point)
            taken_at = exact(point, one + lag)
            taken.append(taken_at)
            two = max(two, taken_at) + hop
            point = max(point_after(two + lag), point)
            self.cross.append(point)
            three = max(three, exact(point, two + lag)) + hop
            self.done.append(point_after(three + lag))
        for m in range(self.total - slots):
            self.done[m] = max(min(self.done[m], self.pair[m + slots]), self.cross[m])
        self.end = three + lag

    def span(self, table, which, step, steps):
        first = count = 0
        for point in sorted(set(table)):
            on = point // self.per_step
            if on in steps and point % self.per_step == which:
                hit = (step == on).astype(jnp.int32)
                first = first + table.index(point) * hit
                count = count + table.count(point) * hit
        return first, first + count

    def left(self, table):
        return sum(1 for at in table if at < self.points)


class Gather:
    def __init__(self, whole, sems, groups):
        self.whole, self.groups = whole, groups
        self.sems = sems
        at = lax.axis_index("dp")
        self.at = at
        self.near = at + 1 - 2 * lax.rem(at, 2)
        self.far = lax.rem(at + 2, 4)
        self.share = whole.shape[1] // 4

    def part(self, shard, lo, hi):
        return self.whole.at[
            lo:hi, pl.ds(pl.multiple_of(shard * self.share, 128), self.share)
        ]

    def direct(self, g, to_near):
        lo, _, hi = self.groups[g]
        return send(
            self.part(self.at, lo, hi),
            self.part(self.at, lo, hi),
            self.sems[0 if to_near else 1],
            g,
            dp=self.near if to_near else self.far,
        )

    def onward(self, g, from_near):
        lo, mid, hi = self.groups[g]
        lo, hi = (lo, mid) if from_near else (mid, hi)
        part = self.part(self.near if from_near else self.far, lo, hi)
        return send(
            part,
            part,
            self.sems[2 if from_near else 3],
            g,
            dp=self.far if from_near else self.near,
        )

    def start(self, g):
        self.direct(g, True).start()
        self.direct(g, False).start()

    def forward(self, g):
        for which in (True, False):
            self.direct(g, which).wait_recv()
            self.onward(g, which).start()

    def take(self, g):
        self.onward(g, True).wait_recv()
        self.onward(g, False).wait_recv()

    def finish(self):
        for g in range(len(self.groups)):
            for which in (True, False):
                self.direct(g, which).wait_send()
                self.onward(g, which).wait_send()


class Reduce:
    def __init__(self, acc, stage, bounds, bufs, sems):
        self.acc, self.stage = acc, stage
        self.halves = (bounds[0:2], bounds[1:3])
        self.bufs, self.sems = bufs, sems
        at = lax.axis_index("dp")
        self.at = at
        self.near = at + 1 - 2 * lax.rem(at, 2)
        self.far = lax.rem(at + 2, 4)
        self.share = acc.shape[1] // 4

    def cols(self, shard):
        return pl.ds(pl.multiple_of(shard * self.share, 128), self.share)

    def first(self, half, slot):
        lo, hi = self.halves[half]
        to = (self.near, self.far)[half]
        shard = to if slot == 0 else 3 - self.at
        return send(
            self.stage.at[lo:hi, self.cols(shard)],
            self.bufs[half].at[slot],
            self.sems[half],
            slot,
            dp=to,
        )

    def second(self, half):
        return send(
            self.bufs[half].at[1],
            self.bufs[2 + half],
            self.sems[half],
            2,
            dp=(self.far, self.near)[half],
        )

    def start(self):
        for slot in (1, 0):
            for half in range(2):
                self.first(half, slot).start()

    def middle(self):
        for half in range(2):
            lo, hi = self.halves[half]
            other = (self.far, self.near)[half]
            self.first(half, 1).wait_recv()
            self.bufs[half][1] = (
                self.acc[lo:hi, self.cols(other)] + self.bufs[half][1].astype(F32)
            ).astype(BF16)
            self.second(half).start()

    def end(self):
        for half in range(2):
            lo, hi = self.halves[half]
            self.first(half, 0).wait_recv()
            self.second(half).wait_recv()
            mine = self.cols(self.at)
            self.acc[lo:hi, mine] = (
                self.acc[lo:hi, mine]
                + self.bufs[half][0].astype(F32)
                + self.bufs[2 + half][...].astype(F32)
            )

    def finish(self):
        for half in range(2):
            self.first(half, 0).wait_send()
            self.first(half, 1).wait_send()
            self.second(half).wait_send()


def layer_kernel(cfg, plan, names, *refs):
    r = types.SimpleNamespace(**dict(zip(names, refs, strict=True)))
    nh, pc, ns, width = cfg.nh, cfg.pc, cfg.ns, cfg.width
    gathers, blocks, units = cfg.gathers, cfg.blocks, cfg.units
    inner = nh * pc
    conv_rows = inner + 2 * ns
    step_row = 2 * ns
    inner_at = step_row + STEP_ROWS
    gate_at = inner_at + inner
    out_at = gate_at + inner
    rows = out_at + inner
    q, half = r.x_own.shape
    hq = q // 2
    unit_rows = q // units
    inner_width = H * P_SIZE
    step_at = pl.program_id(0)
    scans, block_at = walk(step_at, blocks)
    goes_down = step_at >= 2 * blocks
    chain_step = jnp.where(goes_down, step_at - blocks, block_at)
    row_at, col_at, dp_at = (lax.axis_index(name) for name in ("row", "col", "dp"))
    own_at = pl.multiple_of(row_at * half, 128)
    sib_at = pl.multiple_of((1 - row_at) * half, 128)
    own_cols, sib_cols = pl.ds(own_at, half), pl.ds(sib_at, half)
    group = cfg.row_count * cfg.col_count
    me = row_at * cfg.col_count + col_at
    peers = group_peers(cfg.row_count, cfg.col_count)
    friends = [dict(dp=lax.rem(dp_at + k, 4)) for k in range(1, 4)] if gathers else []
    weights = r.weights

    def out_rows(m):
        return r.out_total.at[pl.ds(pl.multiple_of(m * unit_rows, unit_rows), unit_rows)]

    def dn_rows(m):
        at = (2 * blocks - 1 - lax.div(m, units)) * q + lax.rem(m, units) * unit_rows
        return r.dn_total.at[pl.ds(pl.multiple_of(at, unit_rows), unit_rows)]

    chain = Chain(r, plan.total, blocks * units, out_rows, dn_rows)

    def send_parts(sib_part, own_part):
        for u in range(units):
            lo = u * unit_rows
            chain.begin(chain_step * units + u, sib_part[lo : lo + unit_rows])
        own = own_part()
        for u in range(units):
            lo = u * unit_rows
            chain.put_own(chain_step * units + u, own[lo : lo + unit_rows].astype(BF16))
        return own

    def progress(which, steps):
        if which == 0:

            @pl.when(chain_step > 0)
            def _():
                for u in range(units):
                    chain.stage_first((chain_step - 1) * units + u)

        for table, stage in (
            (plan.done, chain.stage_done),
            (plan.pair, chain.stage_pair),
            (plan.cross, chain.stage_cross),
        ):

            def one(m, _, stage=stage):
                stage(m)
                return 0

            lo, hi = plan.span(table, which, chain_step, steps)
            if lo is not hi:
                lax.fori_loop(lo, hi, one, 0)

    up_steps, down_steps = range(blocks), range(blocks, 2 * blocks)

    def token_rows(ref, b):
        return ref.at[pl.ds(pl.multiple_of(b * q, q), q)]

    def swap(which, b):
        src, dst = ((r.x_any, r.x_scr), (r.c_any, r.c_scr))[which]
        sems = (r.swap_sems.at[2 * which], r.swap_sems.at[2 * which + 1])
        return send(token_rows(src, b), dst.at[b], sems, b, row=1 - row_at)

    gain_swap = send(
        r.gain_own,
        r.gain_sib,
        (r.swap_sems.at[0], r.swap_sems.at[1]),
        blocks,
        row=1 - row_at,
    )

    def stat_copy(k):
        sems = (r.stat_sems.at[0], r.stat_sems.at[1])
        return send(r.stats.at[me], r.stats.at[me], sems, k, **peers[k])

    if gathers:
        bounds = (
            (0, cfg.early_split, inner_at),
            (inner_at, inner_at + inner // 2, gate_at),
            (gate_at, gate_at + inner // 2, out_at),
            (out_at, out_at + inner // 2, rows),
        )
        sems = [(r.gather_sems.at[2 * k], r.gather_sems.at[2 * k + 1]) for k in range(4)]
        gather = Gather(weights, sems, bounds)
        early = Reduce(
            r.acc_w,
            weights,
            (0, cfg.early_split, inner_at),
            (r.ea_top, r.ea_low, r.ea_top_last, r.ea_low_last),
            [(r.ea_sems.at[2 * k], r.ea_sems.at[2 * k + 1]) for k in range(2)],
        )
        late = Reduce(
            r.acc_w,
            weights,
            (inner_at, (inner_at + rows) // 2, rows),
            (r.rs_top, r.rs_low, r.rs_top_last, r.rs_low_last),
            [(r.rs_sems.at[2 * k], r.rs_sems.at[2 * k + 1]) for k in range(2)],
        )
        share = width // 4
        mine = early.cols(dp_at)
        raw = (
            (r.inner_w, 0, inner, 0, share),
            (r.state_w, 0, share, share, 2 * ns),
            (r.gate_w, inner, inner, 0, share),
            (r.out_w, 2 * inner, inner, 0, share),
        )

        def raw_copy(k):
            src, lo, count, at, size = raw[k]
            return pltpu.make_async_copy(
                src, r.acc_w.at[lo : lo + count, at : at + size], r.raw_sems.at[k]
            )

        def raw_value(k):
            _, lo, count, at, size = raw[k]
            return r.acc_w[lo : lo + count, at : at + size]

    @pl.when(step_at == 0)
    def _():
        greet(peers + friends)
        if gathers:
            for k in range(len(raw)):
                raw_copy(k).start()
            for k in range(len(raw)):
                raw_copy(k).wait()
            step_rows = jnp.concatenate(
                [r.step_w[...], jnp.zeros((STEP_ROWS - nh, share), F32)], axis=0
            )
            weights[0:step_row, mine] = raw_value(1).T.astype(BF16)
            weights[step_row:inner_at, mine] = step_rows.astype(BF16)
            weights[inner_at:gate_at, mine] = raw_value(0).astype(BF16)
            weights[gate_at:out_at, mine] = raw_value(2).astype(BF16)
            weights[out_at:, mine] = raw_value(3).astype(BF16)
        greeted(peers + friends)
        if gathers:
            gather.start(0)
            gather.start(1)
        gain_swap.start()
        for b in range(blocks):
            swap(0, b).start()
            swap(1, b).start()
        load_columns(r.par_rows, r.head_rows, r.conv, r.head)
        for ref in (r.acc_w, r.state, r.after, r.acc_conv, r.acc_chan, r.acc_head):
            ref[...] = jnp.zeros_like(ref)
        for ref in (r.acc_norm, r.acc_dot, r.scale):
            ref[...] = jnp.zeros_like(ref)
        r.pre[:, 0:128] = jnp.zeros((conv_rows, 128), F32)
        r.prev_seg[...] = jnp.full_like(r.prev_seg, -1.0)
        gain_swap.wait_recv()
        if gathers:
            gather.forward(0)
            gather.forward(1)
            gather.start(2)
            gather.start(3)
            gather.take(0)
            gather.take(1)

    def scan_step():
        b = block_at
        here = pl.ds(pl.multiple_of(b * q, q), q)
        swap(0, b).wait_recv()
        xo = r.x_own[...].astype(F32)
        xs = r.x_scr[b].astype(F32)
        squares = jnp.sum(xo * xo, axis=1, keepdims=True) + jnp.sum(
            xs * xs, axis=1, keepdims=True
        )
        scaling = lax.rsqrt(squares / width + EPSILON)
        lanes = lax.broadcasted_iota(jnp.int32, r.scale.shape, 1)
        r.scale[...] = jnp.where(lanes == b, scaling, r.scale[...])
        no = (xo * scaling * r.gain_own[...]).astype(BF16)
        nsib = (xs * scaling * r.gain_sib[...]).astype(BF16)
        pre = dot_nt(weights[0:gate_at, own_cols], no) + dot_nt(weights[0:gate_at, sib_cols], nsib)
        values = jnp.concatenate([pre[inner_at:gate_at], pre[0:step_row]], axis=0)
        step_pre = pre[step_row:inner_at]
        r.pre[:, pl.ds(pl.multiple_of(b * q + 128, 128), q)] = values
        r.step[:, here] = step_pre
        seg = r.seg[...].astype(F32)
        seg_before = r.prev_seg[...]
        seg_joined = jnp.concatenate([seg_before, seg], axis=1)
        before, final = seg_before[:, 127:128], seg[:, q - 1 : q]
        aux = jnp.concatenate(
            [
                (seg_joined[:, 128 - offset : 128 - offset + q] == seg).astype(F32)
                for offset in range(1, 4)
            ]
            + [
                seg,
                (seg == before).astype(F32),
                (seg == final).astype(F32),
                jnp.broadcast_to((before == final).astype(F32), (1, q)),
                jnp.zeros((1, q), F32),
            ],
            axis=0,
        )
        r.prev_seg[...] = seg[:, q - 128 :]
        r.aux[:, here] = aux
        conv = r.conv[...]
        head = r.head[...]
        arg = conv_args(r, conv, aux, b, q)
        act = arg * sigmoid(arg)
        r.work[...] = act[0:inner]
        in_low = act[inner : inner + ns].astype(BF16)
        out_low = act[inner + ns :].astype(BF16)

        _, step, cumul, last, cols = block_rows(None, step_pre, head, aux)
        source = lax.broadcasted_iota(jnp.int32, (q, q), 0)
        target = lax.broadcasted_iota(jnp.int32, (q, q), 1)
        seg_col = cols[:, STEP_ROWS + 3 : STEP_ROWS + 4]
        bias = jnp.where((source <= target) & (seg_col == aux[3:4]), 0.0, NEG)
        pairs = dot_tn(in_low, out_low)
        entering = r.state[...]
        r.states[b] = entering
        from_state = dot_nn(entering.astype(BF16), out_low)
        reach = aux[4:5] * jnp.exp(cumul)
        tails = aux[5:6] * jnp.exp(last - cumul)
        keep = aux[6:7, 0:1] * jnp.exp(last)
        tail_parts = []
        for h in range(nh):
            lo = h * pc
            x_h = r.work[lo : lo + pc]
            u_h = (x_h * step[h : h + 1]).astype(BF16)
            tail_parts.append((x_h * (step[h : h + 1] * tails[h : h + 1])).astype(BF16))
            col = cols[:, h : h + 1]
            row = cumul[h : h + 1]
            top = (jnp.exp((row - col[:hq]) + bias[:hq]) * pairs[:hq]).astype(BF16)
            low = jnp.exp((row[:, hq:] - col[hq:]) + bias[hq:, hq:]) * pairs[hq:, hq:]
            y_top = dot_nn(u_h[:, :hq], top)
            y_low = dot_nn(u_h[:, hq:], low.astype(BF16))
            y_h = jnp.concatenate([y_top[:, :hq], y_top[:, hq:] + y_low], axis=1)
            y_h = y_h + from_state[lo : lo + pc] * reach[h : h + 1]
            r.mixed[lo : lo + pc, here] = y_h + head[h : h + 1, 2:3] * x_h
        contrib = dot_nt(jnp.concatenate(tail_parts, axis=0), in_low)
        for h in range(nh):
            lo = h * pc
            r.state[lo : lo + pc] = keep[h : h + 1] * entering[lo : lo + pc] + contrib[lo : lo + pc]

    def out_step():
        b = block_at
        here = pl.ds(pl.multiple_of(b * q, q), q)
        gain = r.conv[0:inner, 5:6]
        if gathers:

            @pl.when(step_at == AHEAD)
            def _():
                gather.take(2)

        no, nsib, _ = normed_block(b)
        gate = dot_nt(weights[gate_at:out_at, own_cols], no) + dot_nt(
            weights[gate_at:out_at, sib_cols], nsib
        )
        r.gate[:, here] = gate.astype(BF16)
        progress(0, up_steps)
        gated = r.mixed[:, here] * (gate * sigmoid(gate))
        squares_row = jnp.sum(gated * gated, axis=0, keepdims=True)
        weighted = gated * gain
        low = weighted.astype(BF16)
        if gathers:

            @pl.when(step_at == AHEAD)
            def _():
                gather.take(3)

        send_parts(
            dot_tn(low, weights[out_at:, sib_cols]).astype(BF16),
            lambda: dot_tn(low, weights[out_at:, own_cols]),
        )
        progress(7, up_steps)
        swap(1, b).wait_recv()
        dng = dot_nt(weights[out_at:, own_cols], r.c_own[...]) + dot_nt(
            weights[out_at:, sib_cols], r.c_scr[b]
        )
        r.dng[:, here] = dng.astype(BF16)
        r.stats[me, pl.ds(b, 1)] = squares_row
        r.stats[me, pl.ds(blocks + b, 1)] = jnp.sum(dng * weighted, axis=0, keepdims=True)

    def normed_block(b):
        lanes = lax.broadcasted_iota(jnp.int32, r.scale.shape, 1)
        scaling = jnp.sum(jnp.where(lanes == b, r.scale[...], 0.0), axis=1, keepdims=True)
        no = (r.x_own[...].astype(F32) * scaling * r.gain_own[...]).astype(BF16)
        nsib = (r.x_scr[b].astype(F32) * scaling * r.gain_sib[...]).astype(BF16)
        return no, nsib, lanes

    def backward_step():
        b = block_at
        here = pl.ds(pl.multiple_of(b * q, q), q)
        aux = r.aux[:, here]
        conv = r.conv[...]
        gain = conv[0:inner, 5:6]
        head = r.head[...]
        no, nsib, lanes = normed_block(b)
        arg = conv_args(r, conv, aux, b, q)
        sig_arg = sigmoid(arg)
        act = arg * sig_arg
        r.slope[...] = sig_arg * (1.0 + arg * (1.0 - sig_arg))
        x_all = act[0:inner]
        in_low = act[inner : inner + ns].astype(BF16)
        out_low = act[inner + ns :].astype(BF16)
        step_arg, step, cumul, last, cols = block_rows(None, r.step[:, here], head, aux)
        gate = r.gate[:, here].astype(F32)
        sig = sigmoid(gate)
        silu = gate * sig
        mixed = r.mixed[:, here]
        gated = mixed * silu

        for which in range(len(TURN_AT)):
            progress(which, down_steps)

        @pl.when(step_at == 2 * blocks)
        def _():
            for k in range(group - 1):
                stat_copy(k).wait()

        square_sum, gate_dot = jnp.zeros((1, q), F32), jnp.zeros((1, q), F32)
        for k in range(group):
            square_sum = square_sum + r.stats[k, pl.ds(b, 1)]
            gate_dot = gate_dot + r.stats[k, pl.ds(blocks + b, 1)]
        gate_scale = lax.rsqrt(square_sum / inner_width + EPSILON)
        pull = gate_scale * gate_scale * gate_scale * gate_dot / inner_width
        dng_scaled = r.dng[:, here].astype(F32) * gate_scale
        d_gated = gain * dng_scaled - gated * pull
        r.acc_chan[0] += lane_fold(dng_scaled * gated)
        normed_gate = (gated * (gate_scale * gain)).astype(BF16)
        r.acc_w[out_at:, own_cols] += dot_nn(normed_gate, r.c_own[...])
        r.acc_w[out_at:, sib_cols] += dot_nn(normed_gate, r.c_scr[b])
        grad_mixed = d_gated * silu
        r.low[gate_at:out_at] = (d_gated * mixed * (sig * (1.0 + gate * (1.0 - sig)))).astype(BF16)
        progress(3, down_steps)

        t_at = lax.broadcasted_iota(jnp.int32, (q, q), 0)
        s_at = lax.broadcasted_iota(jnp.int32, (q, q), 1)
        seg_col = cols[:, STEP_ROWS + 3 : STEP_ROWS + 4]
        bias = jnp.where((s_at <= t_at) & (seg_col == aux[3:4]), 0.0, NEG)
        pairs = dot_tn(out_low, in_low)
        reach = aux[4:5] * jnp.exp(cumul)
        tails = aux[5:6] * jnp.exp(last - cumul)
        keep = aux[6:7, 0:1] * jnp.exp(last)
        entering = r.states[b]

        @pl.when(step_at == 2 * blocks)
        def _():
            r.state[...] = jnp.zeros_like(r.state)

        d_next = r.state[...]
        from_next = dot_nn(d_next.astype(BF16), in_low)
        r.acc_chan[1] += lane_fold(grad_mixed * x_all)
        d_pairs_top = jnp.zeros((hq, hq), F32)
        d_pairs_low = jnp.zeros((hq, q), F32)
        reach_parts, tail_parts = [], []
        row_sums, col_sums, x_sums, tail_sums, carry_sums = [], [], [], [], []
        for h in range(nh):
            lo = h * pc
            x_h = x_all[lo : lo + pc]
            u_h = x_h * step[h : h + 1]
            u_low = u_h.astype(BF16)
            g_h = grad_mixed[lo : lo + pc]
            g_low = g_h.astype(BF16)
            col = cols[:, h : h + 1]
            row = cumul[h : h + 1]
            reach_parts.append((g_h * reach[h : h + 1]).astype(BF16))
            tail_parts.append((u_h * tails[h : h + 1]).astype(BF16))
            e_top = jnp.exp((col[:hq] - row[:, :hq]) + bias[:hq, :hq])
            e_low = jnp.exp((col[hq:] - row) + bias[hq:])
            m_top = (e_top * pairs[:hq, :hq]).astype(BF16)
            m_low = (e_low * pairs[hq:]).astype(BF16)
            dm_top = dot_tn(g_low[:, :hq], u_low[:, :hq])
            dm_low = dot_tn(g_low[:, hq:], u_low)
            d_pairs_top = d_pairs_top + dm_top * e_top
            d_pairs_low = d_pairs_low + dm_low * e_low
            du_top = dot_nn(g_low[:, :hq], m_top)
            du_low = dot_nn(g_low[:, hq:], m_low)
            du_local = jnp.concatenate([du_top + du_low[:, :hq], du_low[:, hq:]], axis=1)
            du_next = from_next[lo : lo + pc] * tails[h : h + 1]
            du = du_local + du_next
            skip = head[h : h + 1, 2:3]
            r.work[lo : lo + pc] = du * step[h : h + 1] + skip * g_h
            u_round = u_low.astype(F32)
            y_h = mixed[lo : lo + pc] - skip * x_h
            row_sums.append(jnp.sum(g_low.astype(F32) * y_h, axis=0, keepdims=True))
            next_sum = jnp.sum(u_round * du_next, axis=0, keepdims=True)
            col_sums.append(jnp.sum(u_round * du_local, axis=0, keepdims=True) + next_sum)
            tail_sums.append(next_sum)
            x_sums.append(jnp.sum(x_h * du, axis=0, keepdims=True))
            carry_sums.append(
                jnp.sum(entering[lo : lo + pc] * d_next[lo : lo + pc], axis=0, keepdims=True)
            )
            if h in (nh // 3, 2 * nh // 3):
                progress(3 + h // (nh // 3), down_steps)
        progress(6, down_steps)
        pad_rows = [jnp.zeros((STEP_ROWS - nh, q), F32)]
        row_sum = jnp.concatenate(row_sums + pad_rows, axis=0)
        col_sum = jnp.concatenate(col_sums + pad_rows, axis=0)
        tail_sum = jnp.concatenate(tail_sums + pad_rows, axis=0)
        x_sum = jnp.concatenate(x_sums + pad_rows, axis=0)
        carry = jnp.concatenate(carry_sums + [jnp.zeros((STEP_ROWS - nh, ns), F32)], axis=0)
        d_last = jnp.sum(tail_sum, axis=1, keepdims=True) + keep * jnp.sum(
            carry, axis=1, keepdims=True
        )
        later = (t_at >= s_at).astype(F32)
        d_log = dot_nn(row_sum - col_sum, later, HIGHEST) + d_last
        d_step = x_sum + head[:, 1:2] * d_log
        d_step_arg = d_step * sigmoid(step_arg)
        r.acc_head[0] += lane_fold(d_step_arg)
        r.acc_head[1] += lane_fold(step * d_log)
        r.low[step_row:inner_at] = d_step_arg.astype(BF16)

        g_reach = jnp.concatenate(reach_parts, axis=0)
        u_tail = jnp.concatenate(tail_parts, axis=0)
        d_top_low = d_pairs_top.astype(BF16)
        d_low_low = d_pairs_low.astype(BF16)
        d_out = dot_tn(entering.astype(BF16), g_reach)
        d_out = d_out + jnp.concatenate(
            [dot_nt(in_low[:, :hq], d_top_low), dot_nt(in_low, d_low_low)], axis=1
        )
        d_in = dot_tn(d_next.astype(BF16), u_tail) + dot_nn(out_low[:, hq:], d_low_low)
        d_in_top = dot_nn(out_low[:, :hq], d_top_low)
        d_in = jnp.concatenate([d_in[:, :hq] + d_in_top, d_in[:, hq:]], axis=1)
        d_enter = dot_nt(g_reach, out_low)
        for h in range(nh):
            lo = h * pc
            r.state[lo : lo + pc] = keep[h : h + 1] * d_next[lo : lo + pc] + d_enter[lo : lo + pc]

        err = jnp.concatenate([r.work[...], d_in, d_out], axis=0) * r.slope[...]
        values = r.pre[:, pl.ds(pl.multiple_of(b * q + 128, 128), q)]
        d_pre = conv[:, 3:4] * err
        r.acc_conv[3] += lane_fold(err * values)
        r.acc_conv[4] += lane_fold(err)
        for offset in range(1, 4):
            masked = err * aux[offset - 1 : offset]
            joined = jnp.concatenate([masked, r.after[offset - 1]], axis=1)
            shifted = joined[:, offset : offset + q]
            r.after[offset - 1] = masked[:, :128]
            d_pre = d_pre + conv[:, 3 - offset : 4 - offset] * shifted
            r.acc_conv[3 - offset] += lane_fold(shifted * values)
        r.low[inner_at:gate_at] = d_pre[0:inner].astype(BF16)
        r.low[0:step_row] = d_pre[inner:].astype(BF16)
        progress(7, down_steps)
        low = r.low[...]
        dn_sib = dot_tn(low, weights[0:out_at, sib_cols])
        dn_own = send_parts(
            dn_sib.astype(BF16), lambda: dot_tn(low, weights[0:out_at, own_cols])
        )
        token_dot = jnp.zeros((q, 1), F32)
        for which, (part, seen) in enumerate(((dn_own, no), (dn_sib, nsib))):
            product = part * seen.astype(F32)
            token_dot = token_dot + jnp.sum(product, axis=1, keepdims=True)
            r.acc_norm[which] += jnp.sum(product.reshape(q // 8, 8, half), axis=0)
        r.acc_dot[...] = jnp.where(lanes == b, token_dot, r.acc_dot[...])
        r.acc_w[0:out_at, own_cols] += dot_nn(low, no)
        r.acc_w[0:out_at, sib_cols] += dot_nn(low, nsib)

    def ending():
        lane = 2 * ns
        if gathers:
            weights[0:inner_at] = r.acc_w[0:inner_at].astype(BF16)
            early.start()
        else:
            r.grad_w[...] = r.acc_w[...].astype(BF16)
        for u in range(units):
            chain.stage_first((2 * blocks - 1) * units + u)
        zeros = jnp.zeros((1, 128), F32)
        conv_vec, chan_vec, head_vec = (
            rows_of(ref) for ref in (r.acc_conv, r.acc_chan, r.acc_head)
        )
        norm_vec = [jnp.sum(r.acc_norm[which], axis=0, keepdims=True) for which in range(2)]
        skip = chan_vec[1:2]
        r.group_vec[me] = jnp.concatenate(
            [
                conv_vec[0:5, inner:],
                skip[:, 0:lane],
                jnp.concatenate([skip[:, lane:], head_vec[0:1]], axis=1),
                jnp.concatenate([head_vec[1:2], zeros], axis=1),
                r.acc_dot[...].T[0:blocks],
            ]
            + [vec[:, at : at + lane] for vec in norm_vec for at in range(0, half, lane)]
            + [jnp.zeros((2, lane), F32)],
            axis=0,
        )

        def group_copy(k):
            sems = (r.group_sems.at[0], r.group_sems.at[1])
            return send(r.group_vec.at[me], r.group_vec.at[me], sems, k, **peers[k])

        for k in range(group - 1):
            group_copy(k).start()

        n_pair, n_cross, n_done = (
            plan.left(table) for table in (plan.pair, plan.cross, plan.done)
        )

        def late_cross(m, _):
            chain.stage_cross(m)
            return 0

        lax.fori_loop(n_cross, max(n_cross, n_pair - 1), late_cross, 0)
        n_cross = max(n_cross, n_pair - 1)
        drained = [n_pair]

        def drain(count=None):
            lo = drained[0]
            hi = plan.total + 1 if count is None else min(plan.total, n_pair + count)
            drained[0] = max(lo, hi)

            def one(m, _):
                @pl.when((m - chain.slots >= n_done) & (m < plan.total))
                def _():
                    chain.stage_done(m - chain.slots)

                @pl.when(m < plan.total)
                def _():
                    chain.stage_pair(m)

                @pl.when(m - 1 >= n_cross)
                def _():
                    chain.stage_cross(m - 1)

                return 0

            lax.fori_loop(lo, max(lo, hi), one, 0)

        if gathers:
            middle = (inner_at + rows) // 2
            for at, (lo, hi) in enumerate(((inner_at, middle), (middle, rows))):
                drain(cfg.stops[at])
                weights[lo:hi] = r.acc_w[lo:hi].astype(BF16)
            drain(cfg.stops[2])
            early.middle()
            late.start()
            drain(cfg.stops[3])
            early.end()
            slice_rows = 2 * ns // group
            for k in range(group):
                lo = k * slice_rows
                r.state_send[k] = r.acc_w[lo : lo + slice_rows, mine].astype(BF16)
            r.step_swap[0] = r.acc_w[step_row:inner_at, mine]

            def state_copy(phase, k):
                peer = peers[k]
                sems = (r.state_sems.at[2 * phase], r.state_sems.at[2 * phase + 1])
                to = peer["row"] * cfg.col_count + peer["col"]
                if phase == 0:
                    return send(r.state_send.at[to], r.state_recv.at[me], sems, k, **peer)
                return send(r.state_all.at[me], r.state_all.at[me], sems, k, **peer)

            step_copy = send(
                r.step_swap.at[0],
                r.step_swap.at[1],
                (r.state_sems.at[0], r.state_sems.at[1]),
                group - 1,
                row=1 - row_at,
            )
            for k in range(group - 1):
                state_copy(0, k).start()
            step_copy.start()
            r.state_recv[me] = r.state_send[me]
        drain(cfg.stops[4])

        for k in range(group - 1):
            group_copy(k).wait()
        shared = r.group_vec[0]
        for k in range(1, group):
            shared = shared + r.group_vec[k]
        by_row, by_head = jnp.zeros((3, lane), F32), jnp.zeros((3, lane), F32)
        for k in range(group):
            one = r.group_vec[k]
            same_row, same_col = (k // cfg.col_count) == row_at, (k % cfg.col_count) == col_at
            by_row = by_row + jnp.where(same_row, one[16:19], one[19:22])
            by_head = by_head + jnp.where(same_col, one[5:8], 0.0)
        scale = r.scale[...].T[0:blocks]
        square_sum = r.stats[0, 0:blocks]
        for k in range(1, group):
            square_sum = square_sum + r.stats[k, 0:blocks]
        gate_scale = lax.rsqrt(square_sum / inner_width + EPSILON)
        r.token_out[...] = jnp.concatenate(
            [scale, shared[8:16] * scale * scale / width, gate_scale], axis=0
        )
        norm_sum = jnp.concatenate([by_row[at : at + 1] for at in range(half // lane)], axis=1)
        norm_sum = norm_sum / r.gain_own[...]
        skip_sum = jnp.concatenate([by_head[0:1], by_head[1:2, 0:128]], axis=1)
        r.dp_vec[0] = jnp.concatenate(
            [
                jnp.concatenate([conv_vec[0:5, 0:inner], shared[0:5]], axis=1),
                jnp.concatenate([chan_vec[0:1], by_head[1:2, 128:], by_head[2:3, 0:128]], axis=1),
                jnp.concatenate([skip_sum, norm_sum[:, 0:lane]], axis=1),
                jnp.concatenate([norm_sum[:, lane:], zeros], axis=1),
            ],
            axis=0,
        )

        def dp_copy(k):
            sems = (r.dp_sems.at[0], r.dp_sems.at[1])
            return send(r.dp_vec.at[0], r.dp_vec.at[k], sems, k - 1, **friends[k - 1])

        if not gathers:
            r.vec_out[...] = r.dp_vec[0]
            drain()
        else:
            for k in range(1, 4):
                dp_copy(k).start()
            drain(cfg.stops[5])
            for k in range(group - 1):
                state_copy(0, k).wait()
            summed = r.state_recv[0].astype(F32)
            for k in range(1, group):
                summed = summed + r.state_recv[k].astype(F32)
            r.state_all[me] = summed.astype(BF16)
            for k in range(group - 1):
                state_copy(1, k).start()
            step_copy.wait()
            r.g_step[...] = r.step_swap[0] + r.step_swap[1]
            drain(cfg.stops[6])
            late.middle()
            drain(cfg.stops[7])
            for k in range(1, 4):
                dp_copy(k).wait()
            ordered = [lax.rem(dp_at - k + 4, 4) for k in range(4)]
            total = r.dp_vec[ordered[0]]
            for k in range(1, 4):
                total = total + r.dp_vec[ordered[k]]
            r.vec_out[...] = total
            drain(cfg.stops[8])
            late.end()
            r.g_inner[...] = r.acc_w[inner_at:gate_at, mine]
            r.g_gate[...] = r.acc_w[gate_at:out_at, mine]
            r.g_out[...] = r.acc_w[out_at:, mine]
            drain()
            for k in range(group - 1):
                state_copy(1, k).wait()
            whole_state = [r.state_all[k].astype(F32) for k in range(group)]
            r.g_state[...] = jnp.concatenate(whole_state, axis=0).T
            early.finish()
            late.finish()
        last_done = max(n_done, plan.total - chain.slots)

        def settle(m, _):
            chain.stage_done(m)
            return 0

        lax.fori_loop(last_done, plan.total, settle, 0)
        for m in range(plan.total - chain.out_slots, plan.total):
            chain.exchange(m).wait_send()

    @pl.when(scans == 1)
    def _():
        scan_step()

    if gathers:
        for g, at in ((2, FORWARD_AT[0]), (3, FORWARD_AT[1])):

            @pl.when(step_at == at)
            def _(g=g):
                gather.forward(g)

    @pl.when((scans == 0) & ~goes_down)
    def _():
        out_step()

    @pl.when(step_at == 2 * blocks - 1)
    def _():
        for k in range(group - 1):
            stat_copy(k).start()
        gain_swap.wait_send()
        for b in range(blocks):
            swap(0, b).wait_send()
            swap(1, b).wait_send()
        if gathers:
            gather.finish()

    @pl.when(step_at >= 2 * blocks)
    def _():
        backward_step()

    @pl.when(step_at == 3 * blocks - 1)
    def _():
        ending()


def walk(step, blocks):
    def flag(test):
        return test.astype(jnp.int32)

    mixed = blocks - AHEAD
    at = step - AHEAD
    early = flag(at < 0)
    late = flag(at >= 2 * mixed)
    down = flag(step >= 2 * blocks)
    turn = (1 - early) * (1 - late)
    ahead = at + early * AHEAD
    odd = turn * lax.rem(ahead, 2)
    pair = lax.div(ahead, 2)
    block = (
        early * step
        + turn * (pair + odd * AHEAD)
        + late * (1 - down) * (step - blocks)
        + down * (3 * blocks - 1 - step)
    )
    return early + odd, block


def conv_args(r, conv, aux, b, q):
    rows = conv.shape[0]
    joined = r.pre[:, pl.ds(pl.multiple_of(b * q, q), q + 128)]
    arg = conv[:, 4:5] + conv[:, 3:4] * joined[:, 128:]
    for offset in range(1, 4):
        arg = arg + conv[:, 3 - offset : 4 - offset] * (
            aux[offset - 1 : offset] * joined[:, 128 - offset : 128 - offset + q]
        )
    return arg


def per_device(
    inputs,
    segments,
    cotangent,
    norm_gain,
    gate_proj,
    inner_proj,
    state_proj,
    step_proj,
    conv_inner,
    bias_inner,
    conv_state,
    bias_state,
    step_bias,
    decay_log,
    skip_gain,
    gate_norm,
    out_proj,
):
    length, half = inputs.shape
    row_count = lax.axis_size("row")
    col_count = lax.axis_size("col")
    col_at = lax.axis_index("col")
    width = half * row_count
    share, nh, pc = gate_proj.shape
    inner = nh * pc
    state_width = state_proj.shape[1]
    ns = state_width // 2
    conv_rows = inner + state_width
    gate_at = conv_rows + STEP_ROWS
    out_at = gate_at + inner
    rows = out_at + inner
    q = BLOCK_LEN
    blocks = length // q

    def channel_rows(w):
        return jnp.transpose(w, (1, 2, 0)).reshape(inner, share)

    gathers = lax.axis_size("dp") == 4 and share % 128 == 0
    parts = [
        channel_rows(inner_proj),
        state_proj,
        step_proj.T,
        channel_rows(gate_proj),
        channel_rows(out_proj),
    ]
    if not gathers:
        step_rows = jnp.pad(step_proj.T, ((0, STEP_ROWS - nh), (0, 0)))
        parts = [state_proj.T, step_rows, parts[0], parts[3], parts[4]]
        stacked = jnp.concatenate(parts, axis=0).astype(BF16)
        parts = [lax.all_gather(stacked, "dp", axis=1, tiled=True)]
    gain_own = norm_gain[None, :]
    group = row_count * col_count

    chan_rows = jnp.concatenate(
        [
            conv_inner,
            bias_inner[None],
            gate_norm[None],
            jnp.zeros((2, nh, pc), F32),
        ],
        axis=0,
    ).reshape(8, inner)
    state_rows = jnp.concatenate(
        [conv_state, bias_state[None], jnp.zeros((3, state_width), F32)], axis=0
    )
    par_rows = jnp.concatenate([chan_rows, state_rows], axis=1)
    head_rows = jnp.pad(
        jnp.stack([step_bias, decay_log, skip_gain]), ((0, 5), (0, 128 - nh))
    )

    units = UNITS
    slots = blocks * units
    cfg = types.SimpleNamespace(
        nh=nh,
        pc=pc,
        ns=ns,
        width=width,
        row_count=row_count,
        col_count=col_count,
        gathers=gathers,
        blocks=blocks,
        units=units,
        early_split=144,
        stops=STOPS,
    )
    plan = Plan(blocks, units, slots, *MODEL)

    def fold(i):
        return walk(i, blocks)[1]

    def whole(*shape):
        return pl.BlockSpec(shape, lambda i: (0,) * len(shape), pipeline_mode=pl.Buffered(1))

    sds, dma, vmem = jax.ShapeDtypeStruct, pltpu.SemaphoreType.DMA, pltpu.VMEM
    anywhere = pl.BlockSpec(memory_space=pl.ANY)
    token_block = pl.BlockSpec((q, half), lambda i: (fold(i), 0))
    ins = {
        "x_own": (inputs, token_block),
        "c_own": (cotangent, token_block),
        "x_any": (inputs, anywhere),
        "c_any": (cotangent, anywhere),
        "gain_own": (gain_own, whole(1, half)),
        "seg": (segments, pl.BlockSpec((1, q), lambda i: (0, fold(i)))),
        "par_rows": (par_rows, whole(8, conv_rows)),
        "head_rows": (head_rows, whole(8, 128)),
    }
    outs = {
        "out_total": (sds((length, half), BF16), anywhere),
        "dn_total": (sds((length, half), BF16), anywhere),
        "token_out": (sds((3 * blocks, q), F32), whole(3 * blocks, q)),
        "vec_out": (sds((8, conv_rows), F32), whole(8, conv_rows)),
    }
    scratch = {
        "acc_w": vmem((rows, width), F32),
        "x_scr": vmem((blocks, q, half), BF16),
        "c_scr": vmem((blocks, q, half), BF16),
        "gain_sib": vmem((1, half), F32),
        "conv": vmem((conv_rows, 128), F32),
        "head": vmem((STEP_ROWS, 128), F32),
        "prev_seg": vmem((1, 128), F32),
        "pre": vmem((conv_rows, length + 128), F32),
        "step": vmem((STEP_ROWS, length), F32),
        "gate": vmem((inner, length), BF16),
        "mixed": vmem((inner, length), F32),
        "dng": vmem((inner, length), BF16),
        "aux": vmem((8, length), F32),
        "scale": vmem((q, 128), F32),
        "states": vmem((blocks, inner, ns), F32),
        "state": vmem((inner, ns), F32),
        "stats": vmem((group, 2 * blocks, q), F32),
        "work": vmem((inner, q), F32),
        "slope": vmem((conv_rows, q), F32),
        "low": vmem((out_at, q), BF16),
        "after": vmem((3, conv_rows, 128), F32),
        "acc_conv": vmem((5, conv_rows, 128), F32),
        "acc_chan": vmem((2, inner, 128), F32),
        "acc_head": vmem((2, STEP_ROWS, 128), F32),
        "acc_norm": vmem((2, 8, half), F32),
        "acc_dot": vmem((q, 128), F32),
        "group_vec": vmem((group, 24, 2 * ns), F32),
        "dp_vec": vmem((4, 8, conv_rows), F32),
        "ch_own": vmem((2 * units, q // units, half), BF16),
        "ch_sib": vmem((2 * units, q // units, half), BF16),
        "ch_first": vmem((slots, q // units, half), BF16),
        "ch_pair": vmem((slots, q // units, half), BF16),
        "ch_cross": vmem((slots, q // units, half), BF16),
        "cs_send": dma((4, slots)),
        "cs_recv": dma((4, slots)),
        "cs_keep": dma((slots,)),
        "ch_free": pltpu.SemaphoreType.REGULAR((3,)),
        "swap_sems": dma((4, blocks + 1)),
        "stat_sems": dma((2, group - 1)),
        "group_sems": dma((2, group - 1)),
        "dp_sems": dma((2, 3)),
    }
    if gathers:
        for name, part in zip(("inner_w", "state_w", "step_w", "gate_w", "out_w"), parts):
            ins[name] = (part, whole(*part.shape) if name == "step_w" else anywhere)
        grad_shape = sds((inner, share), F32)
        outs["g_inner"] = (grad_shape, whole(inner, share))
        outs["g_gate"] = (grad_shape, whole(inner, share))
        outs["g_out"] = (grad_shape, whole(inner, share))
        outs["g_state"] = (sds((share, state_width), F32), whole(share, state_width))
        outs["g_step"] = (sds((STEP_ROWS, share), F32), whole(STEP_ROWS, share))
        pieces = (group, state_width // group, share)
        early_rows = state_width + STEP_ROWS
        late_half = (rows - early_rows) // 2
        scratch.update(
            weights=vmem((rows, width), BF16),
            gather_sems=dma((8, 4)),
            raw_sems=dma((4,)),
            ea_top=vmem((2, cfg.early_split, share), BF16),
            ea_low=vmem((2, early_rows - cfg.early_split, share), BF16),
            ea_top_last=vmem((cfg.early_split, share), BF16),
            ea_low_last=vmem((early_rows - cfg.early_split, share), BF16),
            ea_sems=dma((4, 3)),
            rs_top=vmem((2, late_half, share), BF16),
            rs_low=vmem((2, late_half, share), BF16),
            rs_top_last=vmem((late_half, share), BF16),
            rs_low_last=vmem((late_half, share), BF16),
            rs_sems=dma((4, 3)),
            step_swap=vmem((2, STEP_ROWS, share), F32),
            state_send=vmem(pieces, BF16),
            state_recv=vmem(pieces, BF16),
            state_all=vmem(pieces, BF16),
            state_sems=dma((4, group)),
        )
    else:
        ins["weights"] = (parts[0], whole(rows, width))
        outs["grad_w"] = (sds((rows, width), BF16), whole(rows, width))
    names = (*ins, *outs, *scratch)
    results = pl.pallas_call(
        functools.partial(layer_kernel, cfg, plan, names),
        name="layer",
        grid=(3 * blocks,),
        in_specs=[spec for _, spec in ins.values()],
        out_specs=[spec for _, spec in outs.values()],
        out_shape=[shape for shape, _ in outs.values()],
        scratch_shapes=list(scratch.values()),
        compiler_params=pltpu.CompilerParams(
            vmem_limit_bytes=VMEM_LIMIT, collective_id=1, has_side_effects=True
        ),
        cost_estimate=pl.CostEstimate(
            flops=6 * length * width * rows,
            bytes_accessed=60 << 20,
            transcendentals=2 * nh * length * q,
        ),
    )(*(array for array, _ in ins.values()))
    made = types.SimpleNamespace(**dict(zip(outs, results, strict=True)))
    tokens = made.token_out.reshape(3, length)
    scale, pull, gate_scale = (tokens[k][:, None] for k in range(3))
    plain = inputs.astype(F32)
    output = (plain + gate_scale * made.out_total.astype(F32)).astype(BF16)
    weighted = made.dn_total.astype(F32) * gain_own
    grad_inputs = cotangent.astype(F32) + scale * weighted - plain * pull
    vectors = made.vec_out
    if gathers:
        g_inner, g_gate, g_out = made.g_inner, made.g_gate, made.g_out
        g_state, g_step = made.g_state, made.g_step
    else:
        grads = lax.psum_scatter(made.grad_w, "dp", scatter_dimension=1, tiled=True)
        grads = grads.astype(F32)
        vectors = lax.psum(vectors, "dp")
        g_state = lax.psum(grads[0:state_width], ("row", "col")).T
        g_step = lax.psum(grads[state_width : state_width + STEP_ROWS], "row")
        g_inner = grads[state_width + STEP_ROWS : gate_at]
        g_gate = grads[gate_at:out_at]
        g_out = grads[out_at:]

    def feature_rows(w):
        return jnp.transpose(w.reshape(nh, pc, share), (2, 0, 1))

    channel_vecs = vectors[:, 0:inner].reshape(8, nh, pc)
    grad_norm = jnp.concatenate([vectors[6, inner:], vectors[7, : half - 2 * ns]])
    return (
        output,
        grad_inputs,
        grad_norm,
        feature_rows(g_gate),
        feature_rows(g_inner),
        g_state,
        g_step[:nh].T,
        channel_vecs[0:4],
        channel_vecs[4],
        vectors[0:4, inner:],
        vectors[4, inner:],
        vectors[5, inner : inner + nh],
        -vectors[5, inner + 128 : inner + 128 + nh] * jnp.exp(decay_log),
        jnp.sum(channel_vecs[6], axis=1),
        channel_vecs[5],
        feature_rows(g_out),
    )


def solution(mesh):
    return jax.shard_map(
        per_device,
        mesh=mesh,
        in_specs=(
            P("dp", "row"),
            P("dp", None),
            P("dp", "row"),
            P("row"),
            P("dp", "col", "row"),
            P("dp", "col", "row"),
            P("dp", None),
            P("dp", "col"),
            P(None, "col", "row"),
            P("col", "row"),
            P(),
            P(),
            P("col"),
            P("col"),
            P("col"),
            P("col", "row"),
            P("dp", "col", "row"),
        ),
        out_specs=(
            P("dp", "row"),
            P("dp", "row"),
            P("row"),
            P("dp", "col", "row"),
            P("dp", "col", "row"),
            P("dp", None),
            P("dp", "col"),
            P(None, "col", "row"),
            P("col", "row"),
            P(),
            P(),
            P("col"),
            P("col"),
            P("col"),
            P("col", "row"),
            P("dp", "col", "row"),
        ),
        check_vma=False,
    )
```

time: 1350 us -> 268 us (0.20); the launches traced: 1330 us -> 267 us
  waiting for transfers between devices: 656 us -> 0 us
  matrix products: 274 us -> 0 us
  Pallas kernels: 0 us -> 242 us
  other arithmetic: 165 us -> 12.5 us
  local copies, waits for them, and re-layouts: 124 us -> 12.1 us
  blocking collectives: 96.5 us -> 0 us
  between operations: 15.6 us -> 0.75 us
    dot_general x77 -> x0, matrix products: 274 us -> none  [the longest x24 95.9 us: intra_block(): return jnp.einsum('hts,shp->thp', mixing, driven_block, precision=HIGHEST)]
    psum x2 -> x0, waiting for transfers between devices: 251 us -> none  [the longest x1 219 us: per_device(): d_half = lax.psum(d_half, 'col')]
    pallas_call x0 -> x1, Pallas kernels: none -> 242 us  [per_device(): pl.pallas_call(functools.partial(layer_kernel, cfg, plan, names), name='l...]
    unnamed x16 -> x0, waiting for transfers between devices: 211 us -> none
    reduce_scatter x6 -> x0, waiting for transfers between devices: 168 us -> none  [the longest x1 41 us: per_device(): lax.psum_scatter(grad_gate_w.reshape(model_width, head_count, channels),...]
    psum x6 -> x0, blocking collectives: 72.2 us -> none  [the longest x1 18 us: per_device(): lax.psum((d_state_act, wide_step, wide_decay, wide_skip), ('row', 'col'))]
    reduce_sum x15 -> x1, other arithmetic: 35.2 us -> 0.63 us  [per_device(): jnp.sum(channel_vecs[6], axis=1)]
    all_gather x6 -> x0, waiting for transfers between devices: 27 us -> none  [the longest x1 15.4 us: per_device(): output = lax.all_gather(out_rows, 'col', axis=1, tiled=True)]
  transfers between devices with their start and end apart: 15 -> 0, of which waited for: 10 -> 0; matrix products, arithmetic and copies ran while one was open for 24% -> 0% of each run, Pallas kernels for 0% -> 0%
where the time goes in v4:
time: 268 us; the launch traced here: 267 us
  Pallas kernels  242 us (90%)
  other arithmetic  12.5 us (5%)
  local copies, waits for them, and re-layouts  12.1 us (5%)
    pallas_call x1, Pallas kernels, per_device(): pl.pallas_call(functools.partial(layer_kernel, cfg, plan, names), name='l...  242 us
    sub x1, other arithmetic, per_device(): grad_inputs = cotangent.astype(F32) + scale * weighted - plain * pull  8.18 us

profile of v4, /device:TPU:0, one launch (start us, length us, event | category | flops | bytes accessed | tf_op | source)
XLA Modules:
  0.0 267.5 jit_solution(17984411096794534923)
XLA Ops:
  0.6 0.7 copy.35
  1.4 0.1 concatenate.19
  1.5 0.8 concatenate.20
  2.2 0.8 concatenate.21
  3.0 1.3 maximum_maximum_fusion.refs_6_
  4.3 1.3 select_maximum_fusion.refs_7_
  5.6 1.3 broadcast_in_dim.14.refs_4_
  6.9 0.0 copy-start.6
  6.9 242.1 %layer.1 = (bf16[2048,768]{1,0:T(8,128)(2,1)}, bf16[2048,768]{1,0:T(8,128)(2,1)}, f32[24,256]{1,0:T(8,128)}, f32[8,640]{1,0:T(8,128)}, f32[384,384]{1,0:T(8,128)...) custom-call(bf16[2048,768]{1,0:T(8,128)(2,1)} %refs_2_.1, ...), custom_call_target="tpu_custom_call" | custom-call | flops 26877100032 | bytes 62914560 | tf_op jit(solution)/shard_map/layer/pallas_call | solution.py:1390
  249.0 0.7 slice_bitcast_fusion.2
  249.8 0.0 copy-done.6
  249.8 0.0 copy-start.5
  249.8 0.0 copy-start.7
  249.8 0.0 copy-start.4
  249.8 0.0 copy-start.2
  249.9 0.0 copy-start.1
  249.9 0.0 copy-start.3
  249.9 0.0 copy-start
  249.9 8.2 %fusion.1 = (f32[2048,768]{1,0:T(8,128)}, bf16[2048,768]{1,0:T(8,128)(2,1)}) fusion(bf16[2048,768]{1,0:T(8,128)(2,1)} %refs_2_.1, bf16[2048,768]{1,0:T(8,128)(2,1)} %get-tuple-element.27, bf16[2048,768]{1,0:T(8,128)(2,1)} %refs_3_.1, f32[2048]{0:T(1024)S(1)} %bitcast.46, f32[768]{0:T(1024)S(1)} %copy-done.6, f32[2048]{0:T(1024)S(1)} %bitcast.45, ...), kind=kLoop, calls=%fused_computation.3 | loop fusion | flops 18874368 | bytes 22047744 | tf_op jit(solution)/shard_map/sub | solution.py:1413
  258.1 0.0 copy-done.5
  258.1 0.6 fusion.2
  258.6 0.6 pad_maximum_fusion
  259.3 0.1 squeeze.27
  259.4 0.6 reduce_sum.9
  260.0 0.7 squeeze.24
  260.7 0.7 squeeze.28
  261.3 0.1 slice.63
  261.4 0.6 copy.36
  262.0 0.6 slice.65
  262.6 0.0 copy-done.7
  262.6 0.5 bitcast_multiply_fusion
  263.2 0.5 slice_bitcast_fusion.4
  263.7 0.0 copy-done.4
  263.7 0.6 slice_bitcast_fusion
  264.3 0.0 copy-done.2
  264.3 0.8 copy.44
  265.1 0.0 copy-done.1
  265.1 0.8 copy.45
  265.9 0.0 copy-done.3
  265.9 0.7 copy.46
  266.7 0.0 copy-done
  266.7 0.8 copy.47
  (8 shorter events, 0.1 us)
Async XLA Ops:
  6.9 242.9 %copy-start.6 = (f32[768]{0:T(1024)S(1)}, f32[768]{0:T(1024)}, u32[]{:S(2)}) copy-start(f32[768]{0:T(1024)} %param.20) | copy-start | bytes 9220
  249.8 8.3 %copy-start.5 = (f32[8,640]{1,0:T(8,128)S(1)}, f32[8,640]{1,0:T(8,128)}, u32[]{:S(2)}) copy-start(f32[8,640]{1,0:T(8,128)} %get-tuple-element.28) | copy-start | bytes 61444
  249.8 12.8 %copy-start.7 = (f32[12]{0:T(128)S(1)}, f32[12]{0:T(128)}, u32[]{:S(2)}) copy-start(f32[12]{0:T(128)} %param.30) | copy-start | bytes 148
  249.8 13.8 %copy-start.4 = (f32[16,384]{1,0:T(8,128)S(1)}, f32[16,384]{1,0:T(8,128)}, u32[]{:S(2)}) copy-start(f32[16,384]{1,0:T(8,128)} %get-tuple-element.32) | copy-start | bytes 73732
  249.8 14.4 %copy-start.2 = (f32[384,384]{1,0:T(8,128)S(1)}, f32[384,384]{1,0:T(8,128)}, u32[]{:S(2)}) copy-start(f32[384,384]{1,0:T(8,128)} %get-tuple-element.29) | copy-start | bytes 1769476
  249.9 15.2 %copy-start.1 = (f32[384,384]{1,0:T(8,128)S(1)}, f32[384,384]{1,0:T(8,128)}, u32[]{:S(2)}) copy-start(f32[384,384]{1,0:T(8,128)} %get-tuple-element.30) | copy-start | bytes 1769476
  249.9 16.1 %copy-start.3 = (f32[384,256]{1,0:T(8,128)S(1)}, f32[384,256]{1,0:T(8,128)}, u32[]{:S(2)}) copy-start(f32[384,256]{1,0:T(8,128)} %get-tuple-element.97) | copy-start | bytes 1179652
  249.9 16.8 %copy-start = (f32[384,384]{1,0:T(8,128)S(1)}, f32[384,384]{1,0:T(8,128)}, u32[]{:S(2)}) copy-start(f32[384,384]{1,0:T(8,128)} %get-tuple-element.33) | copy-start | bytes 1769476

commit v5 on v4

--- a/solution.py
+++ b/solution.py
@@ -24,6 +24,7 @@
 STOPS = (1, 1, 2, 3, 4, 7, 7, 8, 10)
 DEPTH = 2
 VMEM_LIMIT = 63 << 20
+FINISH_STEPS = 2
 F32 = jnp.float32
 BF16 = jnp.bfloat16
 HIGHEST = lax.Precision.HIGHEST
@@ -75,11 +76,26 @@
     return total.T[0:8]
 
 
-def load_columns(par_rows, head_rows, conv_scr, head_scr):
-    conv_scr[...] = columns_of(par_rows[...])
-    heads = columns_of(head_rows[...])[0:STEP_ROWS]
+def pad_lanes(rows):
+    return jnp.concatenate([rows, jnp.zeros((rows.shape[0], 128 - rows.shape[1]), F32)], axis=1)
+
+
+def load_columns(r):
+    nh, taps, pc = r.conv_in.shape
+    rows = []
+    for h in range(nh):
+        rows += [r.conv_in[h], r.bias_in[h : h + 1], r.gate_gain[h : h + 1]]
+        rows += [jnp.zeros((2, pc), F32)]
+    cols = columns_of(pad_lanes(jnp.concatenate(rows, axis=0)))[0:pc]
+    for h in range(nh):
+        turned = pltpu.roll(cols, 128 - 8 * h, axis=1) if h else cols
+        r.conv[h * pc : (h + 1) * pc] = turned
+    state_rows = jnp.concatenate([r.conv_st[...], r.bias_st[...]], axis=0)
+    r.conv[nh * pc :] = columns_of(state_rows)
+    head_rows = jnp.concatenate([r.step_bias[...], r.decay_log[...], r.skip_gain[...]], axis=0)
+    heads = columns_of(pad_lanes(head_rows))[0:STEP_ROWS]
     lanes = lax.broadcasted_iota(jnp.int32, heads.shape, 1)
-    head_scr[...] = jnp.where(lanes == 1, -jnp.exp(heads), heads)
+    r.head[...] = jnp.where(lanes == 1, -jnp.exp(heads), heads)
 
 
 def block_rows(dims, step_pre, hrow, aux):
@@ -141,7 +157,8 @@
         self.first, self.pair, self.cross = r.ch_first, r.ch_pair, r.ch_cross
         self.slots = self.first.shape[0]
         self.out_slots = self.own.shape[0]
-        self.sems = [(r.cs_send.at[k], r.cs_recv.at[k]) for k in range(4)]
+        self.sems = [(r.cs_send.at[k], r.cs_recv.at[k]) for k in range(3)]
+        self.sems.append((r.cs_out.at[0], r.cs_out.at[1]))
         self.keep_sems = r.cs_keep
         self.free = r.ch_free
         self.first_rows, self.second_rows = first_rows, second_rows
@@ -174,8 +191,7 @@
         return send(self.pair.at[at], self.cross.at[at], self.sems[2], at, col=3 - self.col_at)
 
     def to_outer(self, m, rows):
-        at = self.slot(m)
-        return send(self.cross.at[at], rows, self.sems[3], at, col=self.outward)
+        return send(self.cross.at[self.slot(m)], rows, self.sems[3], m, col=self.outward)
 
     def keep(self, m, rows):
         at = self.slot(m)
@@ -255,17 +271,21 @@
                 self.to_outer(m, self.second_rows(m)).start()
 
     def stage_done(self, m):
-        rows = self.first_rows(0)
-
-        @pl.when(self.is_outer)
-        def _():
-            self.to_outer(m, rows).wait_recv()
-
         @pl.when(~self.is_outer)
         def _():
+            rows = self.first_rows(0)
             self.keep(m, rows).wait()
             self.to_outer(m, rows).wait_send()
             self.credit(2, m, col=3 - self.col_at)
+
+    def totals(self):
+        @pl.when(self.is_outer)
+        def _():
+            def one(m, _):
+                self.to_outer(m, self.first_rows(0)).wait_recv()
+                return 0
+
+            lax.fori_loop(0, self.total, one, 0)
 
 
 class Plan:
@@ -627,7 +647,7 @@
         for b in range(blocks):
             swap(0, b).start()
             swap(1, b).start()
-        load_columns(r.par_rows, r.head_rows, r.conv, r.head)
+        load_columns(r)
         for ref in (r.acc_w, r.state, r.after, r.acc_conv, r.acc_chan, r.acc_head):
             ref[...] = jnp.zeros_like(ref)
         for ref in (r.acc_norm, r.acc_dot, r.scale):
@@ -1124,6 +1144,7 @@
             return 0
 
         lax.fori_loop(last_done, plan.total, settle, 0)
+        chain.totals()
         for m in range(plan.total - chain.out_slots, plan.total):
             chain.exchange(m).wait_send()
 
@@ -1193,6 +1214,79 @@
             aux[offset - 1 : offset] * joined[:, 128 - offset : 128 - offset + q]
         )
     return arg
+
+
+def finish_kernel(
+    nh,
+    x_ref,
+    c_ref,
+    out_total,
+    dn_total,
+    tokens,
+    gain_own,
+    vectors,
+    decay_log,
+    g_inner,
+    g_gate,
+    g_out,
+    g_state,
+    g_step,
+    output,
+    grad_inputs,
+    inner_grad,
+    gate_grad,
+    out_grad,
+    state_grad,
+    step_grad,
+    norm_grad,
+    conv_inner,
+    bias_inner,
+    conv_state,
+    bias_state,
+    head_grad,
+    gate_norm,
+):
+    at = pl.program_id(0)
+    blocks = tokens.shape[0] // 3
+    steps = pl.num_programs(0)
+    cols = []
+    for part in range(blocks // steps):
+        b = at * (blocks // steps) + part
+        rows = [tokens[pl.ds(k * blocks + b, 1)] for k in range(3)]
+        cols.append(columns_of(jnp.concatenate(rows, axis=0)))
+    cols = jnp.concatenate(cols, axis=0)
+    scale, pull, gate_scale = (cols[:, k : k + 1] for k in range(3))
+    plain = x_ref[...].astype(F32)
+    output[...] = (plain + gate_scale * out_total[...].astype(F32)).astype(BF16)
+    weighted = dn_total[...].astype(F32) * gain_own[...]
+    grad_inputs[...] = c_ref[...].astype(F32) + scale * weighted - plain * pull
+    inner_grad[...] = g_inner[...]
+    gate_grad[...] = g_gate[...]
+    out_grad[...] = g_out[...]
+    state_grad[...] = g_state[...]
+
+    @pl.when(at == 0)
+    def _():
+        inner = g_inner.shape[0] * steps
+        pc = inner // nh
+        lane = vectors.shape[1] - inner
+        half = gain_own.shape[1]
+        vec = vectors[...]
+        step_grad[...] = g_step[0:nh]
+        norm_grad[...] = jnp.concatenate([vec[6:7, inner:], vec[7:8, 0 : half - lane]], axis=1)
+        conv_state[...] = vec[0:4, inner:]
+        bias_state[...] = vec[4:5, inner:]
+        skips = []
+        for h in range(nh):
+            part = vec[:, h * pc : (h + 1) * pc]
+            conv_inner[h] = part[0:4]
+            bias_inner[h : h + 1] = part[4:5]
+            gate_norm[h : h + 1] = part[5:6]
+            skips.append(jnp.sum(part[6:7], axis=1, keepdims=True))
+        decay = -vec[5:6, inner + 128 : inner + 128 + nh] * jnp.exp(decay_log[...])
+        head_grad[0:1] = vec[5:6, inner : inner + nh]
+        head_grad[1:2] = decay
+        head_grad[2:3] = jnp.concatenate(skips, axis=1)
 
 
 def per_device(
@@ -1249,23 +1343,6 @@
     gain_own = norm_gain[None, :]
     group = row_count * col_count
 
-    chan_rows = jnp.concatenate(
-        [
-            conv_inner,
-            bias_inner[None],
-            gate_norm[None],
-            jnp.zeros((2, nh, pc), F32),
-        ],
-        axis=0,
-    ).reshape(8, inner)
-    state_rows = jnp.concatenate(
-        [conv_state, bias_state[None], jnp.zeros((3, state_width), F32)], axis=0
-    )
-    par_rows = jnp.concatenate([chan_rows, state_rows], axis=1)
-    head_rows = jnp.pad(
-        jnp.stack([step_bias, decay_log, skip_gain]), ((0, 5), (0, 128 - nh))
-    )
-
     units = UNITS
     slots = blocks * units
     cfg = types.SimpleNamespace(
@@ -1299,8 +1376,14 @@
         "c_any": (cotangent, anywhere),
         "gain_own": (gain_own, whole(1, half)),
         "seg": (segments, pl.BlockSpec((1, q), lambda i: (0, fold(i)))),
-        "par_rows": (par_rows, whole(8, conv_rows)),
-        "head_rows": (head_rows, whole(8, 128)),
+        "conv_in": (jnp.transpose(conv_inner, (1, 0, 2)), whole(nh, 4, pc)),
+        "bias_in": (bias_inner, whole(nh, pc)),
+        "gate_gain": (gate_norm, whole(nh, pc)),
+        "conv_st": (conv_state, whole(4, state_width)),
+        "bias_st": (bias_state[None], whole(1, state_width)),
+        "step_bias": (step_bias[None], whole(1, nh)),
+        "decay_log": (decay_log[None], whole(1, nh)),
+        "skip_gain": (skip_gain[None], whole(1, nh)),
     }
     outs = {
         "out_total": (sds((length, half), BF16), anywhere),
@@ -1342,8 +1425,9 @@
         "ch_first": vmem((slots, q // units, half), BF16),
         "ch_pair": vmem((slots, q // units, half), BF16),
         "ch_cross": vmem((slots, q // units, half), BF16),
-        "cs_send": dma((4, slots)),
-        "cs_recv": dma((4, slots)),
+        "cs_send": dma((3, slots)),
+        "cs_recv": dma((3, slots)),
+        "cs_out": dma((2, plan.total)),
         "cs_keep": dma((slots,)),
         "ch_free": pltpu.SemaphoreType.REGULAR((3,)),
         "swap_sems": dma((4, blocks + 1)),
@@ -1405,6 +1489,8 @@
         ),
     )(*(array for array, _ in ins.values()))
     made = types.SimpleNamespace(**dict(zip(outs, results, strict=True)))
+    if gathers:
+        return finish(nh, blocks, made, inputs, cotangent, gain_own, decay_log[None], ns)
     tokens = made.token_out.reshape(3, length)
     scale, pull, gate_scale = (tokens[k][:, None] for k in range(3))
     plain = inputs.astype(F32)
@@ -1412,18 +1498,14 @@
     weighted = made.dn_total.astype(F32) * gain_own
     grad_inputs = cotangent.astype(F32) + scale * weighted - plain * pull
     vectors = made.vec_out
-    if gathers:
-        g_inner, g_gate, g_out = made.g_inner, made.g_gate, made.g_out
-        g_state, g_step = made.g_state, made.g_step
-    else:
-        grads = lax.psum_scatter(made.grad_w, "dp", scatter_dimension=1, tiled=True)
-        grads = grads.astype(F32)
-        vectors = lax.psum(vectors, "dp")
-        g_state = lax.psum(grads[0:state_width], ("row", "col")).T
-        g_step = lax.psum(grads[state_width : state_width + STEP_ROWS], "row")
-        g_inner = grads[state_width + STEP_ROWS : gate_at]
-        g_gate = grads[gate_at:out_at]
-        g_out = grads[out_at:]
+    grads = lax.psum_scatter(made.grad_w, "dp", scatter_dimension=1, tiled=True)
+    grads = grads.astype(F32)
+    vectors = lax.psum(vectors, "dp")
+    g_state = lax.psum(grads[0:state_width], ("row", "col")).T
+    g_step = lax.psum(grads[state_width : state_width + STEP_ROWS], "row")
+    g_inner = grads[state_width + STEP_ROWS : gate_at]
+    g_gate = grads[gate_at:out_at]
+    g_out = grads[out_at:]
 
     def feature_rows(w):
         return jnp.transpose(w.reshape(nh, pc, share), (2, 0, 1))
@@ -1446,6 +1528,127 @@
         -vectors[5, inner + 128 : inner + 128 + nh] * jnp.exp(decay_log),
         jnp.sum(channel_vecs[6], axis=1),
         channel_vecs[5],
+        feature_rows(g_out),
+    )
+
+
+def finish(nh, blocks, made, inputs, cotangent, gain_own, decay_log, ns):
+    length, half = inputs.shape
+    inner, share = made.g_inner.shape
+    pc = inner // nh
+    q = length // blocks
+    steps = FINISH_STEPS
+    sds = jax.ShapeDtypeStruct
+
+    def whole(*shape):
+        return pl.BlockSpec(shape, lambda i: (0,) * len(shape))
+
+    tokens = pl.BlockSpec((length // steps, half), lambda i: (i, 0))
+    rows = pl.BlockSpec((inner // steps, share), lambda i: (i, 0))
+    state_rows = pl.BlockSpec((share // steps, 2 * ns), lambda i: (i, 0))
+    grad = sds((inner, share), F32)
+    (
+        output,
+        grad_inputs,
+        g_inner,
+        g_gate,
+        g_out,
+        g_state,
+        g_step,
+        norm,
+        conv_inner,
+        bias_inner,
+        conv_state,
+        bias_state,
+        heads,
+        gate_norm,
+    ) = pl.pallas_call(
+        functools.partial(finish_kernel, nh),
+        name="finish",
+        grid=(steps,),
+        in_specs=[
+            tokens,
+            tokens,
+            tokens,
+            tokens,
+            whole(3 * blocks, q),
+            whole(1, half),
+            whole(*made.vec_out.shape),
+            whole(1, nh),
+            rows,
+            rows,
+            rows,
+            state_rows,
+            whole(STEP_ROWS, share),
+        ],
+        out_specs=[
+            tokens,
+            tokens,
+            rows,
+            rows,
+            rows,
+            state_rows,
+            whole(nh, share),
+            whole(1, half),
+            whole(nh, 4, pc),
+            whole(nh, pc),
+            whole(4, 2 * ns),
+            whole(1, 2 * ns),
+            whole(3, nh),
+            whole(nh, pc),
+        ],
+        out_shape=[
+            sds((length, half), BF16),
+            sds((length, half), F32),
+            grad,
+            grad,
+            grad,
+            sds((share, 2 * ns), F32),
+            sds((nh, share), F32),
+            sds((1, half), F32),
+            sds((nh, 4, pc), F32),
+            sds((nh, pc), F32),
+            sds((4, 2 * ns), F32),
+            sds((1, 2 * ns), F32),
+            sds((3, nh), F32),
+            sds((nh, pc), F32),
+        ],
+        compiler_params=pltpu.CompilerParams(vmem_limit_bytes=VMEM_LIMIT),
+    )(
+        inputs,
+        cotangent,
+        made.out_total,
+        made.dn_total,
+        made.token_out,
+        gain_own,
+        made.vec_out,
+        decay_log,
+        made.g_inner,
+        made.g_gate,
+        made.g_out,
+        made.g_state,
+        made.g_step,
+    )
+
+    def feature_rows(w):
+        return jnp.transpose(w.reshape(nh, pc, share), (2, 0, 1))
+
+    return (
+        output,
+        grad_inputs,
+        norm[0],
+        feature_rows(g_gate),
+        feature_rows(g_inner),
+        g_state,
+        g_step.T,
+        jnp.transpose(conv_inner, (1, 0, 2)),
+        bias_inner,
+        conv_state,
+        bias_state[0],
+        heads[0],
+        heads[1],
+        heads[2],
+        gate_norm,
         feature_rows(g_out),
     )
 

time: 268 us -> 257 us (0.959)
  other arithmetic: 12.5 us -> 1.28 us
  Pallas kernels: 242 us -> 252 us
  local copies, waits for them, and re-layouts: 12.1 us -> 2.58 us
    pallas_call x0 -> x1, Pallas kernels: none -> 10 us  [finish(): pl.pallas_call(functools.partial(finish_kernel, nh), name='finish', grid=...]
    sub x1 -> x0, other arithmetic: 8.18 us -> none  [per_device(): grad_inputs = cotangent.astype(F32) + scale * weighted - plain * pull]
    unnamed x26 -> x0, local copies, waits for them, and re-layouts: 5.34 us -> none
where the time goes in v5:
time: 257 us
  Pallas kernels  252 us (98%)
  local copies, waits for them, and re-layouts  2.58 us (1%)
    pallas_call x1, Pallas kernels, per_device(): pl.pallas_call(functools.partial(layer_kernel, cfg, plan, names), name='l...  242 us
    pallas_call x1, Pallas kernels, finish(): pl.pallas_call(functools.partial(finish_kernel, nh), name='finish', grid=...  10 us

profile of v5, /device:TPU:0, one launch (start us, length us, event | category | flops | bytes accessed | tf_op | source)
XLA Modules:
  0.0 256.6 jit_solution(6690728347713798941)
XLA Ops:
  0.6 1.3 broadcast_in_dim.16.refs_4_.gain_own
  1.9 242.0 %layer.1 = (bf16[2048,768]{1,0:T(8,128)(2,1)}, bf16[2048,768]{1,0:T(8,128)(2,1)}, f32[24,256]{1,0:T(8,128)}, f32[8,640]{1,0:T(8,128)}, f32[384,384]{1,0:T(8,128)...) custom-call(bf16[2048,768]{1,0:T(8,128)(2,1)} %x_ref.1, ...), custom_call_target="tpu_custom_call" | custom-call | flops 26877100032 | bytes 62914560 | tf_op jit(solution)/shard_map/layer/pallas_call | solution.py:1474
  244.0 10.0 %finish.1 = (bf16[2048,768]{1,0:T(8,128)(2,1)}, f32[2048,768]{1,0:T(8,128)}, f32[384,384]{1,0:T(8,128)}, f32[384,384]{1,0:T(8,128)}, f32[384,384]{1,0:T(8,128)},...) custom-call(bf16[2048,768]{1,0:T(8,128)(2,1)} %x_ref.1, ...), custom_call_target="tpu_custom_call" | custom-call | tf_op jit(solution)/shard_map/finish/pallas_call | solution.py:1565
  254.0 1.3 slice_bitcast_fusion
  255.3 1.3 reduce

commit v6 on v5

--- a/solution.py
+++ b/solution.py
@@ -626,6 +626,7 @@
     @pl.when(step_at == 0)
     def _():
         greet(peers + friends)
+        r.gain_own[...] = r.gain_in[...].reshape(1, half)
         if gathers:
             for k in range(len(raw)):
                 raw_copy(k).start()
@@ -1243,7 +1244,9 @@
     bias_inner,
     conv_state,
     bias_state,
-    head_grad,
+    step_bias,
+    decay_grad,
+    skip_grad,
     gate_norm,
 ):
     at = pl.program_id(0)
@@ -1258,7 +1261,7 @@
     scale, pull, gate_scale = (cols[:, k : k + 1] for k in range(3))
     plain = x_ref[...].astype(F32)
     output[...] = (plain + gate_scale * out_total[...].astype(F32)).astype(BF16)
-    weighted = dn_total[...].astype(F32) * gain_own[...]
+    weighted = dn_total[...].astype(F32) * gain_own[...].reshape(1, -1)
     grad_inputs[...] = c_ref[...].astype(F32) + scale * weighted - plain * pull
     inner_grad[...] = g_inner[...]
     gate_grad[...] = g_gate[...]
@@ -1270,12 +1273,12 @@
         inner = g_inner.shape[0] * steps
         pc = inner // nh
         lane = vectors.shape[1] - inner
-        half = gain_own.shape[1]
+        half = gain_own.shape[0]
         vec = vectors[...]
         step_grad[...] = g_step[0:nh]
-        norm_grad[...] = jnp.concatenate([vec[6:7, inner:], vec[7:8, 0 : half - lane]], axis=1)
+        norm_grad[...] = jnp.concatenate([vec[6:7, inner:], vec[7:8, 0 : half - lane]], axis=1)[0]
         conv_state[...] = vec[0:4, inner:]
-        bias_state[...] = vec[4:5, inner:]
+        bias_state[...] = vec[4, inner:]
         skips = []
         for h in range(nh):
             part = vec[:, h * pc : (h + 1) * pc]
@@ -1284,9 +1287,9 @@
             gate_norm[h : h + 1] = part[5:6]
             skips.append(jnp.sum(part[6:7], axis=1, keepdims=True))
         decay = -vec[5:6, inner + 128 : inner + 128 + nh] * jnp.exp(decay_log[...])
-        head_grad[0:1] = vec[5:6, inner : inner + nh]
-        head_grad[1:2] = decay
-        head_grad[2:3] = jnp.concatenate(skips, axis=1)
+        step_bias[...] = vec[5, inner : inner + nh]
+        decay_grad[...] = decay[0]
+        skip_grad[...] = jnp.concatenate(skips, axis=1)[0]
 
 
 def per_device(
@@ -1374,7 +1377,7 @@
         "c_own": (cotangent, token_block),
         "x_any": (inputs, anywhere),
         "c_any": (cotangent, anywhere),
-        "gain_own": (gain_own, whole(1, half)),
+        "gain_in": (norm_gain, whole(half)),
         "seg": (segments, pl.BlockSpec((1, q), lambda i: (0, fold(i)))),
         "conv_in": (jnp.transpose(conv_inner, (1, 0, 2)), whole(nh, 4, pc)),
         "bias_in": (bias_inner, whole(nh, pc)),
@@ -1395,6 +1398,7 @@
         "acc_w": vmem((rows, width), F32),
         "x_scr": vmem((blocks, q, half), BF16),
         "c_scr": vmem((blocks, q, half), BF16),
+        "gain_own": vmem((1, half), F32),
         "gain_sib": vmem((1, half), F32),
         "conv": vmem((conv_rows, 128), F32),
         "head": vmem((STEP_ROWS, 128), F32),
@@ -1490,7 +1494,7 @@
     )(*(array for array, _ in ins.values()))
     made = types.SimpleNamespace(**dict(zip(outs, results, strict=True)))
     if gathers:
-        return finish(nh, blocks, made, inputs, cotangent, gain_own, decay_log[None], ns)
+        return finish(nh, blocks, made, inputs, cotangent, norm_gain, decay_log[None], ns)
     tokens = made.token_out.reshape(3, length)
     scale, pull, gate_scale = (tokens[k][:, None] for k in range(3))
     plain = inputs.astype(F32)
@@ -1560,7 +1564,9 @@
         bias_inner,
         conv_state,
         bias_state,
-        heads,
+        step_bias,
+        decay,
+        skip,
         gate_norm,
     ) = pl.pallas_call(
         functools.partial(finish_kernel, nh),
@@ -1572,7 +1578,7 @@
             tokens,
             tokens,
             whole(3 * blocks, q),
-            whole(1, half),
+            whole(half),
             whole(*made.vec_out.shape),
             whole(1, nh),
             rows,
@@ -1589,12 +1595,14 @@
             rows,
             state_rows,
             whole(nh, share),
-            whole(1, half),
+            whole(half),
             whole(nh, 4, pc),
             whole(nh, pc),
             whole(4, 2 * ns),
-            whole(1, 2 * ns),
-            whole(3, nh),
+            whole(2 * ns),
+            whole(nh),
+            whole(nh),
+            whole(nh),
             whole(nh, pc),
         ],
         out_shape=[
@@ -1605,12 +1613,14 @@
             grad,
             sds((share, 2 * ns), F32),
             sds((nh, share), F32),
-            sds((1, half), F32),
+            sds((half,), F32),
             sds((nh, 4, pc), F32),
             sds((nh, pc), F32),
             sds((4, 2 * ns), F32),
-            sds((1, 2 * ns), F32),
-            sds((3, nh), F32),
+            sds((2 * ns,), F32),
+            sds((nh,), F32),
+            sds((nh,), F32),
+            sds((nh,), F32),
             sds((nh, pc), F32),
         ],
         compiler_params=pltpu.CompilerParams(vmem_limit_bytes=VMEM_LIMIT),
@@ -1636,7 +1646,7 @@
     return (
         output,
         grad_inputs,
-        norm[0],
+        norm,
         feature_rows(g_gate),
         feature_rows(g_inner),
         g_state,
@@ -1644,10 +1654,10 @@
         jnp.transpose(conv_inner, (1, 0, 2)),
         bias_inner,
         conv_state,
-        bias_state[0],
-        heads[0],
-        heads[1],
-        heads[2],
+        bias_state,
+        step_bias,
+        decay,
+        skip,
         gate_norm,
         feature_rows(g_out),
     )

time: 257 us -> 254 us (0.988)
  local copies, waits for them, and re-layouts: 2.58 us -> 0 us
where the time goes in v6:
time: 254 us; the launch traced here: 253 us
  Pallas kernels  253 us (100%)
    pallas_call x1, Pallas kernels, per_device(): pl.pallas_call(functools.partial(layer_kernel, cfg, plan, names), name='l...  243 us
    pallas_call x1, Pallas kernels, finish(): pl.pallas_call(functools.partial(finish_kernel, nh), name='finish', grid=...  10 us

profile of v6, /device:TPU:0, one launch (start us, length us, event | category | flops | bytes accessed | tf_op | source)
XLA Modules:
  0.0 253.4 jit_solution(9307936070634057336)
XLA Ops:
  0.7 242.6 %layer.1 = (bf16[2048,768]{1,0:T(8,128)(2,1)}, bf16[2048,768]{1,0:T(8,128)(2,1)}, f32[24,256]{1,0:T(8,128)}, f32[8,640]{1,0:T(8,128)}, f32[384,384]{1,0:T(8,128)...) custom-call(bf16[2048,768]{1,0:T(8,128)(2,1)} %x_ref.1, ...), custom_call_target="tpu_custom_call" | custom-call | flops 26877100032 | bytes 62914560 | tf_op jit(solution)/shard_map/layer/pallas_call | solution.py:1478
  243.2 10.0 %finish.1 = (bf16[2048,768]{1,0:T(8,128)(2,1)}, f32[2048,768]{1,0:T(8,128)}, f32[384,384]{1,0:T(8,128)}, f32[384,384]{1,0:T(8,128)}, f32[384,384]{1,0:T(8,128)},...) custom-call(bf16[2048,768]{1,0:T(8,128)(2,1)} %x_ref.1, ...), custom_call_target="tpu_custom_call" | custom-call | tf_op jit(solution)/shard_map/finish/pallas_call | solution.py:1571

commit v7 on v6

--- a/solution.py
+++ b/solution.py
@@ -20,7 +20,7 @@
 TURN_AT = (0.3, 0.6, 0.9)
 AHEAD = 5
 MODEL = (2.4, 3.7, 10.0, 8.2, 8.0, 0.5)
-FORWARD_AT = (2, 4)
+FORWARD_AT = (1, 3)
 STOPS = (1, 1, 2, 3, 4, 7, 7, 8, 10)
 DEPTH = 2
 VMEM_LIMIT = 63 << 20

time: 254 us -> 250 us (0.984)
  Pallas kernels: 253 us -> 249 us
    pallas_call x1, Pallas kernels: 243 us -> 239 us  [per_device(): pl.pallas_call(functools.partial(layer_kernel, cfg, plan, names), name='l...]
where the time goes in v7:
time: 250 us
  Pallas kernels  249 us (100%)
    pallas_call x1, Pallas kernels, per_device(): pl.pallas_call(functools.partial(layer_kernel, cfg, plan, names), name='l...  239 us
    pallas_call x1, Pallas kernels, finish(): pl.pallas_call(functools.partial(finish_kernel, nh), name='finish', grid=...  10 us

profile of v7, /device:TPU:0, one launch (start us, length us, event | category | flops | bytes accessed | tf_op | source)
XLA Modules:
  0.0 249.9 jit_solution(15607361506034498175)
XLA Ops:
  0.7 239.1 %layer.1 = (bf16[2048,768]{1,0:T(8,128)(2,1)}, bf16[2048,768]{1,0:T(8,128)(2,1)}, f32[24,256]{1,0:T(8,128)}, f32[8,640]{1,0:T(8,128)}, f32[384,384]{1,0:T(8,128)...) custom-call(bf16[2048,768]{1,0:T(8,128)(2,1)} %x_ref.1, ...), custom_call_target="tpu_custom_call" | custom-call | flops 26877100032 | bytes 62914560 | tf_op jit(solution)/shard_map/layer/pallas_call | solution.py:1478
  239.7 10.0 %finish.1 = (bf16[2048,768]{1,0:T(8,128)(2,1)}, f32[2048,768]{1,0:T(8,128)}, f32[384,384]{1,0:T(8,128)}, f32[384,384]{1,0:T(8,128)}, f32[384,384]{1,0:T(8,128)},...) custom-call(bf16[2048,768]{1,0:T(8,128)(2,1)} %x_ref.1, ...), custom_call_target="tpu_custom_call" | custom-call | tf_op jit(solution)/shard_map/finish/pallas_call | solution.py:1571
